TPU v7x, 32 devices: a whole 2x2x4 slice. The times are simulated.
32 devices in a mesh: groups: 2 (over x), ep: 16 (over z, y, core).
Axes of the slice: x: 2, y: 2, z: 4, core: 2. Of those that a mesh axis runs over, the one named last changes fastest.
Arguments:
- hidden_in: bfloat16 [1024, 2048], P(('groups', 'ep')), parts along dimension 0, may hold values from -6 to 6
- queries: bfloat16 [1024, 2048], P(('groups', 'ep')), parts along dimension 0, may hold values from -400 to 400
- stored_keys: bfloat16 [1024, 64, 256], P(('groups', 'ep')), parts along dimension 0, may hold values from -6 to 6
- stored_values: bfloat16 [1024, 64, 256], P(('groups', 'ep')), parts along dimension 0, may hold values from -6 to 6
- stored_lengths: int32 [1024], P(('groups', 'ep')), parts along dimension 0, may hold values from 2 to 64, as said below
- norm_gain: float32 [2048], replicated, may hold values from 0.25 to 1.75
- expert_ids: int32 [1024, 8], P(('groups', 'ep')), parts along dimension 0, may hold values from 0 to 15, all different within a row; in each aligned block of 16 rows (0 to 15, 16 to 31, ...) at most 12 rows name the same one
- gate_weights: float32 [1024, 8], P(('groups', 'ep')), parts along dimension 0, may hold values from 0.05 to 1
- w_gate: bfloat16 [16, 2048, 768], P('ep'), may hold values from -0.125 to 0.125
- w_up: bfloat16 [16, 2048, 768], P('ep'), may hold values from -0.125 to 0.125
- w_down: bfloat16 [16, 768, 2048], P('ep'), may hold values from -0.21875 to 0.21875
Outputs:
- layer_out: bfloat16 [1024, 2048], P(('groups', 'ep')), parts along dimension 0
There are 2 independent parts, one for each index of `groups`. A program takes and returns all parts, laid end to end along the dimension named above; an argument that names none is the same for every part. Nothing has to cross between parts.
Inputs may be any that keep to these rules, and one draw needn't show every extreme that they name: `expert_ids`: every row names 8 different experts. In each aligned block of 16 rows (one micro-batch of one device, micro-batches in order within a device's rows) no expert is named by more than 12 rows, a bound that some block reaches. `stored_lengths`: the largest value 64 is taken by some request.
All inputs are finite; a program needn't handle non-finite values.
Results may differ from a plain program's by a relative error of at most 0.0059.
Values may be sent and summed in bfloat16 or wider, within the bound.
No kernel may reach another device: no remote copies, remote signals or barrier semaphores. Data moves between devices by JAX's collectives and lax.ppermute only.
A program may use at most 64 MiB of HBM per device.

v0:
```python
import math

import jax
import jax.numpy as jnp
from jax import lax
from jax.sharding import PartitionSpec as P

QUERY_HEADS = 16
KEY_VALUE_HEADS = 2
MB = 2
MB_ROWS = 16


def cached_attention(queries, stored_keys, stored_values, stored_lengths, heads, kv_heads):
    row_count = queries.shape[0]
    slots = stored_keys.shape[1]
    head_size = queries.shape[1] // heads
    query_head_rows = queries.reshape(row_count, kv_heads, heads // kv_heads, head_size)
    key_head_rows = stored_keys.reshape(row_count, slots, kv_heads, head_size)
    value_head_rows = stored_values.reshape(row_count, slots, kv_heads, head_size)
    scores = jnp.einsum(
        "nkgd,nckd->nkgc", query_head_rows, key_head_rows, preferred_element_type=jnp.float32
    ) / math.sqrt(head_size)
    visible = jnp.arange(slots, dtype=jnp.int32)[None, :] < stored_lengths[:, None]
    visible = visible[:, None, None, :]
    scores = jnp.where(visible, scores, -1e30)
    top_score = jnp.max(scores, axis=-1, keepdims=True)
    expo = jnp.where(visible, jnp.exp(scores - top_score), 0.0)
    probs = (expo / jnp.sum(expo, axis=-1, keepdims=True)).astype(jnp.bfloat16)
    attention_output = jnp.einsum(
        "nkgc,nckd->nkgd", probs, value_head_rows, preferred_element_type=jnp.float32
    )
    return attention_output.reshape(row_count, heads * head_size)


def expert_work(blocks, w_gate, w_up, w_down):
    gate_part = jnp.einsum("secd,edf->secf", blocks, w_gate, preferred_element_type=jnp.float32)
    up_part = jnp.einsum("secd,edf->secf", blocks, w_up, preferred_element_type=jnp.float32)
    inner = (jax.nn.silu(gate_part) * up_part).astype(jnp.bfloat16)
    return jnp.einsum("secf,efd->secd", inner, w_down, preferred_element_type=jnp.float32).astype(
        jnp.bfloat16
    )


def routed(normed, expert_ids, gate_weights, w_gate, w_up, w_down, capacity):
    devices = lax.axis_size("ep")
    local_count = w_gate.shape[0]
    experts = devices * local_count
    width = normed.shape[1]
    row_count, top_count = expert_ids.shape
    flat_ids = expert_ids.reshape(-1)
    onehot_table = (flat_ids[:, None] == jnp.arange(experts, dtype=jnp.int32)[None, :]).astype(
        jnp.int32
    )
    before = jnp.cumsum(onehot_table, axis=0) - onehot_table
    slot_index = jnp.sum(before * onehot_table, axis=1)
    target = flat_ids * capacity + slot_index
    target_rows = target.reshape(row_count, top_count)
    placing = jnp.sum(
        (
            target_rows[:, :, None]
            == jnp.arange(experts * capacity, dtype=jnp.int32)[None, None, :]
        ).astype(jnp.float32),
        axis=1,
    ).astype(jnp.bfloat16)
    buffer = jnp.einsum("tp,td->pd", placing, normed, preferred_element_type=jnp.float32).astype(
        jnp.bfloat16
    )
    buffer = buffer.reshape(experts, capacity, width)
    arrived = lax.all_to_all(buffer, "ep", split_axis=0, concat_axis=0, tiled=True)
    item_count = arrived.shape[1]
    blocks = arrived.reshape(devices, local_count, item_count, width)
    finished = expert_work(blocks, w_gate, w_up, w_down).reshape(experts, item_count, width)
    results = lax.all_to_all(finished, "ep", split_axis=0, concat_axis=0, tiled=True)
    picked = jnp.take(results.reshape(experts * capacity, width), target, axis=0)
    picked = picked.reshape(row_count, top_count, width).astype(jnp.float32)
    return jnp.sum(picked * gate_weights[:, :, None], axis=1)


def layer_rows(
    hidden_in,
    queries,
    stored_keys,
    stored_values,
    stored_lengths,
    norm_gain,
    expert_ids,
    gate_weights,
    w_gate,
    w_up,
    w_down,
    capacity,
):
    attention_output = cached_attention(
        queries, stored_keys, stored_values, stored_lengths, QUERY_HEADS, KEY_VALUE_HEADS
    )
    resid = hidden_in.astype(jnp.float32) + attention_output
    mean_square = jnp.mean(resid * resid, axis=-1, keepdims=True)
    normed = (resid * lax.rsqrt(mean_square + 1e-06) * norm_gain[None, :]).astype(jnp.bfloat16)
    mixture = routed(normed, expert_ids, gate_weights, w_gate, w_up, w_down, capacity)
    return (resid + mixture).astype(jnp.bfloat16)


def local(
    hidden_in,
    queries,
    stored_keys,
    stored_values,
    stored_lengths,
    norm_gain,
    expert_ids,
    gate_weights,
    w_gate,
    w_up,
    w_down,
):
    experts = lax.axis_size("ep") * w_gate.shape[0]
    top_count = expert_ids.shape[1]
    capacity = max(2, 3 * MB_ROWS * top_count // (2 * experts))
    return layer_rows(
        hidden_in,
        queries,
        stored_keys,
        stored_values,
        stored_lengths,
        norm_gain,
        expert_ids,
        gate_weights,
        w_gate,
        w_up,
        w_down,
        MB * capacity,
    )


def solution(mesh):
    in_specs = (
        P(("groups", "ep"), None),
        P(("groups", "ep"), None),
        P(("groups", "ep"), None, None),
        P(("groups", "ep"), None, None),
        P(("groups", "ep")),
        P(),
        P(("groups", "ep"), None),
        P(("groups", "ep"), None),
        P("ep", None, None),
        P("ep", None, None),
        P("ep", None, None),
    )
    out_specs = P(("groups", "ep"), None)
    return jax.shard_map(local, mesh=mesh, in_specs=in_specs, out_specs=out_specs, check_vma=False)
```

profile of v0, /device:TPU:13, one launch (start us, length us, event | category | flops | bytes accessed | tf_op | source)
XLA Modules:
  0.0 114.1 jit_solution(12084656877042410913)
XLA Ops:
  0.0 0.0 copy-start
  0.0 0.9 copy.26
  0.9 0.1 eq.39
  1.0 0.1 reshape.141
  1.1 0.6 reduce-window.6
  1.7 0.2 slice_reduce_fusion
  1.9 0.1 fusion.43
  2.0 0.0 copy-start.4
  2.0 0.1 reduce_sum.51
  2.1 0.6 compare_and_fusion
  2.7 0.8 convert_reduce_fusion
  3.5 0.0 copy-done.4
  3.5 0.9 copy.34
  4.4 0.7 iota_compare_fusion.3
  5.2 3.3 %fusion.48 = (f32[32,2,8]{2,1,0:T(2,128)}, f32[32,2,8,64]{3,2,1,0:T(8,128)}) fusion(pred[32,64]{1,0:T(8,128)(4,1)S(1)} %iota_compare_fusion.3, bf16[32,2,8,128]{3,2,1,0:T(8,128)(2,1)S(1)} %bitcast.117, bf16[32,64,256]{2,1,0:T(8,128)(2,1)} %param.13), kind=kOutput, calls=%fused_computation.57 | convolution fusion | flops 8552511 | bytes 1314816 | tf_op jit(solution)/shard_map/sub | solution.py:28
  8.5 0.0 copy-start.2
  8.5 0.0 copy-start.3
  8.5 0.0 copy-start.5
  8.5 1.8 %fusion.29 = f32[32,2,8,128]{3,2,1,0:T(8,128)S(1)} fusion(f32[32,2,8,64]{3,2,1,0:T(8,128)} %get-tuple-element.8, f32[32,2,8]{2,1,0:T(2,128)} %get-tuple-element.7, bf16[32,64,256]{2,1,0:T(8,128)(2,1)} %param.14), kind=kOutput, calls=%fused_computation.21 | convolution fusion | flops 8454144 | bytes 1443840 | tf_op jit(solution)/shard_map/nkgc,nckd->nkgd/dot_general | solution.py:30
  10.3 0.0 copy-done.2
  10.3 0.2 multiply_reduce_fusion.1
  10.5 0.0 copy-done.3
  10.5 0.0 copy-done.5
  10.5 0.6 convolution_convert_fusion
  11.1 0.0 copy-start.6
  11.1 42.6 %all_to_all.10 = bf16[16,24,2048]{2,1,0:T(8,128)(2,1)S(1)} all-to-all(bf16[16,24,2048]{2,1,0:T(8,128)(2,1)S(1)} %bitcast.112), channel_id=1, replica_groups=mesh['groups'=2,'ep'=16] {'ep'}, dimensions={0} | all-to-all | bytes 3145728 | tf_op jit(solution)/shard_map/all_to_all | solution.py:70
  53.8 0.0 copy-start.1
  53.8 1.1 %copy-done.1 = bf16[16,24,2048]{2,1,0:T(8,128)(2,1)} copy-done((bf16[16,24,2048]{2,1,0:T(8,128)(2,1)}, bf16[16,24,2048]{2,1,0:T(8,128)(2,1)S(1)}, u32[]{:S(2)}) %copy-start.1) | copy-done | bytes 1572888
  54.9 0.0 copy-done.6
  54.9 2.5 %fusion.10 = f32[16,1,24,768]{3,2,0,1:T(8,128)} fusion(bf16[16,24,2048]{2,1,0:T(8,128)(2,1)S(1)} %all_to_all.10, bf16[1,2048,768]{2,1,0:T(8,128)(2,1)S(1)} %copy-done.6), kind=kOutput, calls=%fused_computation.11 | convolution fusion | flops 1207959552 | bytes 5898240 | tf_op jit(solution)/shard_map/secd,edf->secf/dot_general | solution.py:37
  57.4 0.0 copy-done
  57.4 6.9 %fusion.7 = bf16[16,24,2048]{2,1,0:T(8,128)(2,1)} fusion(bf16[1,768,2048]{2,1,0:T(8,128)(2,1)S(1)} %copy-done, bf16[16,24,2048]{2,1,0:T(8,128)(2,1)} %copy-done.1, bf16[1,2048,768]{2,1,0:T(8,128)(2,1)} %param.20, f32[16,1,24,768]{3,2,0,1:T(8,128)} %fusion.10), kind=kOutput, calls=%fused_computation.8 | convolution fusion | flops 2418475008 | bytes 10616832 | tf_op jit(solution)/shard_map/secf,efd->secd/dot_general | solution.py:40
  64.3 5.0 %all-to-all-start.1 = ((bf16[16,24,2048]{2,1,0:T(8,128)(2,1)}), bf16[16,24,2048]{2,1,0:T(8,128)(2,1)}, u32[]{:S(2)}, u32[]{:S(2)}) async-start(bf16[16,24,2048]{2,1,0:T(8,128)(2,1)} %fusion.7), calls=%async_computation.1 | async-start | bytes 3145728 | tf_op jit(solution)/shard_map/all_to_all | solution.py:74
  69.2 0.6 broadcast_multiply_fusion
  69.9 1.4 %mul.68 = s32[256,1]{0,1:T(1,128)} reshape(s32[32,8]{1,0:T(8,128)} %broadcast_multiply_fusion) | data formatting | bytes 2048 | tf_op jit(solution)/shard_map/mul | solution.py:57
  71.2 0.8 copy.30
  72.0 0.7 compare_select_fusion.1
  72.7 0.6 pad_clamp_fusion
  73.3 32.3 %all-to-all-done.1 = bf16[16,24,2048]{2,1,0:T(8,128)(2,1)} async-done(((bf16[16,24,2048]{2,1,0:T(8,128)(2,1)}), bf16[16,24,2048]{2,1,0:T(8,128)(2,1)}, u32[]{:S(2)}, u32[]{:S(2)}) %all-to-all-start.1) | async-done | bytes 1572896 | tf_op jit(solution)/shard_map/all_to_all | solution.py:74
  105.5 5.1 %gather_fusion = bf16[256,2048]{1,0:T(8,128)(2,1)} fusion(bf16[384,2048]{1,0:T(8,128)(2,1)} %bitcast.17, s32[1024]{0:T(1024)} %pad_clamp_fusion), kind=kCustom, calls=%fused_computation | custom fusion | bytes 2098176 | tf_op jit(solution)/shard_map/jit(_take)/gather | solution.py:75
  110.6 2.7 %multiply_reduce_fusion = f32[32,2048]{1,0:T(8,128)S(1)} fusion(bf16[256,2048]{1,0:T(8,128)(2,1)} %gather_fusion, f32[32,8]{1,0:T(8,128)S(1)} %copy.30, pred[32,8]{1,0:T(8,128)(4,1)} %get-tuple-element.5), kind=kLoop, calls=%fused_computation.10 | loop fusion | flops 2031616 | bytes 1312000 | tf_op jit(solution)/shard_map/reduce_sum | solution.py:77
  113.3 0.8 add_convert_fusion
  (4 shorter events, 0.1 us)
Async XLA Ops:
  0.0 57.4 %copy-start = (bf16[1,768,2048]{2,1,0:T(8,128)(2,1)S(1)}, bf16[1,768,2048]{2,1,0:T(8,128)(2,1)}, u32[]{:S(2)}) copy-start(bf16[1,768,2048]{2,1,0:T(8,128)(2,1)} %param.21) | copy-start | bytes 9437188
  2.0 1.5 %copy-start.4 = (s32[256]{0:T(256)}, s32[256]{0:T(256)S(1)}, u32[]{:S(2)}) copy-start(s32[256]{0:T(256)S(1)} %fusion.43) | copy-start | bytes 3076
  8.5 1.8 %copy-start.2 = (bf16[32,2048]{1,0:T(8,128)(2,1)S(1)}, bf16[32,2048]{1,0:T(8,128)(2,1)}, u32[]{:S(2)}) copy-start(bf16[32,2048]{1,0:T(8,128)(2,1)} %param.11) | copy-start | bytes 393220
  8.5 2.0 %copy-start.3 = (bf16[32,384]{1,0:T(8,128)(2,1)S(1)}, bf16[32,384]{1,0:T(8,128)(2,1)}, u32[]{:S(2)}) copy-start(bf16[32,384]{1,0:T(8,128)(2,1)} %convert_reduce_fusion) | copy-start | bytes 73732
  8.5 2.0 %copy-start.5 = (f32[2048]{0:T(1024)S(1)}, f32[2048]{0:T(1024)}, u32[]{:S(2)}) copy-start(f32[2048]{0:T(1024)} %param.16) | copy-start | bytes 24580
  11.1 43.8 %copy-start.6 = (bf16[1,2048,768]{2,1,0:T(8,128)(2,1)S(1)}, bf16[1,2048,768]{2,1,0:T(8,128)(2,1)}, u32[]{:S(2)}) copy-start(bf16[1,2048,768]{2,1,0:T(8,128)(2,1)} %param.19) | copy-start | bytes 9437188
  53.8 1.1 %copy-start.1 = (bf16[16,24,2048]{2,1,0:T(8,128)(2,1)}, bf16[16,24,2048]{2,1,0:T(8,128)(2,1)S(1)}, u32[]{:S(2)}) copy-start(bf16[16,24,2048]{2,1,0:T(8,128)(2,1)S(1)} %all_to_all.10) | copy-start | bytes 4718596
  64.3 41.2 %all-to-all-start.1 = ((bf16[16,24,2048]{2,1,0:T(8,128)(2,1)}), bf16[16,24,2048]{2,1,0:T(8,128)(2,1)}, u32[]{:S(2)}, u32[]{:S(2)}) async-start(bf16[16,24,2048]{2,1,0:T(8,128)(2,1)} %fusion.7), calls=%async_computation.1 | async-start | bytes 3145728 | tf_op jit(solution)/shard_map/all_to_all | solution.py:74
where the time goes:
time: 115 us; the launch traced here: 114 us
  blocking collectives  42.6 us (37%)
  waiting for transfers between devices  32.3 us (28%)
  matrix products  15.1 us (13%)
  local copies, waits for them, and re-layouts  10.7 us (9%)
  other arithmetic  8.38 us (7%)
  starting transfers between devices  4.95 us (4%)
    all_to_all x1, blocking collectives, routed(): lax.all_to_all(buffer, 'ep', split_axis=0, concat_axis=0, tiled=True)  42.6 us
    all_to_all x1, waiting for transfers between devices, routed(): lax.all_to_all(finished, 'ep', split_axis=0, concat_axis=0, tiled=True)  32.3 us
    dot_general x1, matrix products, expert_work(): jnp.einsum('secf,efd->secd', inner, w_down, preferred_element_type=jnp.fl...  6.91 us
    gather x1, local copies, waits for them, and re-layouts, routed(): jnp.take(results.reshape(experts * capacity, width), target, axis=0)  5.1 us
    all_to_all x1, starting transfers between devices, routed(): lax.all_to_all(finished, 'ep', split_axis=0, concat_axis=0, tiled=True)  4.95 us
    unnamed x17, local copies, waits for them, and re-layouts  3.77 us
    sub x1, matrix products, cached_attention(): expo = jnp.where(visible, jnp.exp(scores - top_score), 0.0)  3.29 us
    reduce_sum x1, other arithmetic, routed(): return jnp.sum(picked * gate_weights[:, :, None], axis=1)  2.66 us
  transfers between devices with their start and end apart: 1, of which 1 were waited for; matrix products, arithmetic and copies ran while one was open for 4% of the time, Pallas kernels for 0%

commit v1 on v0

--- a/solution.py
+++ b/solution.py
@@ -77,6 +77,104 @@
     return jnp.sum(picked * gate_weights[:, :, None], axis=1)
 
 
+def grid_of(devices):
+    cores = 2 if devices % 2 == 0 else 1
+    chips = devices // cores
+    minor = max(d for d in range(1, chips + 1) if chips % d == 0 and d * d <= chips)
+    return chips // minor, minor, cores
+
+
+def shifted(devices, dz, dy, dc):
+    zs, ys, cs = grid_of(devices)
+    pairs = []
+    for i in range(devices):
+        z, y, c = i // (ys * cs), i // cs % ys, i % cs
+        to = (((z + dz) % zs) * ys + (y + dy) % ys) * cs + (c + dc) % cs
+        pairs.append((i, to))
+    return pairs
+
+
+def send(x, dz, dy, dc):
+    return lax.ppermute(x, "ep", shifted(lax.axis_size("ep"), dz, dy, dc))
+
+
+def gathered(x):
+    zs, ys, cs = grid_of(lax.axis_size("ep"))
+    pieces = {(0, 0, 0): x}
+    for dy in range(1, ys):
+        pieces[0, dy, 0] = send(x, 0, dy, 0)
+    for dz in sorted(range(1, zs), key=lambda d: -min(d, zs - d)):
+        pieces[dz, 0, 0] = send(x, dz, 0, 0)
+    for dz in sorted(range(1, zs), key=lambda d: -min(d, zs - d)):
+        for dy in range(1, ys):
+            pieces[dz, dy, 0] = send(pieces[dz, 0, 0], 0, dy, 0)
+    for dz, dy, _ in list(pieces):
+        for dc in range(1, cs):
+            pieces[dz, dy, dc] = send(pieces[dz, dy, 0], 0, 0, dc)
+    return pieces
+
+
+def reduced(pieces):
+    zs, ys, cs = grid_of(lax.axis_size("ep"))
+
+    def joined(own, others):
+        total = own.astype(jnp.float32)
+        for other in others:
+            total = total + other.astype(jnp.float32)
+        return total
+
+    order = sorted(range(zs), key=lambda d: -min(d, zs - d))
+    by_z = []
+    for dz in order:
+        by_y = []
+        for dy in range(ys):
+            arrived = [send(pieces[dz, dy, dc], 0, 0, -dc) for dc in range(1, cs)]
+            by_y.append(joined(pieces[dz, dy, 0], arrived))
+        arrived = [send(by_y[dy].astype(jnp.bfloat16), 0, -dy, 0) for dy in range(1, ys)]
+        by_z.append(joined(by_y[0], arrived))
+    arrived = [
+        send(part.astype(jnp.bfloat16), -dz, 0, 0) for dz, part in zip(order, by_z) if dz
+    ]
+    return joined(by_z[order.index(0)], arrived)
+
+
+LANES = 128
+
+
+def spread(expert_ids, gate_weights, experts):
+    chosen = expert_ids[:, :, None] == jnp.arange(experts, dtype=jnp.int32)[None, None, :]
+    table = jnp.sum(jnp.where(chosen, gate_weights[:, :, None], 0.0), axis=1)
+    high = lax.reduce_precision(table, 8, 7)
+    middle = lax.reduce_precision(table - high, 8, 7)
+    low = table - high - middle
+    parts = jnp.concatenate([high, middle, low], axis=1).astype(jnp.bfloat16)
+    return jnp.pad(parts, ((0, 0), (0, -parts.shape[1] % LANES)))
+
+
+def dense(normed, expert_ids, gate_weights, w_gate, w_up, w_down):
+    devices = lax.axis_size("ep")
+    local_count, width = w_gate.shape[:2]
+    experts = devices * local_count
+    table = spread(expert_ids, gate_weights, experts)
+    pieces = gathered(jnp.concatenate([normed, table], axis=1))
+    names = list(pieces)
+    rows = jnp.concatenate([pieces[name] for name in names], axis=0)
+    blocks, table = rows[:, :width], rows[:, width:].astype(jnp.float32)
+    total = 0.0
+    for local in range(local_count):
+        expert = lax.axis_index("ep") * local_count + local
+        column = jnp.arange(table.shape[1], dtype=jnp.int32)
+        mine = (column % experts == expert) & (column < 3 * experts)
+        weight = jnp.sum(jnp.where(mine[None, :], table, 0.0), axis=1)
+        gate_part = jnp.dot(blocks, w_gate[local], preferred_element_type=jnp.float32)
+        up_part = jnp.dot(blocks, w_up[local], preferred_element_type=jnp.float32)
+        inner = (jax.nn.silu(gate_part) * up_part).astype(jnp.bfloat16)
+        out = jnp.dot(inner, w_down[local], preferred_element_type=jnp.float32)
+        total = total + weight[:, None] * out.astype(jnp.bfloat16).astype(jnp.float32)
+    total = total.astype(jnp.bfloat16).reshape(len(names), -1, width)
+    return reduced({name: total[i] for i, name in enumerate(names)})
+
+
 def layer_rows(
     hidden_in,
     queries,
@@ -97,7 +195,11 @@
     resid = hidden_in.astype(jnp.float32) + attention_output
     mean_square = jnp.mean(resid * resid, axis=-1, keepdims=True)
     normed = (resid * lax.rsqrt(mean_square + 1e-06) * norm_gain[None, :]).astype(jnp.bfloat16)
-    mixture = routed(normed, expert_ids, gate_weights, w_gate, w_up, w_down, capacity)
+    experts = lax.axis_size("ep") * w_gate.shape[0]
+    if 2 * expert_ids.shape[1] >= experts:
+        mixture = dense(normed, expert_ids, gate_weights, w_gate, w_up, w_down)
+    else:
+        mixture = routed(normed, expert_ids, gate_weights, w_gate, w_up, w_down, capacity)
     return (resid + mixture).astype(jnp.bfloat16)
 
 

time: 115 us -> 88.2 us (0.77)
  the two profiles are of different devices: /device:TPU:13 before, /device:TPU:0 now
where the time goes in v1:
time: 88.2 us; the launch traced here: 87.8 us
  starting transfers between devices  24.2 us (27%)
  waiting for transfers between devices  22 us (25%)
  local copies, waits for them, and re-layouts  18.2 us (21%)
  matrix products  17.9 us (20%)
  other arithmetic  5.32 us (6%)
    ppermute x30, starting transfers between devices, send(): return lax.ppermute(x, 'ep', shifted(lax.axis_size('ep'), dz, dy, dc))  24.2 us
    ppermute x30, waiting for transfers between devices, send(): return lax.ppermute(x, 'ep', shifted(lax.axis_size('ep'), dz, dy, dc))  22 us
    unnamed x28, local copies, waits for them, and re-layouts  16 us
    dot_general x1, matrix products, dense(): out = jnp.dot(inner, w_down[local], preferred_element_type=jnp.float32)  8.29 us
    dot_general x1, matrix products, dense(): up_part = jnp.dot(blocks, w_up[local], preferred_element_type=jnp.float32)  4.57 us
    sub x1, matrix products, cached_attention(): expo = jnp.where(visible, jnp.exp(scores - top_score), 0.0)  3.29 us
  transfers between devices with their start and end apart: 30, of which 10 were waited for; matrix products, arithmetic and copies ran while one was open for 17% of the time, Pallas kernels for 0%

profile of v1, /device:TPU:0, one launch (start us, length us, event | category | flops | bytes accessed | tf_op | source)
XLA Modules:
  0.0 87.8 jit_solution(5669509191647490571)
XLA Ops:
  0.0 1.1 %copy.26 = bf16[4,8,16,128]{3,2,1,0:T(8,128)(2,1)S(1)} copy(bf16[4,8,16,128]{3,1,2,0:T(8,128)(2,1)} %bitcast.51) | data formatting | bytes 262144
  1.1 0.7 iota_compare_fusion.2
  1.9 3.3 %fusion.38 = (f32[32,2,8]{2,1,0:T(2,128)}, f32[32,2,8,64]{3,2,1,0:T(8,128)}) fusion(pred[32,64]{1,0:T(8,128)(4,1)S(1)} %iota_compare_fusion.2, bf16[32,2,8,128]{3,2,1,0:T(8,128)(2,1)S(1)} %bitcast.52, bf16[32,64,256]{2,1,0:T(8,128)(2,1)} %param.13), kind=kOutput, calls=%fused_computation.70 | convolution fusion | flops 8552511 | bytes 1314816 | tf_op jit(solution)/shard_map/sub | solution.py:28
  5.1 1.8 %fusion.18 = f32[32,2,8,128]{3,2,1,0:T(8,128)S(1)} fusion(f32[32,2,8,64]{3,2,1,0:T(8,128)} %get-tuple-element.26, f32[32,2,8]{2,1,0:T(2,128)} %get-tuple-element.25, bf16[32,64,256]{2,1,0:T(8,128)(2,1)} %param.14), kind=kOutput, calls=%fused_computation.17 | convolution fusion | flops 8454144 | bytes 1443840 | tf_op jit(solution)/shard_map/nkgc,nckd->nkgd/dot_general | solution.py:30
  6.9 0.2 multiply_reduce_fusion
  7.2 0.7 copy.23
  7.9 0.8 multiply_convert_fusion.3
  8.7 1.4 %fusion.33 = (bf16[32,2176]{1,0:T(8,128)(2,1)}, bf16[512,2176]{1,0:T(8,128)(2,1)}) fusion(bf16[32,48]{1,0:T(8,128)(2,1)} %copy.23, bf16[32,2048]{1,0:T(8,128)(2,1)S(1)} %multiply_convert_fusion.3), kind=kLoop, calls=%fused_computation.38 | loop fusion | flops 417791 | bytes 412672 | tf_op jit(solution)/shard_map/concatenate | solution.py:159
  10.1 3.0 %collective-permute-start = (bf16[32,2176]{1,0:T(8,128)(2,1)}, bf16[32,2176]{1,0:T(8,128)(2,1)}, u32[]{:S(2)}, u32[]{:S(2)}) collective-permute-start(bf16[32,2176]{1,0:T(8,128)(2,1)} %get-tuple-element.20), channel_id=1, source_target_pairs={{0,2},{1,3},{2,0},{3,1},{4,6},{5,7},{6,4},{7,5},{8,10},{9,11},{10,... | collective-permute-start | bytes 417800 | tf_op jit(solution)/shard_map/ppermute | solution.py:98
  13.1 2.6 %collective-permute-start.1 = (bf16[32,2176]{1,0:T(8,128)(2,1)}, bf16[32,2176]{1,0:T(8,128)(2,1)}, u32[]{:S(2)}, u32[]{:S(2)}) collective-permute-start(bf16[32,2176]{1,0:T(8,128)(2,1)} %get-tuple-element.20), channel_id=1, source_target_pairs={{0,8},{1,9},{2,10},{3,11},{4,12},{5,13},{6,14},{7,15},{8,0},{9,1},... | collective-permute-start | bytes 417800 | tf_op jit(solution)/shard_map/ppermute | solution.py:98
  15.7 1.6 %collective-permute-start.2 = (bf16[32,2176]{1,0:T(8,128)(2,1)}, bf16[32,2176]{1,0:T(8,128)(2,1)}, u32[]{:S(2)}, u32[]{:S(2)}) collective-permute-start(bf16[32,2176]{1,0:T(8,128)(2,1)} %get-tuple-element.20), channel_id=1, source_target_pairs={{0,4},{1,5},{2,6},{3,7},{4,8},{5,9},{6,10},{7,11},{8,12},{9,13},{1... | collective-permute-start | bytes 417800 | tf_op jit(solution)/shard_map/ppermute | solution.py:98
  17.3 2.2 %collective-permute-start.3 = (bf16[32,2176]{1,0:T(8,128)(2,1)}, bf16[32,2176]{1,0:T(8,128)(2,1)}, u32[]{:S(2)}, u32[]{:S(2)}) collective-permute-start(bf16[32,2176]{1,0:T(8,128)(2,1)} %get-tuple-element.20), channel_id=1, source_target_pairs={{0,12},{1,13},{2,14},{3,15},{4,0},{5,1},{6,2},{7,3},{8,4},{9,5},{1... | collective-permute-start | bytes 417800 | tf_op jit(solution)/shard_map/ppermute | solution.py:98
  19.5 0.6 collective-permute-start.8
  20.1 1.9 %constant_dynamic-update-slice_fusion.14 = bf16[512,2176]{1,0:T(8,128)(2,1)} fusion(bf16[512,2176]{1,0:T(8,128)(2,1)} %get-tuple-element.21, bf16[32,2176]{1,0:T(8,128)(2,1)} %collective-permute-done), kind=kLoop, calls=%fused_computation.56 | loop fusion | bytes 278528
  22.0 4.6 %collective-permute-done.1 = bf16[32,2176]{1,0:T(8,128)(2,1)} collective-permute-done((bf16[32,2176]{1,0:T(8,128)(2,1)}, bf16[32,2176]{1,0:T(8,128)(2,1)}, u32[]{:S(2)}, u32[]{:S(2)}) %collective-permute-start.1) | collective-permute-done | bytes 139296 | tf_op jit(solution)/shard_map/ppermute | solution.py:98
  26.6 0.5 collective-permute-start.4
  27.1 1.6 %constant_dynamic-update-slice_fusion.13 = bf16[512,2176]{1,0:T(8,128)(2,1)} fusion(bf16[512,2176]{1,0:T(8,128)(2,1)} %constant_dynamic-update-slice_fusion.14, bf16[32,2176]{1,0:T(8,128)(2,1)} %collective-permute-done.1), kind=kLoop, calls=%fused_computation.55 | loop fusion | bytes 278528
  28.7 1.5 %collective-permute-start.5 = (bf16[32,2176]{1,0:T(8,128)(2,1)}, bf16[32,2176]{1,0:T(8,128)(2,1)S(1)}, u32[]{:S(2)}, u32[]{:S(2)}) collective-permute-start(bf16[32,2176]{1,0:T(8,128)(2,1)} %collective-permute-done.2), channel_id=1, source_target_pairs={{0,2},{1,3},{2,0},{3,1},{4,6},{5,7},{6,4},{7,5},{8,10},{9,11},{10,... | collective-permute-start | bytes 417800 | tf_op jit(solution)/shard_map/ppermute | solution.py:98
  30.2 1.6 %constant_dynamic-update-slice_fusion.12 = bf16[512,2176]{1,0:T(8,128)(2,1)} fusion(bf16[512,2176]{1,0:T(8,128)(2,1)} %constant_dynamic-update-slice_fusion.13, bf16[32,2176]{1,0:T(8,128)(2,1)} %collective-permute-done.2), kind=kLoop, calls=%fused_computation.54 | loop fusion | bytes 278528
  31.8 0.5 collective-permute-start.6
  32.3 1.6 %constant_dynamic-update-slice_fusion.11 = bf16[512,2176]{1,0:T(8,128)(2,1)} fusion(bf16[512,2176]{1,0:T(8,128)(2,1)} %constant_dynamic-update-slice_fusion.12, bf16[32,2176]{1,0:T(8,128)(2,1)} %collective-permute-done.3), kind=kLoop, calls=%fused_computation.53 | loop fusion | bytes 278528
  33.9 0.7 constant_dynamic-update-slice_fusion.10
  34.6 0.4 collective-permute-done.5
  35.0 0.1 collective-permute-start.10
  35.1 0.7 constant_dynamic-update-slice_fusion.9
  35.8 1.3 %collective-permute-done.6 = bf16[32,2176]{1,0:T(8,128)(2,1)S(1)} collective-permute-done((bf16[32,2176]{1,0:T(8,128)(2,1)}, bf16[32,2176]{1,0:T(8,128)(2,1)S(1)}, u32[]{:S(2)}, u32[]{:S(2)}) %collective-permute-start.6) | collective-permute-done | bytes 139296 | tf_op jit(solution)/shard_map/ppermute | solution.py:98
  37.1 0.7 constant_dynamic-update-slice_fusion.8
  37.8 0.5 collective-permute-start.12
  38.3 1.6 %constant_dynamic-update-slice_fusion.7 = bf16[512,2176]{1,0:T(8,128)(2,1)} fusion(bf16[512,2176]{1,0:T(8,128)(2,1)} %constant_dynamic-update-slice_fusion.8, bf16[32,2176]{1,0:T(8,128)(2,1)} %collective-permute-done.7), kind=kLoop, calls=%fused_computation.49 | loop fusion | bytes 278528
  39.8 0.7 constant_dynamic-update-slice_fusion.6
  40.5 0.5 collective-permute-start.14
  41.0 0.7 constant_dynamic-update-slice_fusion.5
  41.7 0.7 constant_dynamic-update-slice_fusion.4
  42.4 0.7 constant_dynamic-update-slice_fusion.3
  43.0 0.7 constant_dynamic-update-slice_fusion.2
  43.7 0.7 constant_dynamic-update-slice_fusion.1
  44.4 0.6 constant_dynamic-update-slice_fusion
  45.0 4.6 %fusion.3 = f32[512,768]{1,0:T(8,128)} fusion(bf16[1,2048,768]{2,1,0:T(8,128)(2,1)S(1)} %copy-done.5, bf16[512,2176]{1,0:T(8,128)(2,1)} %constant_dynamic-update-slice_fusion), kind=kOutput, calls=%fused_computation.4 | convolution fusion | flops 1610612736 | bytes 6815744 | tf_op jit(solution)/shard_map/dot_general | solution.py:170
  49.6 1.0 %select_reduce_fusion = f32[512]{0:T(512)S(1)} fusion(bf16[512,2176]{1,0:T(8,128)(2,1)} %constant_dynamic-update-slice_fusion, pred[128]{0:T(512)(128)(4,1)S(1)} %compare_and_fusion), kind=kLoop, calls=%fused_computation.34 | loop fusion | flops 196096 | bytes 133248 | tf_op jit(solution)/shard_map/reduce_sum | solution.py:168
  50.6 8.3 %multiply_convert_fusion = bf16[512,2048]{1,0:T(8,128)(2,1)} fusion(bf16[1,768,2048]{2,1,0:T(8,128)(2,1)S(1)} %copy-done, f32[512]{0:T(512)S(1)} %select_reduce_fusion, f32[512,768]{1,0:T(8,128)} %fusion.3, bf16[1,2048,768]{2,1,0:T(8,128)(2,1)} %param.19, bf16[512,2176]{1,0:T(8,128)(2,1)} %constant_dynamic-update-slice_fusion), kind=kOutput, calls=%fused_computation.1 | convolution fusion | flops 3227779072 | bytes 12060672 | tf_op jit(solution)/shard_map/dot_general | solution.py:172
  58.9 1.5 %fusion.37 = (bf16[32,2048]{1,0:T(8,128)(2,1)S(1)}, bf16[32,2048]{1,0:T(8,128)(2,1)S(1)}, bf16[32,2048]{1,0:T(8,128)(2,1)S(1)}, bf16[32,2048]{1,0:T(8,128)(2,1)S...) fusion(bf16[512,2048]{1,0:T(8,128)(2,1)} %multiply_convert_fusion), kind=kLoop, calls=%fused_computation.69 | loop fusion | bytes 2097152 | tf_op jit(solution)/shard_map/slice | solution.py:175
  60.5 0.5 collective-permute-start.19
  61.0 0.1 collective-permute-start.23
  61.1 0.4 collective-permute-start.27
  61.5 0.1 collective-permute-start.18
  61.6 0.2 collective-permute-done.16
  61.8 0.2 collective-permute-start.22
  62.0 0.3 collective-permute-start.26
  62.4 0.2 collective-permute-done.27
  62.5 0.1 add_convert_fusion.7
  62.7 1.1 %collective-permute-start.20 = (bf16[32,2048]{1,0:T(8,128)(2,1)S(1)}, bf16[32,2048]{1,0:T(8,128)(2,1)S(1)}, u32[]{:S(2)}, u32[]{:S(2)}) collective-permute-start(bf16[32,2048]{1,0:T(8,128)(2,1)S(1)} %get-tuple-element.16), channel_id=1, source_target_pairs={{0,2},{1,3},{2,0},{3,1},{4,6},{5,7},{6,4},{7,5},{8,10},{9,11},{10,... | collective-permute-start | bytes 393224 | tf_op jit(solution)/shard_map/ppermute | solution.py:98
  63.8 1.0 %collective-permute-start.24 = (bf16[32,2048]{1,0:T(8,128)(2,1)S(1)}, bf16[32,2048]{1,0:T(8,128)(2,1)S(1)}, u32[]{:S(2)}, u32[]{:S(2)}) collective-permute-start(bf16[32,2048]{1,0:T(8,128)(2,1)S(1)} %get-tuple-element.15), channel_id=1, source_target_pairs={{0,2},{1,3},{2,0},{3,1},{4,6},{5,7},{6,4},{7,5},{8,10},{9,11},{10,... | collective-permute-start | bytes 393224 | tf_op jit(solution)/shard_map/ppermute | solution.py:98
  64.8 1.0 %collective-permute-start.28 = (bf16[32,2048]{1,0:T(8,128)(2,1)S(1)}, bf16[32,2048]{1,0:T(8,128)(2,1)S(1)}, u32[]{:S(2)}, u32[]{:S(2)}) collective-permute-start(bf16[32,2048]{1,0:T(8,128)(2,1)S(1)} %get-tuple-element.14), channel_id=1, source_target_pairs={{0,2},{1,3},{2,0},{3,1},{4,6},{5,7},{6,4},{7,5},{8,10},{9,11},{10,... | collective-permute-start | bytes 393224 | tf_op jit(solution)/shard_map/ppermute | solution.py:98
  65.8 1.1 %collective-permute-start.17 = (bf16[32,2048]{1,0:T(8,128)(2,1)S(1)}, bf16[32,2048]{1,0:T(8,128)(2,1)S(1)}, u32[]{:S(2)}, u32[]{:S(2)}) collective-permute-start(bf16[32,2048]{1,0:T(8,128)(2,1)S(1)} %get-tuple-element.13), channel_id=1, source_target_pairs={{0,2},{1,3},{2,0},{3,1},{4,6},{5,7},{6,4},{7,5},{8,10},{9,11},{10,... | collective-permute-start | bytes 393224 | tf_op jit(solution)/shard_map/ppermute | solution.py:98
  66.9 2.2 %collective-permute-done.20 = bf16[32,2048]{1,0:T(8,128)(2,1)S(1)} collective-permute-done((bf16[32,2048]{1,0:T(8,128)(2,1)S(1)}, bf16[32,2048]{1,0:T(8,128)(2,1)S(1)}, u32[]{:S(2)}, u32[]{:S(2)}) %collective-permute-start.20) | collective-permute-done | bytes 131104 | tf_op jit(solution)/shard_map/ppermute | solution.py:98
  69.1 2.8 %collective-permute-done.24 = bf16[32,2048]{1,0:T(8,128)(2,1)S(1)} collective-permute-done((bf16[32,2048]{1,0:T(8,128)(2,1)S(1)}, bf16[32,2048]{1,0:T(8,128)(2,1)S(1)}, u32[]{:S(2)}, u32[]{:S(2)}) %collective-permute-start.24) | collective-permute-done | bytes 131104 | tf_op jit(solution)/shard_map/ppermute | solution.py:98
  71.9 2.8 %collective-permute-done.28 = bf16[32,2048]{1,0:T(8,128)(2,1)S(1)} collective-permute-done((bf16[32,2048]{1,0:T(8,128)(2,1)S(1)}, bf16[32,2048]{1,0:T(8,128)(2,1)S(1)}, u32[]{:S(2)}, u32[]{:S(2)}) %collective-permute-start.28) | collective-permute-done | bytes 131104 | tf_op jit(solution)/shard_map/ppermute | solution.py:98
  74.7 0.1 add_convert_fusion.5
  74.9 2.8 %collective-permute-start.21 = (bf16[32,2048]{1,0:T(8,128)(2,1)S(1)}, bf16[32,2048]{1,0:T(8,128)(2,1)S(1)}, u32[]{:S(2)}, u32[]{:S(2)}) collective-permute-start(bf16[32,2048]{1,0:T(8,128)(2,1)S(1)} %get-tuple-element.17), channel_id=1, source_target_pairs={{0,8},{1,9},{2,10},{3,11},{4,12},{5,13},{6,14},{7,15},{8,0},{9,1},... | collective-permute-start | bytes 393224 | tf_op jit(solution)/shard_map/ppermute | solution.py:98
  77.6 0.4 collective-permute-start.25
  78.1 1.6 %collective-permute-start.29 = (bf16[32,2048]{1,0:T(8,128)(2,1)S(1)}, bf16[32,2048]{1,0:T(8,128)(2,1)S(1)}, u32[]{:S(2)}, u32[]{:S(2)}) collective-permute-start(bf16[32,2048]{1,0:T(8,128)(2,1)S(1)} %get-tuple-element.18), channel_id=1, source_target_pairs={{0,4},{1,5},{2,6},{3,7},{4,8},{5,9},{6,10},{7,11},{8,12},{9,13},{1... | collective-permute-start | bytes 393224 | tf_op jit(solution)/shard_map/ppermute | solution.py:98
  79.7 6.8 %collective-permute-done.21 = bf16[32,2048]{1,0:T(8,128)(2,1)S(1)} collective-permute-done((bf16[32,2048]{1,0:T(8,128)(2,1)S(1)}, bf16[32,2048]{1,0:T(8,128)(2,1)S(1)}, u32[]{:S(2)}, u32[]{:S(2)}) %collective-permute-start.21) | collective-permute-done | bytes 131104 | tf_op jit(solution)/shard_map/ppermute | solution.py:98
  86.4 0.5 collective-permute-done.25
  87.0 0.8 add_convert_fusion
  (43 shorter events, 0.2 us)
Async XLA Ops:
  0.0 50.6 %copy-start = (bf16[1,768,2048]{2,1,0:T(8,128)(2,1)S(1)}, bf16[1,768,2048]{2,1,0:T(8,128)(2,1)}, u32[]{:S(2)}) copy-start(bf16[1,768,2048]{2,1,0:T(8,128)(2,1)} %param.21) | copy-start | bytes 9437188
  0.0 6.9 %copy-start.2 = (bf16[32,2048]{1,0:T(8,128)(2,1)S(1)}, bf16[32,2048]{1,0:T(8,128)(2,1)}, u32[]{:S(2)}) copy-start(bf16[32,2048]{1,0:T(8,128)(2,1)} %param.11) | copy-start | bytes 393220
  1.1 6.0 %copy-start.3 = (f32[32,8]{0,1:T(8,128)S(1)}, f32[32,8]{0,1:T(8,128)}, u32[]{:S(2)}) copy-start(f32[32,8]{0,1:T(8,128)} %param.18) | copy-start | bytes 3076
  1.1 6.0 %copy-start.4 = (s32[32,8]{0,1:T(8,128)S(1)}, s32[32,8]{0,1:T(8,128)}, u32[]{:S(2)}) copy-start(s32[32,8]{0,1:T(8,128)} %param.17) | copy-start | bytes 3076
  10.1 9.4 %collective-permute-start = (bf16[32,2176]{1,0:T(8,128)(2,1)}, bf16[32,2176]{1,0:T(8,128)(2,1)}, u32[]{:S(2)}, u32[]{:S(2)}) collective-permute-start(bf16[32,2176]{1,0:T(8,128)(2,1)} %get-tuple-element.20), channel_id=1, source_target_pairs={{0,2},{1,3},{2,0},{3,1},{4,6},{5,7},{6,4},{7,5},{8,10},{9,11},{10,... | collective-permute-start | bytes 417800 | tf_op jit(solution)/shard_map/ppermute | solution.py:98
  13.1 13.5 %collective-permute-start.1 = (bf16[32,2176]{1,0:T(8,128)(2,1)}, bf16[32,2176]{1,0:T(8,128)(2,1)}, u32[]{:S(2)}, u32[]{:S(2)}) collective-permute-start(bf16[32,2176]{1,0:T(8,128)(2,1)} %get-tuple-element.20), channel_id=1, source_target_pairs={{0,8},{1,9},{2,10},{3,11},{4,12},{5,13},{6,14},{7,15},{8,0},{9,1},... | collective-permute-start | bytes 417800 | tf_op jit(solution)/shard_map/ppermute | solution.py:98
  15.7 13.0 %collective-permute-start.2 = (bf16[32,2176]{1,0:T(8,128)(2,1)}, bf16[32,2176]{1,0:T(8,128)(2,1)}, u32[]{:S(2)}, u32[]{:S(2)}) collective-permute-start(bf16[32,2176]{1,0:T(8,128)(2,1)} %get-tuple-element.20), channel_id=1, source_target_pairs={{0,4},{1,5},{2,6},{3,7},{4,8},{5,9},{6,10},{7,11},{8,12},{9,13},{1... | collective-permute-start | bytes 417800 | tf_op jit(solution)/shard_map/ppermute | solution.py:98
  17.3 14.6 %collective-permute-start.3 = (bf16[32,2176]{1,0:T(8,128)(2,1)}, bf16[32,2176]{1,0:T(8,128)(2,1)}, u32[]{:S(2)}, u32[]{:S(2)}) collective-permute-start(bf16[32,2176]{1,0:T(8,128)(2,1)} %get-tuple-element.20), channel_id=1, source_target_pairs={{0,12},{1,13},{2,14},{3,15},{4,0},{5,1},{6,2},{7,3},{8,4},{9,5},{1... | collective-permute-start | bytes 417800 | tf_op jit(solution)/shard_map/ppermute | solution.py:98
  19.5 18.3 %collective-permute-start.7 = (bf16[32,2176]{1,0:T(8,128)(2,1)}, bf16[32,2176]{1,0:T(8,128)(2,1)}, u32[]{:S(2)}, u32[]{:S(2)}) collective-permute-start(bf16[32,2176]{1,0:T(8,128)(2,1)} %get-tuple-element.20), channel_id=1, source_target_pairs={{0,1},{1,0},{2,3},{3,2},{4,5},{5,4},{6,7},{7,6},{8,9},{9,8},{10,11... | collective-permute-start | bytes 417800 | tf_op jit(solution)/shard_map/ppermute | solution.py:98
  19.5 25.5 %copy-start.5 = (bf16[1,2048,768]{2,1,0:T(8,128)(2,1)S(1)}, bf16[1,2048,768]{2,1,0:T(8,128)(2,1)}, u32[]{:S(2)}) copy-start(bf16[1,2048,768]{2,1,0:T(8,128)(2,1)} %param.20) | copy-start | bytes 9437188
  19.5 20.3 %collective-permute-start.8 = (bf16[32,2176]{1,0:T(8,128)(2,1)}, bf16[32,2176]{1,0:T(8,128)(2,1)S(1)}, u32[]{:S(2)}, u32[]{:S(2)}) collective-permute-start(bf16[32,2176]{1,0:T(8,128)(2,1)} %collective-permute-done), channel_id=1, source_target_pairs={{0,1},{1,0},{2,3},{3,2},{4,5},{5,4},{6,7},{7,6},{8,9},{9,8},{10,11... | collective-permute-start | bytes 417800 | tf_op jit(solution)/shard_map/ppermute | solution.py:98
  26.6 7.3 %collective-permute-start.4 = (bf16[32,2176]{1,0:T(8,128)(2,1)}, bf16[32,2176]{1,0:T(8,128)(2,1)S(1)}, u32[]{:S(2)}, u32[]{:S(2)}) collective-permute-start(bf16[32,2176]{1,0:T(8,128)(2,1)} %collective-permute-done.1), channel_id=1, source_target_pairs={{0,2},{1,3},{2,0},{3,1},{4,6},{5,7},{6,4},{7,5},{8,10},{9,11},{10,... | collective-permute-start | bytes 417800 | tf_op jit(solution)/shard_map/ppermute | solution.py:98
  28.7 6.3 %collective-permute-start.5 = (bf16[32,2176]{1,0:T(8,128)(2,1)}, bf16[32,2176]{1,0:T(8,128)(2,1)S(1)}, u32[]{:S(2)}, u32[]{:S(2)}) collective-permute-start(bf16[32,2176]{1,0:T(8,128)(2,1)} %collective-permute-done.2), channel_id=1, source_target_pairs={{0,2},{1,3},{2,0},{3,1},{4,6},{5,7},{6,4},{7,5},{8,10},{9,11},{10,... | collective-permute-start | bytes 417800 | tf_op jit(solution)/shard_map/ppermute | solution.py:98
  31.8 5.3 %collective-permute-start.6 = (bf16[32,2176]{1,0:T(8,128)(2,1)}, bf16[32,2176]{1,0:T(8,128)(2,1)S(1)}, u32[]{:S(2)}, u32[]{:S(2)}) collective-permute-start(bf16[32,2176]{1,0:T(8,128)(2,1)} %collective-permute-done.3), channel_id=1, source_target_pairs={{0,2},{1,3},{2,0},{3,1},{4,6},{5,7},{6,4},{7,5},{8,10},{9,11},{10,... | collective-permute-start | bytes 417800 | tf_op jit(solution)/shard_map/ppermute | solution.py:98
  33.9 6.6 %collective-permute-start.9 = (bf16[32,2176]{1,0:T(8,128)(2,1)}, bf16[32,2176]{1,0:T(8,128)(2,1)S(1)}, u32[]{:S(2)}, u32[]{:S(2)}) collective-permute-start(bf16[32,2176]{1,0:T(8,128)(2,1)} %collective-permute-done.1), channel_id=1, source_target_pairs={{0,1},{1,0},{2,3},{3,2},{4,5},{5,4},{6,7},{7,6},{8,9},{9,8},{10,11... | collective-permute-start | bytes 417800 | tf_op jit(solution)/shard_map/ppermute | solution.py:98
  35.0 6.7 %collective-permute-start.10 = (bf16[32,2176]{1,0:T(8,128)(2,1)}, bf16[32,2176]{1,0:T(8,128)(2,1)S(1)}, u32[]{:S(2)}, u32[]{:S(2)}) collective-permute-start(bf16[32,2176]{1,0:T(8,128)(2,1)} %collective-permute-done.2), channel_id=1, source_target_pairs={{0,1},{1,0},{2,3},{3,2},{4,5},{5,4},{6,7},{7,6},{8,9},{9,8},{10,11... | collective-permute-start | bytes 417800 | tf_op jit(solution)/shard_map/ppermute | solution.py:98
  37.1 5.3 %collective-permute-start.11 = (bf16[32,2176]{1,0:T(8,128)(2,1)}, bf16[32,2176]{1,0:T(8,128)(2,1)S(1)}, u32[]{:S(2)}, u32[]{:S(2)}) collective-permute-start(bf16[32,2176]{1,0:T(8,128)(2,1)} %collective-permute-done.3), channel_id=1, source_target_pairs={{0,1},{1,0},{2,3},{3,2},{4,5},{5,4},{6,7},{7,6},{8,9},{9,8},{10,11... | collective-permute-start | bytes 417800 | tf_op jit(solution)/shard_map/ppermute | solution.py:98
  37.8 5.3 %collective-permute-start.12 = (bf16[32,2176]{1,0:T(8,128)(2,1)S(1)}, bf16[32,2176]{1,0:T(8,128)(2,1)S(1)}, u32[]{:S(2)}, u32[]{:S(2)}) collective-permute-start(bf16[32,2176]{1,0:T(8,128)(2,1)S(1)} %collective-permute-done.4), channel_id=1, source_target_pairs={{0,1},{1,0},{2,3},{3,2},{4,5},{5,4},{6,7},{7,6},{8,9},{9,8},{10,11... | collective-permute-start | bytes 417800 | tf_op jit(solution)/shard_map/ppermute | solution.py:98
  39.8 3.9 %collective-permute-start.13 = (bf16[32,2176]{1,0:T(8,128)(2,1)S(1)}, bf16[32,2176]{1,0:T(8,128)(2,1)S(1)}, u32[]{:S(2)}, u32[]{:S(2)}) collective-permute-start(bf16[32,2176]{1,0:T(8,128)(2,1)S(1)} %collective-permute-done.5), channel_id=1, source_target_pairs={{0,1},{1,0},{2,3},{3,2},{4,5},{5,4},{6,7},{7,6},{8,9},{9,8},{10,11... | collective-permute-start | bytes 417800 | tf_op jit(solution)/shard_map/ppermute | solution.py:98
  40.5 3.8 %collective-permute-start.14 = (bf16[32,2176]{1,0:T(8,128)(2,1)S(1)}, bf16[32,2176]{1,0:T(8,128)(2,1)S(1)}, u32[]{:S(2)}, u32[]{:S(2)}) collective-permute-start(bf16[32,2176]{1,0:T(8,128)(2,1)S(1)} %collective-permute-done.6), channel_id=1, source_target_pairs={{0,1},{1,0},{2,3},{3,2},{4,5},{5,4},{6,7},{7,6},{8,9},{9,8},{10,11... | collective-permute-start | bytes 417800 | tf_op jit(solution)/shard_map/ppermute | solution.py:98
  58.9 3.6 %copy-start.1 = (bf16[512,2048]{1,0:T(8,128)(2,1)S(1)}, bf16[512,2048]{1,0:T(8,128)(2,1)}, u32[]{:S(2)}) copy-start(bf16[512,2048]{1,0:T(8,128)(2,1)} %multiply_convert_fusion) | copy-start | bytes 6291460
  60.4 1.4 %collective-permute-start.16 = (bf16[32,2048]{1,0:T(8,128)(2,1)S(1)}, bf16[32,2048]{1,0:T(8,128)(2,1)S(1)}, u32[]{:S(2)}, u32[]{:S(2)}) collective-permute-start(bf16[32,2048]{1,0:T(8,128)(2,1)S(1)} %get-tuple-element.12), channel_id=1, source_target_pairs={{0,1},{1,0},{2,3},{3,2},{4,5},{5,4},{6,7},{7,6},{8,9},{9,8},{10,11... | collective-permute-start | bytes 393224 | tf_op jit(solution)/shard_map/ppermute | solution.py:98
  60.5 1.5 %collective-permute-start.19 = (bf16[32,2048]{1,0:T(8,128)(2,1)S(1)}, bf16[32,2048]{1,0:T(8,128)(2,1)S(1)}, u32[]{:S(2)}, u32[]{:S(2)}) collective-permute-start(bf16[32,2048]{1,0:T(8,128)(2,1)S(1)} %get-tuple-element.10), channel_id=1, source_target_pairs={{0,1},{1,0},{2,3},{3,2},{4,5},{5,4},{6,7},{7,6},{8,9},{9,8},{10,11... | collective-permute-start | bytes 393224 | tf_op jit(solution)/shard_map/ppermute | solution.py:98
  61.0 1.4 %collective-permute-start.23 = (bf16[32,2048]{1,0:T(8,128)(2,1)S(1)}, bf16[32,2048]{1,0:T(8,128)(2,1)S(1)}, u32[]{:S(2)}, u32[]{:S(2)}) collective-permute-start(bf16[32,2048]{1,0:T(8,128)(2,1)S(1)} %get-tuple-element.8), channel_id=1, source_target_pairs={{0,1},{1,0},{2,3},{3,2},{4,5},{5,4},{6,7},{7,6},{8,9},{9,8},{10,11... | collective-permute-start | bytes 393224 | tf_op jit(solution)/shard_map/ppermute | solution.py:98
  61.1 1.5 %collective-permute-start.27 = (bf16[32,2048]{1,0:T(8,128)(2,1)S(1)}, bf16[32,2048]{1,0:T(8,128)(2,1)S(1)}, u32[]{:S(2)}, u32[]{:S(2)}) collective-permute-start(bf16[32,2048]{1,0:T(8,128)(2,1)S(1)} %get-tuple-element.6), channel_id=1, source_target_pairs={{0,1},{1,0},{2,3},{3,2},{4,5},{5,4},{6,7},{7,6},{8,9},{9,8},{10,11... | collective-permute-start | bytes 393224 | tf_op jit(solution)/shard_map/ppermute | solution.py:98
  61.5 3.3 %collective-permute-start.18 = (bf16[32,2048]{1,0:T(8,128)(2,1)S(1)}, bf16[32,2048]{1,0:T(8,128)(2,1)S(1)}, u32[]{:S(2)}, u32[]{:S(2)}) collective-permute-start(bf16[32,2048]{1,0:T(8,128)(2,1)S(1)} %get-tuple-element.11), channel_id=1, source_target_pairs={{0,1},{1,0},{2,3},{3,2},{4,5},{5,4},{6,7},{7,6},{8,9},{9,8},{10,11... | collective-permute-start | bytes 393224 | tf_op jit(solution)/shard_map/ppermute | solution.py:98
  61.8 3.9 %collective-permute-start.22 = (bf16[32,2048]{1,0:T(8,128)(2,1)S(1)}, bf16[32,2048]{1,0:T(8,128)(2,1)S(1)}, u32[]{:S(2)}, u32[]{:S(2)}) collective-permute-start(bf16[32,2048]{1,0:T(8,128)(2,1)S(1)} %get-tuple-element.9), channel_id=1, source_target_pairs={{0,1},{1,0},{2,3},{3,2},{4,5},{5,4},{6,7},{7,6},{8,9},{9,8},{10,11... | collective-permute-start | bytes 393224 | tf_op jit(solution)/shard_map/ppermute | solution.py:98
  62.0 3.8 %collective-permute-start.26 = (bf16[32,2048]{1,0:T(8,128)(2,1)S(1)}, bf16[32,2048]{1,0:T(8,128)(2,1)S(1)}, u32[]{:S(2)}, u32[]{:S(2)}) collective-permute-start(bf16[32,2048]{1,0:T(8,128)(2,1)S(1)} %get-tuple-element.7), channel_id=1, source_target_pairs={{0,1},{1,0},{2,3},{3,2},{4,5},{5,4},{6,7},{7,6},{8,9},{9,8},{10,11... | collective-permute-start | bytes 393224 | tf_op jit(solution)/shard_map/ppermute | solution.py:98
  62.7 6.4 %collective-permute-start.20 = (bf16[32,2048]{1,0:T(8,128)(2,1)S(1)}, bf16[32,2048]{1,0:T(8,128)(2,1)S(1)}, u32[]{:S(2)}, u32[]{:S(2)}) collective-permute-start(bf16[32,2048]{1,0:T(8,128)(2,1)S(1)} %get-tuple-element.16), channel_id=1, source_target_pairs={{0,2},{1,3},{2,0},{3,1},{4,6},{5,7},{6,4},{7,5},{8,10},{9,11},{10,... | collective-permute-start | bytes 393224 | tf_op jit(solution)/shard_map/ppermute | solution.py:98
  63.8 8.2 %collective-permute-start.24 = (bf16[32,2048]{1,0:T(8,128)(2,1)S(1)}, bf16[32,2048]{1,0:T(8,128)(2,1)S(1)}, u32[]{:S(2)}, u32[]{:S(2)}) collective-permute-start(bf16[32,2048]{1,0:T(8,128)(2,1)S(1)} %get-tuple-element.15), channel_id=1, source_target_pairs={{0,2},{1,3},{2,0},{3,1},{4,6},{5,7},{6,4},{7,5},{8,10},{9,11},{10,... | collective-permute-start | bytes 393224 | tf_op jit(solution)/shard_map/ppermute | solution.py:98
  64.8 10.0 %collective-permute-start.28 = (bf16[32,2048]{1,0:T(8,128)(2,1)S(1)}, bf16[32,2048]{1,0:T(8,128)(2,1)S(1)}, u32[]{:S(2)}, u32[]{:S(2)}) collective-permute-start(bf16[32,2048]{1,0:T(8,128)(2,1)S(1)} %get-tuple-element.14), channel_id=1, source_target_pairs={{0,2},{1,3},{2,0},{3,1},{4,6},{5,7},{6,4},{7,5},{8,10},{9,11},{10,... | collective-permute-start | bytes 393224 | tf_op jit(solution)/shard_map/ppermute | solution.py:98
  65.8 13.9 %collective-permute-start.15 = (bf16[32,2048]{1,0:T(8,128)(2,1)S(1)}, bf16[32,2048]{1,0:T(8,128)(2,1)S(1)}, u32[]{:S(2)}, u32[]{:S(2)}) collective-permute-start(bf16[32,2048]{1,0:T(8,128)(2,1)S(1)} %get-tuple-element.5), channel_id=1, source_target_pairs={{0,1},{1,0},{2,3},{3,2},{4,5},{5,4},{6,7},{7,6},{8,9},{9,8},{10,11... | collective-permute-start | bytes 393224 | tf_op jit(solution)/shard_map/ppermute | solution.py:98
  65.8 13.9 %collective-permute-start.17 = (bf16[32,2048]{1,0:T(8,128)(2,1)S(1)}, bf16[32,2048]{1,0:T(8,128)(2,1)S(1)}, u32[]{:S(2)}, u32[]{:S(2)}) collective-permute-start(bf16[32,2048]{1,0:T(8,128)(2,1)S(1)} %get-tuple-element.13), channel_id=1, source_target_pairs={{0,2},{1,3},{2,0},{3,1},{4,6},{5,7},{6,4},{7,5},{8,10},{9,11},{10,... | collective-permute-start | bytes 393224 | tf_op jit(solution)/shard_map/ppermute | solution.py:98
  74.9 11.5 %collective-permute-start.21 = (bf16[32,2048]{1,0:T(8,128)(2,1)S(1)}, bf16[32,2048]{1,0:T(8,128)(2,1)S(1)}, u32[]{:S(2)}, u32[]{:S(2)}) collective-permute-start(bf16[32,2048]{1,0:T(8,128)(2,1)S(1)} %get-tuple-element.17), channel_id=1, source_target_pairs={{0,8},{1,9},{2,10},{3,11},{4,12},{5,13},{6,14},{7,15},{8,0},{9,1},... | collective-permute-start | bytes 393224 | tf_op jit(solution)/shard_map/ppermute | solution.py:98
  77.6 9.3 %collective-permute-start.25 = (bf16[32,2048]{1,0:T(8,128)(2,1)S(1)}, bf16[32,2048]{1,0:T(8,128)(2,1)S(1)}, u32[]{:S(2)}, u32[]{:S(2)}) collective-permute-start(bf16[32,2048]{1,0:T(8,128)(2,1)S(1)} %get-tuple-element.19), channel_id=1, source_target_pairs={{0,12},{1,13},{2,14},{3,15},{4,0},{5,1},{6,2},{7,3},{8,4},{9,5},{1... | collective-permute-start | bytes 393224 | tf_op jit(solution)/shard_map/ppermute | solution.py:98
  78.1 8.9 %collective-permute-start.29 = (bf16[32,2048]{1,0:T(8,128)(2,1)S(1)}, bf16[32,2048]{1,0:T(8,128)(2,1)S(1)}, u32[]{:S(2)}, u32[]{:S(2)}) collective-permute-start(bf16[32,2048]{1,0:T(8,128)(2,1)S(1)} %get-tuple-element.18), channel_id=1, source_target_pairs={{0,4},{1,5},{2,6},{3,7},{4,8},{5,9},{6,10},{7,11},{8,12},{9,13},{1... | collective-permute-start | bytes 393224 | tf_op jit(solution)/shard_map/ppermute | solution.py:98

commit v2 on v0

--- a/solution.py
+++ b/solution.py
@@ -1,8 +1,11 @@
+import functools
 import math
 
 import jax
 import jax.numpy as jnp
 from jax import lax
+from jax.experimental import pallas as pl
+from jax.experimental.pallas import tpu as pltpu
 from jax.sharding import PartitionSpec as P
 
 QUERY_HEADS = 16
@@ -77,6 +80,302 @@
     return jnp.sum(picked * gate_weights[:, :, None], axis=1)
 
 
+def grid_of(devices):
+    cores = 2 if devices % 2 == 0 else 1
+    chips = devices // cores
+    minor = max(d for d in range(1, chips + 1) if chips % d == 0 and d * d <= chips)
+    return chips // minor, minor, cores
+
+
+def shifted(devices, dz, dy, dc):
+    zs, ys, cs = grid_of(devices)
+    pairs = []
+    for i in range(devices):
+        z, y, c = i // (ys * cs), i // cs % ys, i % cs
+        to = (((z + dz) % zs) * ys + (y + dy) % ys) * cs + (c + dc) % cs
+        pairs.append((i, to))
+    return pairs
+
+
+def send(x, dz, dy, dc):
+    return lax.ppermute(x, "ep", shifted(lax.axis_size("ep"), dz, dy, dc))
+
+
+def far_first(zs):
+    return sorted(range(zs), key=lambda d: (-min(d, zs - d), d))
+
+
+def gathered(x):
+    zs, ys, cs = grid_of(lax.axis_size("ep"))
+    pieces = {(0, 0, 0): x}
+    for dy in range(1, ys):
+        pieces[0, dy, 0] = send(x, 0, dy, 0)
+    for dz in far_first(zs):
+        if dz:
+            pieces[dz, 0, 0] = send(x, dz, 0, 0)
+    for dz in far_first(zs):
+        for dy in range(1, ys):
+            if dz:
+                pieces[dz, dy, 0] = send(pieces[dz, 0, 0], 0, dy, 0)
+    for dz, dy, _ in list(pieces):
+        for dc in range(1, cs):
+            pieces[dz, dy, dc] = send(pieces[dz, dy, 0], 0, 0, dc)
+    return pieces
+
+
+LANES = 128
+MIB = 1 << 20
+
+
+def attention_body(
+    lengths, hidden, queries, keys, values, gain, ids, gates, payload, resid, parts, *, experts
+):
+    rows, width = hidden.shape
+    _, slots, kv_width = keys.shape
+    head = LANES
+    kv_heads = kv_width // head
+    heads = width // head
+    group = heads // kv_heads
+    step = pl.program_id(0)
+    pair = LANES // slots
+    scale = 1.0 / math.sqrt(head)
+    f32 = jnp.float32
+
+    blocks = []
+    for g in range(kv_heads):
+        own = jnp.concatenate(
+            [queries[:, h * head : (h + 1) * head] for h in range(g * group, (g + 1) * group)],
+            axis=0,
+        )
+        blank = jnp.zeros_like(own)
+        blocks.append(
+            jnp.concatenate([own if i == g else blank for i in range(kv_heads)], axis=1)
+        )
+    stacked = jnp.concatenate(blocks, axis=0)
+    flat_keys = keys[...].reshape(rows * slots, kv_width)
+    flat_values = values[...].reshape(rows * slots, kv_width)
+    scores = lax.dot_general(
+        stacked, flat_keys, (((1,), (1,)), ((), ())), preferred_element_type=f32
+    )
+
+    request = lax.broadcasted_iota(jnp.int32, (rows, LANES), 0)
+    lane = lax.broadcasted_iota(jnp.int32, (rows, LANES), 1)
+    length = jnp.zeros((rows, LANES), jnp.int32)
+    for t in range(rows):
+        length = jnp.where(request == t, lengths[step * rows + t], length)
+    seen = (lane // slots == request % pair) & (lane % slots < length)
+    seen = jnp.concatenate([seen.astype(jnp.int32)] * heads, axis=0) != 0
+    slab = jnp.concatenate([request // pair] * heads, axis=0)
+    compact = scores[:, :LANES]
+    for j in range(1, rows // pair):
+        compact = jnp.where(slab == j, scores[:, j * LANES : (j + 1) * LANES], compact)
+    compact = jnp.where(seen, compact * scale, -1e30)
+    top = jnp.max(compact, axis=-1, keepdims=True)
+    expo = jnp.where(seen, jnp.exp(compact - top), 0.0)
+    probs = (expo / jnp.sum(expo, axis=-1, keepdims=True)).astype(jnp.bfloat16)
+    probs = probs.astype(f32)
+    wide = jnp.concatenate(
+        [jnp.where(slab == j, probs, 0.0).astype(jnp.bfloat16) for j in range(rows // pair)],
+        axis=1,
+    )
+    attended = jnp.dot(wide, flat_values, preferred_element_type=f32)
+
+    square = jnp.zeros((rows, LANES), f32)
+    for h in range(heads):
+        g = h // group
+        cols = slice(h * head, (h + 1) * head)
+        total = hidden[:, cols].astype(f32)
+        total = total + attended[h * rows : (h + 1) * rows, g * head : (g + 1) * head]
+        resid[:, cols] = total
+        square = square + total * total
+    mean_square = jnp.sum(square, axis=-1, keepdims=True) / width
+    inverse = lax.rsqrt(mean_square + 1e-06)
+    for h in range(heads):
+        cols = slice(h * head, (h + 1) * head)
+        payload[:, cols] = (resid[:, cols] * inverse * gain[:, cols]).astype(jnp.bfloat16)
+
+    all_rows = ids.shape[1]
+    top_count = ids.shape[0]
+    number = lax.broadcasted_iota(jnp.int32, (experts, all_rows), 0)
+    table = jnp.zeros((experts, all_rows), f32)
+    for k in range(top_count):
+        table = table + jnp.where(ids[k : k + 1, :] == number, gates[k : k + 1, :], 0.0)
+    high = table.astype(jnp.bfloat16).astype(f32)
+    middle = (table - high).astype(jnp.bfloat16).astype(f32)
+    low = table - high - middle
+    parts[...] = jnp.zeros_like(parts)
+    for i, part in enumerate((high, middle, low)):
+        parts[i * experts : (i + 1) * experts, :all_rows] = part
+    flipped = parts[...].T.astype(jnp.bfloat16)
+
+    for i in range(all_rows // rows):
+
+        @pl.when(step == i)
+        def _():
+            payload[:, width:] = flipped[i * rows : (i + 1) * rows, :]
+
+
+def attention(
+    hidden_in, queries, stored_keys, stored_values, stored_lengths, norm_gain, expert_ids,
+    gate_weights, experts,
+):
+    rows, width = hidden_in.shape
+    _, slots, kv_width = stored_keys.shape
+    block = MB_ROWS
+    whole = width + LANES
+
+    def row(columns):
+        return pl.BlockSpec((block, columns), lambda i, n: (i, 0))
+
+    def cache():
+        return pl.BlockSpec((block, slots, kv_width), lambda i, n: (i, 0, 0))
+
+    def full(shape):
+        return pl.BlockSpec(shape, lambda i, n: (0, 0))
+
+    return pl.pallas_call(
+        functools.partial(attention_body, experts=experts),
+        out_shape=(
+            jax.ShapeDtypeStruct((rows, whole), jnp.bfloat16),
+            jax.ShapeDtypeStruct((rows, width), jnp.float32),
+        ),
+        grid_spec=pltpu.PrefetchScalarGridSpec(
+            num_scalar_prefetch=1,
+            grid=(rows // block,),
+            in_specs=[
+                row(width),
+                row(width),
+                cache(),
+                cache(),
+                full((1, width)),
+                full((expert_ids.shape[1], rows)),
+                full((expert_ids.shape[1], rows)),
+            ],
+            out_specs=(row(whole), row(width)),
+            scratch_shapes=[pltpu.VMEM((LANES, LANES), jnp.float32)],
+        ),
+        compiler_params=pltpu.CompilerParams(vmem_limit_bytes=16 * MIB),
+        name="attention",
+    )(
+        stored_lengths,
+        hidden_in,
+        queries,
+        stored_keys,
+        stored_values,
+        norm_gain[None, :],
+        expert_ids.T,
+        gate_weights.T,
+    )
+
+
+TILE = 256
+
+
+def expert_body(*refs, count, experts, local_count):
+    pieces = refs[:count]
+    w_gate, w_up, w_down, away, kept, inner, weight = refs[count:]
+    width = w_gate.shape[1]
+    hidden = w_gate.shape[2]
+    rows = pieces[0].shape[0]
+    f32 = jnp.float32
+    x = jnp.concatenate([piece[:, :width] for piece in pieces], axis=0)
+    table = jnp.concatenate([piece[:, width:] for piece in pieces], axis=0).astype(f32)
+    lane = lax.broadcasted_iota(jnp.int32, table.shape, 1)
+    for local in range(local_count):
+        expert = lax.axis_index("ep") * local_count + local
+        mine = (
+            (lane == expert) | (lane == expert + experts) | (lane == expert + 2 * experts)
+        )
+        weight[...] = jnp.broadcast_to(
+            jnp.sum(jnp.where(mine, table, 0.0), axis=1, keepdims=True), weight.shape
+        )
+        for f in range(0, hidden, TILE):
+            cols = slice(f, f + TILE)
+            gate_part = jnp.dot(x, w_gate[local, :, cols], preferred_element_type=f32)
+            up_part = jnp.dot(x, w_up[local, :, cols], preferred_element_type=f32)
+            silu = gate_part / (1.0 + jnp.exp(-gate_part))
+            inner[:, cols] = (silu * up_part).astype(jnp.bfloat16)
+        mid = inner[...]
+        half = count // 2 * rows
+        for d in range(0, width, TILE):
+            cols = slice(d, d + TILE)
+            out = jnp.dot(mid, w_down[local, :, cols], preferred_element_type=f32)
+            out = out.astype(jnp.bfloat16).astype(f32)
+            for j in range(0, TILE, LANES):
+                part = slice(d + j, d + j + LANES)
+                scaled = out[:, j : j + LANES] * weight[...]
+                if local == 0:
+                    away_sum, kept_sum = scaled[:half], scaled[half:]
+                else:
+                    away_sum = away[:, part].astype(f32) + scaled[:half]
+                    kept_sum = kept[:, part] + scaled[half:]
+                away[:, part] = away_sum.astype(away.dtype)
+                kept[:, part] = kept_sum
+
+
+def expert_rows(pieces, w_gate, w_up, w_down, experts):
+    rows = pieces[0].shape[0]
+    local_count, width, hidden = w_gate.shape
+    count = len(pieces)
+    half = count // 2 * rows
+    vmem = pl.BlockSpec(memory_space=pltpu.VMEM)
+    return pl.pallas_call(
+        functools.partial(
+            expert_body, count=count, experts=experts, local_count=local_count
+        ),
+        out_shape=(
+            jax.ShapeDtypeStruct((half, width), jnp.bfloat16),
+            jax.ShapeDtypeStruct((count * rows - half, width), jnp.float32),
+        ),
+        in_specs=[vmem] * (count + 3),
+        out_specs=(vmem, vmem),
+        scratch_shapes=[
+            pltpu.VMEM((count * rows, hidden), jnp.bfloat16),
+            pltpu.VMEM((count * rows, LANES), jnp.float32),
+        ],
+        compiler_params=pltpu.CompilerParams(vmem_limit_bytes=40 * MIB),
+        cost_estimate=pl.CostEstimate(
+            flops=6 * count * rows * width * hidden * local_count,
+            bytes_accessed=6 * width * hidden * local_count,
+            transcendentals=count * rows * hidden,
+        ),
+        name="expert_rows",
+    )(*pieces, w_gate, w_up, w_down)
+
+
+def dense(payload, resid, w_gate, w_up, w_down):
+    devices = lax.axis_size("ep")
+    local_count, width = w_gate.shape[:2]
+    experts = devices * local_count
+    zs, ys, cs = grid_of(devices)
+    bf16, f32 = jnp.bfloat16, jnp.float32
+    rows = payload.shape[0]
+    pieces = gathered(payload)
+    order = far_first(zs)
+    near = [dz for dz in order if dz in (0, zs // 2)]
+    rest = [dz for dz in order if dz not in near]
+    total = resid
+    for chunk in (near, rest):
+        if not chunk:
+            continue
+        dys = list(range(1, ys)) + [0]
+        names = [(dz, dy, dc) for dc in (1, 0) for dy in dys for dz in chunk]
+        away, kept = expert_rows(
+            [pieces[name] for name in names], w_gate, w_up, w_down, experts
+        )
+        chip = kept + send(away, 0, 0, 1).astype(f32)
+        span = len(chunk) * rows
+        level = chip[(ys - 1) * span :]
+        for i, dy in enumerate(range(1, ys)):
+            level = level + send(
+                chip[i * span : (i + 1) * span].astype(bf16), 0, -dy, 0
+            ).astype(f32)
+        for i, dz in enumerate(chunk):
+            part = level[i * rows : (i + 1) * rows]
+            total = total + (send(part.astype(bf16), -dz, 0, 0).astype(f32) if dz else part)
+    return total.astype(bf16)
+
+
 def layer_rows(
     hidden_in,
     queries,
@@ -91,6 +390,14 @@
     w_down,
     capacity,
 ):
+    devices = lax.axis_size("ep")
+    experts = devices * w_gate.shape[0]
+    if 2 * expert_ids.shape[1] >= experts and grid_of(devices)[2] == 2 and 3 * experts <= LANES:
+        payload, resid = attention(
+            hidden_in, queries, stored_keys, stored_values, stored_lengths, norm_gain,
+            expert_ids, gate_weights, experts,
+        )
+        return dense(payload, resid, w_gate, w_up, w_down)
     attention_output = cached_attention(
         queries, stored_keys, stored_values, stored_lengths, QUERY_HEADS, KEY_VALUE_HEADS
     )

time: 115 us -> 75.5 us (0.66)
  the two profiles are of different devices: /device:TPU:13 before, /device:TPU:0 now
where the time goes in v2:
time: 75.5 us; the launch traced here: 75.1 us
  waiting for transfers between devices  33.3 us (44%)
  starting transfers between devices  20.3 us (27%)
  local copies, waits for them, and re-layouts  12.7 us (17%)
  Pallas kernels  7.53 us (10%)
  other arithmetic  1.06 us (1%)
    ppermute x22, waiting for transfers between devices, send(): return lax.ppermute(x, 'ep', shifted(lax.axis_size('ep'), dz, dy, dc))  33.3 us
    ppermute x22, starting transfers between devices, send(): return lax.ppermute(x, 'ep', shifted(lax.axis_size('ep'), dz, dy, dc))  20.3 us
    unnamed x24, local copies, waits for them, and re-layouts  12.6 us
    pallas_call x2, Pallas kernels, expert_rows(): pl.pallas_call(functools.partial(expert_body, count=count, experts=expert...  5.31 us
    pallas_call x1, Pallas kernels, attention(): pl.pallas_call(functools.partial(attention_body, experts=experts), out_sh...  2.23 us
  transfers between devices with their start and end apart: 22, of which 10 were waited for; matrix products, arithmetic and copies ran while one was open for 1% of the time, Pallas kernels for 7%

profile of v2, /device:TPU:0, one launch (start us, length us, event | category | flops | bytes accessed | tf_op | source)
XLA Modules:
  0.0 75.1 jit_solution(18061339094488723177)
XLA Ops:
  0.0 0.0 copy-start.4
  0.0 1.2 %copy-done.4 = bf16[32,64,256]{2,1,0:T(8,128)(2,1)S(1)} copy-done((bf16[32,64,256]{2,1,0:T(8,128)(2,1)S(1)}, bf16[32,64,256]{2,1,0:T(8,128)(2,1)}, u32[]{:S(2)}) %copy-start.4) | copy-done | bytes 1048600
  1.2 1.2 %copy-done.5 = bf16[32,64,256]{2,1,0:T(8,128)(2,1)S(1)} copy-done((bf16[32,64,256]{2,1,0:T(8,128)(2,1)S(1)}, bf16[32,64,256]{2,1,0:T(8,128)(2,1)}, u32[]{:S(2)}) %copy-start.5) | copy-done | bytes 1048600
  2.5 0.9 %copy-done.6 = bf16[32,2048]{1,0:T(8,128)(2,1)S(1)} copy-done((bf16[32,2048]{1,0:T(8,128)(2,1)S(1)}, bf16[32,2048]{1,0:T(8,128)(2,1)}, u32[]{:S(2)}) %copy-start.6) | copy-done | bytes 131096
  3.4 0.9 %copy-done.7 = bf16[32,2048]{1,0:T(8,128)(2,1)S(1)} copy-done((bf16[32,2048]{1,0:T(8,128)(2,1)S(1)}, bf16[32,2048]{1,0:T(8,128)(2,1)}, u32[]{:S(2)}) %copy-start.7) | copy-done | bytes 131096
  4.3 0.7 copy-done.8
  5.0 0.7 copy-done.9
  5.6 0.7 copy-done.10
  6.3 0.7 copy-done.11
  7.0 2.2 %attention.1 = (bf16[32,2176]{1,0:T(8,128)(2,1)S(1)}, f32[32,2048]{1,0:T(8,128)S(1)}) custom-call(s32[32]{0:T(128)S(1)} %copy-done.11, bf16[32,2048]{1,0:T(8,128)(2,1)S(1)} %copy-done.6, bf16[32,2048]{1,0:T(8,128)(2,1)S(1)} %copy-done.7, bf16[32,64,256]{2,1,0:T(8,128)(2,1)S(1)} %copy-done.4, bf16[32,64,256]{2,1,0:T(8,128)(2,1)S(1)} %copy-done.5, ...), custom_call_target="tpu_custom_call" | custom-call | tf_op jit(solution)/shard_map/attention/pallas_call | solution.py:236
  9.2 3.1 %collective-permute-start.10 = (bf16[32,2176]{1,0:T(8,128)(2,1)S(1)}, bf16[32,2176]{1,0:T(8,128)(2,1)S(1)}, u32[]{:S(2)}, u32[]{:S(2)}) collective-permute-start(bf16[32,2176]{1,0:T(8,128)(2,1)S(1)} %get-tuple-element.12.refs_7_), channel_id=1, source_target_pairs={{0,4},{1,5},{2,6},{3,7},{4,8},{5,9},{6,10},{7,11},{8,12},{9,13},{1... | collective-permute-start | bytes 417800 | tf_op jit(solution)/shard_map/ppermute | solution.py:101
  12.3 2.1 %collective-permute-start.13 = (bf16[32,2176]{1,0:T(8,128)(2,1)S(1)}, bf16[32,2176]{1,0:T(8,128)(2,1)S(1)}, u32[]{:S(2)}, u32[]{:S(2)}) collective-permute-start(bf16[32,2176]{1,0:T(8,128)(2,1)S(1)} %get-tuple-element.12.refs_7_), channel_id=1, source_target_pairs={{0,12},{1,13},{2,14},{3,15},{4,0},{5,1},{6,2},{7,3},{8,4},{9,5},{1... | collective-permute-start | bytes 417800 | tf_op jit(solution)/shard_map/ppermute | solution.py:101
  14.4 4.5 %collective-permute-done.10.refs_6_ = bf16[32,2176]{1,0:T(8,128)(2,1)S(1)} collective-permute-done((bf16[32,2176]{1,0:T(8,128)(2,1)S(1)}, bf16[32,2176]{1,0:T(8,128)(2,1)S(1)}, u32[]{:S(2)}, u32[]{:S(2)}) %collective-permute-start.10) | collective-permute-done | bytes 139296 | tf_op jit(solution)/shard_map/ppermute | solution.py:101
  18.9 1.7 %collective-permute-start.11 = (bf16[32,2176]{1,0:T(8,128)(2,1)S(1)}, bf16[32,2176]{1,0:T(8,128)(2,1)S(1)}, u32[]{:S(2)}, u32[]{:S(2)}) collective-permute-start(bf16[32,2176]{1,0:T(8,128)(2,1)S(1)} %collective-permute-done.10.refs_6_), channel_id=1, source_target_pairs={{0,2},{1,3},{2,0},{3,1},{4,6},{5,7},{6,4},{7,5},{8,10},{9,11},{10,... | collective-permute-start | bytes 417800 | tf_op jit(solution)/shard_map/ppermute | solution.py:101
  20.6 0.0 collective-permute-done.13.refs_7_
  20.6 1.3 %collective-permute-start.14 = (bf16[32,2176]{1,0:T(8,128)(2,1)S(1)}, bf16[32,2176]{1,0:T(8,128)(2,1)S(1)}, u32[]{:S(2)}, u32[]{:S(2)}) collective-permute-start(bf16[32,2176]{1,0:T(8,128)(2,1)S(1)} %collective-permute-done.13.refs_7_), channel_id=1, source_target_pairs={{0,2},{1,3},{2,0},{3,1},{4,6},{5,7},{6,4},{7,5},{8,10},{9,11},{10,... | collective-permute-start | bytes 417800 | tf_op jit(solution)/shard_map/ppermute | solution.py:101
  22.0 0.0 collective-permute-start.16
  22.0 0.5 collective-permute-start.17
  22.5 3.0 %collective-permute-done.11.refs_4_ = bf16[32,2176]{1,0:T(8,128)(2,1)S(1)} collective-permute-done((bf16[32,2176]{1,0:T(8,128)(2,1)S(1)}, bf16[32,2176]{1,0:T(8,128)(2,1)S(1)}, u32[]{:S(2)}, u32[]{:S(2)}) %collective-permute-start.11) | collective-permute-done | bytes 139296 | tf_op jit(solution)/shard_map/ppermute | solution.py:101
  25.4 0.0 collective-permute-start.12
  25.4 1.5 %collective-permute-done.14.refs_5_ = bf16[32,2176]{1,0:T(8,128)(2,1)S(1)} collective-permute-done((bf16[32,2176]{1,0:T(8,128)(2,1)S(1)}, bf16[32,2176]{1,0:T(8,128)(2,1)S(1)}, u32[]{:S(2)}, u32[]{:S(2)}) %collective-permute-start.14) | collective-permute-done | bytes 139296 | tf_op jit(solution)/shard_map/ppermute | solution.py:101
  26.9 0.0 collective-permute-start.15
  26.9 1.4 %collective-permute-start = (bf16[32,2176]{1,0:T(8,128)(2,1)S(1)}, bf16[32,2176]{1,0:T(8,128)(2,1)S(1)}, u32[]{:S(2)}, u32[]{:S(2)}) collective-permute-start(bf16[32,2176]{1,0:T(8,128)(2,1)S(1)} %get-tuple-element.12.refs_7_), channel_id=1, source_target_pairs={{0,8},{1,9},{2,10},{3,11},{4,12},{5,13},{6,14},{7,15},{8,0},{9,1},... | collective-permute-start | bytes 417800 | tf_op jit(solution)/shard_map/ppermute | solution.py:101
  28.3 0.0 collective-permute-done.16.refs_2_
  28.3 0.0 collective-permute-done.17.refs_3_
  28.3 0.0 collective-permute-done.12.refs_0_
  28.3 0.0 collective-permute-done.15.refs_1_
  28.3 0.0 copy-start
  28.4 1.9 %copy-done = bf16[1,2048,768]{2,1,0:T(8,128)(2,1)S(1)} copy-done((bf16[1,2048,768]{2,1,0:T(8,128)(2,1)S(1)}, bf16[1,2048,768]{2,1,0:T(8,128)(2,1)}, u32[]{:S(2)}) %copy-start) | copy-done | bytes 3145752
  30.2 1.9 %copy-done.2 = bf16[1,2048,768]{2,1,0:T(8,128)(2,1)S(1)} copy-done((bf16[1,2048,768]{2,1,0:T(8,128)(2,1)S(1)}, bf16[1,2048,768]{2,1,0:T(8,128)(2,1)}, u32[]{:S(2)}) %copy-start.2) | copy-done | bytes 3145752
  32.1 1.9 %copy-done.3 = bf16[1,768,2048]{2,1,0:T(8,128)(2,1)S(1)} copy-done((bf16[1,768,2048]{2,1,0:T(8,128)(2,1)S(1)}, bf16[1,768,2048]{2,1,0:T(8,128)(2,1)}, u32[]{:S(2)}) %copy-start.3) | copy-done | bytes 3145752
  34.0 2.7 %expert_rows.3 = (bf16[128,2048]{1,0:T(8,128)(2,1)S(1)}, f32[128,2048]{1,0:T(8,128)S(1)}) custom-call(bf16[32,2176]{1,0:T(8,128)(2,1)S(1)} %collective-permute-done.12.refs_0_, bf16[32,2176]{1,0:T(8,128)(2,1)S(1)} %collective-permute-done.15.refs_1_, bf16[32,2176]{1,0:T(8,128)(2,1)S(1)} %collective-permute-done.16.refs_2_, ...), custom_call_target="tpu_custom_call" | custom-call | flops 2415919104 | bytes 9437184 | tf_op jit(solution)/shard_map/expert_rows/pallas_call | solution.py:322
  36.7 0.3 collective-permute-start.18
  37.0 1.5 %collective-permute-start.3 = (bf16[32,2176]{1,0:T(8,128)(2,1)S(1)}, bf16[32,2176]{1,0:T(8,128)(2,1)S(1)}, u32[]{:S(2)}, u32[]{:S(2)}) collective-permute-start(bf16[32,2176]{1,0:T(8,128)(2,1)S(1)} %get-tuple-element.12.refs_7_), channel_id=1, source_target_pairs={{0,2},{1,3},{2,0},{3,1},{4,6},{5,7},{6,4},{7,5},{8,10},{9,11},{10,... | collective-permute-start | bytes 417800 | tf_op jit(solution)/shard_map/ppermute | solution.py:101
  38.5 0.0 collective-permute-done.refs_6_
  38.5 0.5 collective-permute-start.1
  39.0 0.0 collective-permute-start.6
  39.0 0.5 collective-permute-start.5
  39.5 4.0 %collective-permute-done.3.refs_5_ = bf16[32,2176]{1,0:T(8,128)(2,1)S(1)} collective-permute-done((bf16[32,2176]{1,0:T(8,128)(2,1)S(1)}, bf16[32,2176]{1,0:T(8,128)(2,1)S(1)}, u32[]{:S(2)}, u32[]{:S(2)}) %collective-permute-start.3) | collective-permute-done | bytes 139296 | tf_op jit(solution)/shard_map/ppermute | solution.py:101
  43.5 0.0 collective-permute-start.4
  43.5 2.3 %collective-permute-done.1.refs_4_ = bf16[32,2176]{1,0:T(8,128)(2,1)S(1)} collective-permute-done((bf16[32,2176]{1,0:T(8,128)(2,1)S(1)}, bf16[32,2176]{1,0:T(8,128)(2,1)S(1)}, u32[]{:S(2)}, u32[]{:S(2)}) %collective-permute-start.1) | collective-permute-done | bytes 139296 | tf_op jit(solution)/shard_map/ppermute | solution.py:101
  45.8 0.0 collective-permute-start.2
  45.8 0.0 collective-permute-done.6.refs_3_
  45.8 0.0 collective-permute-done.5.refs_2_
  45.8 0.0 collective-permute-done.4.refs_1_
  45.8 1.3 %collective-permute-done.2.refs_0_ = bf16[32,2176]{1,0:T(8,128)(2,1)S(1)} collective-permute-done((bf16[32,2176]{1,0:T(8,128)(2,1)S(1)}, bf16[32,2176]{1,0:T(8,128)(2,1)S(1)}, u32[]{:S(2)}, u32[]{:S(2)}) %collective-permute-start.2) | collective-permute-done | bytes 139296 | tf_op jit(solution)/shard_map/ppermute | solution.py:101
  47.2 0.0 copy-done.1
  47.2 2.7 %expert_rows.2 = (bf16[128,2048]{1,0:T(8,128)(2,1)S(1)}, f32[128,2048]{1,0:T(8,128)S(1)}) custom-call(bf16[32,2176]{1,0:T(8,128)(2,1)S(1)} %collective-permute-done.2.refs_0_, bf16[32,2176]{1,0:T(8,128)(2,1)S(1)} %collective-permute-done.4.refs_1_, bf16[32,2176]{1,0:T(8,128)(2,1)S(1)} %collective-permute-done.5.refs_2_, ...), custom_call_target="tpu_custom_call" | custom-call | flops 2415919104 | bytes 9437184 | tf_op jit(solution)/shard_map/expert_rows/pallas_call | solution.py:322
  49.8 0.2 collective-permute-start.7
  50.1 0.0 collective-permute-done.18
  50.1 0.1 convert_add_fusion
  50.2 1.6 %collective-permute-start.19 = (bf16[64,2048]{1,0:T(8,128)(2,1)S(1)}, bf16[64,2048]{1,0:T(8,128)(2,1)S(1)}, u32[]{:S(2)}, u32[]{:S(2)}) collective-permute-start(bf16[64,2048]{1,0:T(8,128)(2,1)S(1)} %slice.59), channel_id=1, source_target_pairs={{0,2},{1,3},{2,0},{3,1},{4,6},{5,7},{6,4},{7,5},{8,10},{9,11},{10,... | collective-permute-start | bytes 786440 | tf_op jit(solution)/shard_map/ppermute | solution.py:101
  51.8 0.0 collective-permute-done.7
  51.8 0.1 convert_add_fusion.1
  52.0 1.6 %collective-permute-start.8 = (bf16[64,2048]{1,0:T(8,128)(2,1)S(1)}, bf16[64,2048]{1,0:T(8,128)(2,1)S(1)}, u32[]{:S(2)}, u32[]{:S(2)}) collective-permute-start(bf16[64,2048]{1,0:T(8,128)(2,1)S(1)} %slice.60), channel_id=1, source_target_pairs={{0,2},{1,3},{2,0},{3,1},{4,6},{5,7},{6,4},{7,5},{8,10},{9,11},{10,... | collective-permute-start | bytes 786440 | tf_op jit(solution)/shard_map/ppermute | solution.py:101
  53.5 5.9 %collective-permute-done.19 = bf16[64,2048]{1,0:T(8,128)(2,1)S(1)} collective-permute-done((bf16[64,2048]{1,0:T(8,128)(2,1)S(1)}, bf16[64,2048]{1,0:T(8,128)(2,1)S(1)}, u32[]{:S(2)}, u32[]{:S(2)}) %collective-permute-start.19) | collective-permute-done | bytes 262176 | tf_op jit(solution)/shard_map/ppermute | solution.py:101
  59.6 2.4 %collective-permute-start.20 = (bf16[32,2048]{1,0:T(8,128)(2,1)S(1)}, bf16[32,2048]{1,0:T(8,128)(2,1)S(1)}, u32[]{:S(2)}, u32[]{:S(2)}) collective-permute-start(bf16[32,2048]{1,0:T(8,128)(2,1)S(1)} %get-tuple-element.17), channel_id=1, source_target_pairs={{0,12},{1,13},{2,14},{3,15},{4,0},{5,1},{6,2},{7,3},{8,4},{9,5},{1... | collective-permute-start | bytes 393224 | tf_op jit(solution)/shard_map/ppermute | solution.py:101
  62.0 0.0 collective-permute-start.21
  62.0 2.5 %collective-permute-done.8 = bf16[64,2048]{1,0:T(8,128)(2,1)S(1)} collective-permute-done((bf16[64,2048]{1,0:T(8,128)(2,1)S(1)}, bf16[64,2048]{1,0:T(8,128)(2,1)S(1)}, u32[]{:S(2)}, u32[]{:S(2)}) %collective-permute-start.8) | collective-permute-done | bytes 262176 | tf_op jit(solution)/shard_map/ppermute | solution.py:101
  64.6 1.6 %collective-permute-start.9 = (bf16[32,2048]{1,0:T(8,128)(2,1)S(1)}, bf16[32,2048]{1,0:T(8,128)(2,1)S(1)}, u32[]{:S(2)}, u32[]{:S(2)}) collective-permute-start(bf16[32,2048]{1,0:T(8,128)(2,1)S(1)} %slice.61), channel_id=1, source_target_pairs={{0,8},{1,9},{2,10},{3,11},{4,12},{5,13},{6,14},{7,15},{8,0},{9,1},... | collective-permute-start | bytes 393224 | tf_op jit(solution)/shard_map/ppermute | solution.py:101
  66.2 0.0 collective-permute-done.20
  66.2 2.7 %collective-permute-done.21 = bf16[32,2048]{1,0:T(8,128)(2,1)S(1)} collective-permute-done((bf16[32,2048]{1,0:T(8,128)(2,1)S(1)}, bf16[32,2048]{1,0:T(8,128)(2,1)S(1)}, u32[]{:S(2)}, u32[]{:S(2)}) %collective-permute-start.21) | collective-permute-done | bytes 131104 | tf_op jit(solution)/shard_map/ppermute | solution.py:101
  68.9 5.5 %collective-permute-done.9 = bf16[32,2048]{1,0:T(8,128)(2,1)S(1)} collective-permute-done((bf16[32,2048]{1,0:T(8,128)(2,1)S(1)}, bf16[32,2048]{1,0:T(8,128)(2,1)S(1)}, u32[]{:S(2)}, u32[]{:S(2)}) %collective-permute-start.9) | collective-permute-done | bytes 131104 | tf_op jit(solution)/shard_map/ppermute | solution.py:101
  74.3 0.7 fusion.3
  (16 shorter events, 0.2 us)
Async XLA Ops:
  0.0 1.2 %copy-start.4 = (bf16[32,64,256]{2,1,0:T(8,128)(2,1)S(1)}, bf16[32,64,256]{2,1,0:T(8,128)(2,1)}, u32[]{:S(2)}) copy-start(bf16[32,64,256]{2,1,0:T(8,128)(2,1)} %keys.1) | copy-start | bytes 3145732
  1.2 1.2 %copy-start.5 = (bf16[32,64,256]{2,1,0:T(8,128)(2,1)S(1)}, bf16[32,64,256]{2,1,0:T(8,128)(2,1)}, u32[]{:S(2)}) copy-start(bf16[32,64,256]{2,1,0:T(8,128)(2,1)} %values.1) | copy-start | bytes 3145732
  2.5 0.9 %copy-start.6 = (bf16[32,2048]{1,0:T(8,128)(2,1)S(1)}, bf16[32,2048]{1,0:T(8,128)(2,1)}, u32[]{:S(2)}) copy-start(bf16[32,2048]{1,0:T(8,128)(2,1)} %hidden.1) | copy-start | bytes 393220
  3.4 0.9 %copy-start.7 = (bf16[32,2048]{1,0:T(8,128)(2,1)S(1)}, bf16[32,2048]{1,0:T(8,128)(2,1)}, u32[]{:S(2)}) copy-start(bf16[32,2048]{1,0:T(8,128)(2,1)} %queries.1) | copy-start | bytes 393220
  4.3 0.7 copy-start.8
  5.0 0.7 copy-start.9
  5.6 0.7 copy-start.10
  6.3 0.7 copy-start.11
  9.2 9.7 %collective-permute-start.10 = (bf16[32,2176]{1,0:T(8,128)(2,1)S(1)}, bf16[32,2176]{1,0:T(8,128)(2,1)S(1)}, u32[]{:S(2)}, u32[]{:S(2)}) collective-permute-start(bf16[32,2176]{1,0:T(8,128)(2,1)S(1)} %get-tuple-element.12.refs_7_), channel_id=1, source_target_pairs={{0,4},{1,5},{2,6},{3,7},{4,8},{5,9},{6,10},{7,11},{8,12},{9,13},{1... | collective-permute-start | bytes 417800 | tf_op jit(solution)/shard_map/ppermute | solution.py:101
  12.3 8.3 %collective-permute-start.13 = (bf16[32,2176]{1,0:T(8,128)(2,1)S(1)}, bf16[32,2176]{1,0:T(8,128)(2,1)S(1)}, u32[]{:S(2)}, u32[]{:S(2)}) collective-permute-start(bf16[32,2176]{1,0:T(8,128)(2,1)S(1)} %get-tuple-element.12.refs_7_), channel_id=1, source_target_pairs={{0,12},{1,13},{2,14},{3,15},{4,0},{5,1},{6,2},{7,3},{8,4},{9,5},{1... | collective-permute-start | bytes 417800 | tf_op jit(solution)/shard_map/ppermute | solution.py:101
  18.9 6.5 %collective-permute-start.11 = (bf16[32,2176]{1,0:T(8,128)(2,1)S(1)}, bf16[32,2176]{1,0:T(8,128)(2,1)S(1)}, u32[]{:S(2)}, u32[]{:S(2)}) collective-permute-start(bf16[32,2176]{1,0:T(8,128)(2,1)S(1)} %collective-permute-done.10.refs_6_), channel_id=1, source_target_pairs={{0,2},{1,3},{2,0},{3,1},{4,6},{5,7},{6,4},{7,5},{8,10},{9,11},{10,... | collective-permute-start | bytes 417800 | tf_op jit(solution)/shard_map/ppermute | solution.py:101
  20.6 6.3 %collective-permute-start.14 = (bf16[32,2176]{1,0:T(8,128)(2,1)S(1)}, bf16[32,2176]{1,0:T(8,128)(2,1)S(1)}, u32[]{:S(2)}, u32[]{:S(2)}) collective-permute-start(bf16[32,2176]{1,0:T(8,128)(2,1)S(1)} %collective-permute-done.13.refs_7_), channel_id=1, source_target_pairs={{0,2},{1,3},{2,0},{3,1},{4,6},{5,7},{6,4},{7,5},{8,10},{9,11},{10,... | collective-permute-start | bytes 417800 | tf_op jit(solution)/shard_map/ppermute | solution.py:101
  22.0 6.4 %collective-permute-start.16 = (bf16[32,2176]{1,0:T(8,128)(2,1)S(1)}, bf16[32,2176]{1,0:T(8,128)(2,1)S(1)}, u32[]{:S(2)}, u32[]{:S(2)}) collective-permute-start(bf16[32,2176]{1,0:T(8,128)(2,1)S(1)} %collective-permute-done.10.refs_6_), channel_id=1, source_target_pairs={{0,1},{1,0},{2,3},{3,2},{4,5},{5,4},{6,7},{7,6},{8,9},{9,8},{10,11... | collective-permute-start | bytes 417800 | tf_op jit(solution)/shard_map/ppermute | solution.py:101
  22.0 6.4 %collective-permute-start.17 = (bf16[32,2176]{1,0:T(8,128)(2,1)S(1)}, bf16[32,2176]{1,0:T(8,128)(2,1)S(1)}, u32[]{:S(2)}, u32[]{:S(2)}) collective-permute-start(bf16[32,2176]{1,0:T(8,128)(2,1)S(1)} %collective-permute-done.13.refs_7_), channel_id=1, source_target_pairs={{0,1},{1,0},{2,3},{3,2},{4,5},{5,4},{6,7},{7,6},{8,9},{9,8},{10,11... | collective-permute-start | bytes 417800 | tf_op jit(solution)/shard_map/ppermute | solution.py:101
  25.4 2.9 %collective-permute-start.12 = (bf16[32,2176]{1,0:T(8,128)(2,1)S(1)}, bf16[32,2176]{1,0:T(8,128)(2,1)S(1)}, u32[]{:S(2)}, u32[]{:S(2)}) collective-permute-start(bf16[32,2176]{1,0:T(8,128)(2,1)S(1)} %collective-permute-done.11.refs_4_), channel_id=1, source_target_pairs={{0,1},{1,0},{2,3},{3,2},{4,5},{5,4},{6,7},{7,6},{8,9},{9,8},{10,11... | collective-permute-start | bytes 417800 | tf_op jit(solution)/shard_map/ppermute | solution.py:101
  26.9 1.4 %collective-permute-start.15 = (bf16[32,2176]{1,0:T(8,128)(2,1)S(1)}, bf16[32,2176]{1,0:T(8,128)(2,1)S(1)}, u32[]{:S(2)}, u32[]{:S(2)}) collective-permute-start(bf16[32,2176]{1,0:T(8,128)(2,1)S(1)} %collective-permute-done.14.refs_5_), channel_id=1, source_target_pairs={{0,1},{1,0},{2,3},{3,2},{4,5},{5,4},{6,7},{7,6},{8,9},{9,8},{10,11... | collective-permute-start | bytes 417800 | tf_op jit(solution)/shard_map/ppermute | solution.py:101
  26.9 11.5 %collective-permute-start = (bf16[32,2176]{1,0:T(8,128)(2,1)S(1)}, bf16[32,2176]{1,0:T(8,128)(2,1)S(1)}, u32[]{:S(2)}, u32[]{:S(2)}) collective-permute-start(bf16[32,2176]{1,0:T(8,128)(2,1)S(1)} %get-tuple-element.12.refs_7_), channel_id=1, source_target_pairs={{0,8},{1,9},{2,10},{3,11},{4,12},{5,13},{6,14},{7,15},{8,0},{9,1},... | collective-permute-start | bytes 417800 | tf_op jit(solution)/shard_map/ppermute | solution.py:101
  28.3 1.9 %copy-start = (bf16[1,2048,768]{2,1,0:T(8,128)(2,1)S(1)}, bf16[1,2048,768]{2,1,0:T(8,128)(2,1)}, u32[]{:S(2)}) copy-start(bf16[1,2048,768]{2,1,0:T(8,128)(2,1)} %refs_8_.3) | copy-start | bytes 9437188
  30.2 1.9 %copy-start.2 = (bf16[1,2048,768]{2,1,0:T(8,128)(2,1)S(1)}, bf16[1,2048,768]{2,1,0:T(8,128)(2,1)}, u32[]{:S(2)}) copy-start(bf16[1,2048,768]{2,1,0:T(8,128)(2,1)} %refs_9_.3) | copy-start | bytes 9437188
  32.1 1.9 %copy-start.3 = (bf16[1,768,2048]{2,1,0:T(8,128)(2,1)S(1)}, bf16[1,768,2048]{2,1,0:T(8,128)(2,1)}, u32[]{:S(2)}) copy-start(bf16[1,768,2048]{2,1,0:T(8,128)(2,1)} %refs_10_.3) | copy-start | bytes 9437188
  34.0 13.2 %copy-start.1 = (bf16[1,2048,768]{2,1,0:T(8,128)(2,1)S(1)}, bf16[1,2048,768]{2,1,0:T(8,128)(2,1)}, u32[]{:S(2)}) copy-start(bf16[1,2048,768]{2,1,0:T(8,128)(2,1)} %refs_8_.3) | copy-start | bytes 9437188
  36.7 13.4 %collective-permute-start.18 = (bf16[128,2048]{1,0:T(8,128)(2,1)S(1)}, bf16[128,2048]{1,0:T(8,128)(2,1)S(1)}, u32[]{:S(2)}, u32[]{:S(2)}) collective-permute-start(bf16[128,2048]{1,0:T(8,128)(2,1)S(1)} %get-tuple-element.16), channel_id=1, source_target_pairs={{0,1},{1,0},{2,3},{3,2},{4,5},{5,4},{6,7},{7,6},{8,9},{9,8},{10,11... | collective-permute-start | bytes 1572872 | tf_op jit(solution)/shard_map/ppermute | solution.py:101
  37.0 6.5 %collective-permute-start.3 = (bf16[32,2176]{1,0:T(8,128)(2,1)S(1)}, bf16[32,2176]{1,0:T(8,128)(2,1)S(1)}, u32[]{:S(2)}, u32[]{:S(2)}) collective-permute-start(bf16[32,2176]{1,0:T(8,128)(2,1)S(1)} %get-tuple-element.12.refs_7_), channel_id=1, source_target_pairs={{0,2},{1,3},{2,0},{3,1},{4,6},{5,7},{6,4},{7,5},{8,10},{9,11},{10,... | collective-permute-start | bytes 417800 | tf_op jit(solution)/shard_map/ppermute | solution.py:101
  38.5 7.4 %collective-permute-start.1 = (bf16[32,2176]{1,0:T(8,128)(2,1)S(1)}, bf16[32,2176]{1,0:T(8,128)(2,1)S(1)}, u32[]{:S(2)}, u32[]{:S(2)}) collective-permute-start(bf16[32,2176]{1,0:T(8,128)(2,1)S(1)} %collective-permute-done.refs_6_), channel_id=1, source_target_pairs={{0,2},{1,3},{2,0},{3,1},{4,6},{5,7},{6,4},{7,5},{8,10},{9,11},{10,... | collective-permute-start | bytes 417800 | tf_op jit(solution)/shard_map/ppermute | solution.py:101
  39.0 6.8 %collective-permute-start.6 = (bf16[32,2176]{1,0:T(8,128)(2,1)S(1)}, bf16[32,2176]{1,0:T(8,128)(2,1)S(1)}, u32[]{:S(2)}, u32[]{:S(2)}) collective-permute-start(bf16[32,2176]{1,0:T(8,128)(2,1)S(1)} %get-tuple-element.12.refs_7_), channel_id=1, source_target_pairs={{0,1},{1,0},{2,3},{3,2},{4,5},{5,4},{6,7},{7,6},{8,9},{9,8},{10,11... | collective-permute-start | bytes 417800 | tf_op jit(solution)/shard_map/ppermute | solution.py:101
  39.0 6.8 %collective-permute-start.5 = (bf16[32,2176]{1,0:T(8,128)(2,1)S(1)}, bf16[32,2176]{1,0:T(8,128)(2,1)S(1)}, u32[]{:S(2)}, u32[]{:S(2)}) collective-permute-start(bf16[32,2176]{1,0:T(8,128)(2,1)S(1)} %collective-permute-done.refs_6_), channel_id=1, source_target_pairs={{0,1},{1,0},{2,3},{3,2},{4,5},{5,4},{6,7},{7,6},{8,9},{9,8},{10,11... | collective-permute-start | bytes 417800 | tf_op jit(solution)/shard_map/ppermute | solution.py:101
  43.5 2.3 %collective-permute-start.4 = (bf16[32,2176]{1,0:T(8,128)(2,1)S(1)}, bf16[32,2176]{1,0:T(8,128)(2,1)S(1)}, u32[]{:S(2)}, u32[]{:S(2)}) collective-permute-start(bf16[32,2176]{1,0:T(8,128)(2,1)S(1)} %collective-permute-done.3.refs_5_), channel_id=1, source_target_pairs={{0,1},{1,0},{2,3},{3,2},{4,5},{5,4},{6,7},{7,6},{8,9},{9,8},{10,11... | collective-permute-start | bytes 417800 | tf_op jit(solution)/shard_map/ppermute | solution.py:101
  45.8 1.4 %collective-permute-start.2 = (bf16[32,2176]{1,0:T(8,128)(2,1)S(1)}, bf16[32,2176]{1,0:T(8,128)(2,1)S(1)}, u32[]{:S(2)}, u32[]{:S(2)}) collective-permute-start(bf16[32,2176]{1,0:T(8,128)(2,1)S(1)} %collective-permute-done.1.refs_4_), channel_id=1, source_target_pairs={{0,1},{1,0},{2,3},{3,2},{4,5},{5,4},{6,7},{7,6},{8,9},{9,8},{10,11... | collective-permute-start | bytes 417800 | tf_op jit(solution)/shard_map/ppermute | solution.py:101
  49.8 2.0 %collective-permute-start.7 = (bf16[128,2048]{1,0:T(8,128)(2,1)S(1)}, bf16[128,2048]{1,0:T(8,128)(2,1)S(1)}, u32[]{:S(2)}, u32[]{:S(2)}) collective-permute-start(bf16[128,2048]{1,0:T(8,128)(2,1)S(1)} %get-tuple-element.14), channel_id=1, source_target_pairs={{0,1},{1,0},{2,3},{3,2},{4,5},{5,4},{6,7},{7,6},{8,9},{9,8},{10,11... | collective-permute-start | bytes 1572872 | tf_op jit(solution)/shard_map/ppermute | solution.py:101
  50.2 9.2 %collective-permute-start.19 = (bf16[64,2048]{1,0:T(8,128)(2,1)S(1)}, bf16[64,2048]{1,0:T(8,128)(2,1)S(1)}, u32[]{:S(2)}, u32[]{:S(2)}) collective-permute-start(bf16[64,2048]{1,0:T(8,128)(2,1)S(1)} %slice.59), channel_id=1, source_target_pairs={{0,2},{1,3},{2,0},{3,1},{4,6},{5,7},{6,4},{7,5},{8,10},{9,11},{10,... | collective-permute-start | bytes 786440 | tf_op jit(solution)/shard_map/ppermute | solution.py:101
  52.0 12.5 %collective-permute-start.8 = (bf16[64,2048]{1,0:T(8,128)(2,1)S(1)}, bf16[64,2048]{1,0:T(8,128)(2,1)S(1)}, u32[]{:S(2)}, u32[]{:S(2)}) collective-permute-start(bf16[64,2048]{1,0:T(8,128)(2,1)S(1)} %slice.60), channel_id=1, source_target_pairs={{0,2},{1,3},{2,0},{3,1},{4,6},{5,7},{6,4},{7,5},{8,10},{9,11},{10,... | collective-permute-start | bytes 786440 | tf_op jit(solution)/shard_map/ppermute | solution.py:101
  59.6 6.6 %collective-permute-start.20 = (bf16[32,2048]{1,0:T(8,128)(2,1)S(1)}, bf16[32,2048]{1,0:T(8,128)(2,1)S(1)}, u32[]{:S(2)}, u32[]{:S(2)}) collective-permute-start(bf16[32,2048]{1,0:T(8,128)(2,1)S(1)} %get-tuple-element.17), channel_id=1, source_target_pairs={{0,12},{1,13},{2,14},{3,15},{4,0},{5,1},{6,2},{7,3},{8,4},{9,5},{1... | collective-permute-start | bytes 393224 | tf_op jit(solution)/shard_map/ppermute | solution.py:101
  62.0 6.9 %collective-permute-start.21 = (bf16[32,2048]{1,0:T(8,128)(2,1)S(1)}, bf16[32,2048]{1,0:T(8,128)(2,1)S(1)}, u32[]{:S(2)}, u32[]{:S(2)}) collective-permute-start(bf16[32,2048]{1,0:T(8,128)(2,1)S(1)} %get-tuple-element.18), channel_id=1, source_target_pairs={{0,4},{1,5},{2,6},{3,7},{4,8},{5,9},{6,10},{7,11},{8,12},{9,13},{1... | collective-permute-start | bytes 393224 | tf_op jit(solution)/shard_map/ppermute | solution.py:101
  64.6 9.8 %collective-permute-start.9 = (bf16[32,2048]{1,0:T(8,128)(2,1)S(1)}, bf16[32,2048]{1,0:T(8,128)(2,1)S(1)}, u32[]{:S(2)}, u32[]{:S(2)}) collective-permute-start(bf16[32,2048]{1,0:T(8,128)(2,1)S(1)} %slice.61), channel_id=1, source_target_pairs={{0,8},{1,9},{2,10},{3,11},{4,12},{5,13},{6,14},{7,15},{8,0},{9,1},... | collective-permute-start | bytes 393224 | tf_op jit(solution)/shard_map/ppermute | solution.py:101

commit v3 on v2

--- a/solution.py
+++ b/solution.py
@@ -7,6 +7,7 @@
 from jax.experimental import pallas as pl
 from jax.experimental.pallas import tpu as pltpu
 from jax.sharding import PartitionSpec as P
+
 
 QUERY_HEADS = 16
 KEY_VALUE_HEADS = 2
@@ -108,15 +109,12 @@
 def gathered(x):
     zs, ys, cs = grid_of(lax.axis_size("ep"))
     pieces = {(0, 0, 0): x}
-    for dy in range(1, ys):
-        pieces[0, dy, 0] = send(x, 0, dy, 0)
     for dz in far_first(zs):
         if dz:
             pieces[dz, 0, 0] = send(x, dz, 0, 0)
-    for dz in far_first(zs):
+    for dz in range(zs):
         for dy in range(1, ys):
-            if dz:
-                pieces[dz, dy, 0] = send(pieces[dz, 0, 0], 0, dy, 0)
+            pieces[dz, dy, 0] = send(pieces[dz, 0, 0], 0, dy, 0)
     for dz, dy, _ in list(pieces):
         for dc in range(1, cs):
             pieces[dz, dy, dc] = send(pieces[dz, dy, 0], 0, 0, dc)
@@ -128,7 +126,9 @@
 
 
 def attention_body(
-    lengths, hidden, queries, keys, values, gain, ids, gates, payload, resid, parts, *, experts
+    lengths_in, hidden_in, queries_in, keys_in, values_in, gain_in, ids_in, gates_in,
+    payload, resid,
+    lengths, hidden, queries, keys, values, gain, ids, gates, parts, sems, *, experts,
 ):
     rows, width = hidden.shape
     _, slots, kv_width = keys.shape
@@ -136,83 +136,111 @@
     kv_heads = kv_width // head
     heads = width // head
     group = heads // kv_heads
-    step = pl.program_id(0)
+    block = MB_ROWS
     pair = LANES // slots
     scale = 1.0 / math.sqrt(head)
     f32 = jnp.float32
 
-    blocks = []
-    for g in range(kv_heads):
-        own = jnp.concatenate(
-            [queries[:, h * head : (h + 1) * head] for h in range(g * group, (g + 1) * group)],
-            axis=0,
-        )
-        blank = jnp.zeros_like(own)
-        blocks.append(
-            jnp.concatenate([own if i == g else blank for i in range(kv_heads)], axis=1)
-        )
-    stacked = jnp.concatenate(blocks, axis=0)
-    flat_keys = keys[...].reshape(rows * slots, kv_width)
-    flat_values = values[...].reshape(rows * slots, kv_width)
-    scores = lax.dot_general(
-        stacked, flat_keys, (((1,), (1,)), ((), ())), preferred_element_type=f32
-    )
-
-    request = lax.broadcasted_iota(jnp.int32, (rows, LANES), 0)
-    lane = lax.broadcasted_iota(jnp.int32, (rows, LANES), 1)
-    length = jnp.zeros((rows, LANES), jnp.int32)
-    for t in range(rows):
-        length = jnp.where(request == t, lengths[step * rows + t], length)
-    seen = (lane // slots == request % pair) & (lane % slots < length)
-    seen = jnp.concatenate([seen.astype(jnp.int32)] * heads, axis=0) != 0
-    slab = jnp.concatenate([request // pair] * heads, axis=0)
-    compact = scores[:, :LANES]
-    for j in range(1, rows // pair):
-        compact = jnp.where(slab == j, scores[:, j * LANES : (j + 1) * LANES], compact)
-    compact = jnp.where(seen, compact * scale, -1e30)
-    top = jnp.max(compact, axis=-1, keepdims=True)
-    expo = jnp.where(seen, jnp.exp(compact - top), 0.0)
-    probs = (expo / jnp.sum(expo, axis=-1, keepdims=True)).astype(jnp.bfloat16)
-    probs = probs.astype(f32)
-    wide = jnp.concatenate(
-        [jnp.where(slab == j, probs, 0.0).astype(jnp.bfloat16) for j in range(rows // pair)],
-        axis=1,
-    )
-    attended = jnp.dot(wide, flat_values, preferred_element_type=f32)
-
-    square = jnp.zeros((rows, LANES), f32)
-    for h in range(heads):
-        g = h // group
-        cols = slice(h * head, (h + 1) * head)
-        total = hidden[:, cols].astype(f32)
-        total = total + attended[h * rows : (h + 1) * rows, g * head : (g + 1) * head]
-        resid[:, cols] = total
-        square = square + total * total
-    mean_square = jnp.sum(square, axis=-1, keepdims=True) / width
-    inverse = lax.rsqrt(mean_square + 1e-06)
-    for h in range(heads):
-        cols = slice(h * head, (h + 1) * head)
-        payload[:, cols] = (resid[:, cols] * inverse * gain[:, cols]).astype(jnp.bfloat16)
-
-    all_rows = ids.shape[1]
-    top_count = ids.shape[0]
-    number = lax.broadcasted_iota(jnp.int32, (experts, all_rows), 0)
-    table = jnp.zeros((experts, all_rows), f32)
-    for k in range(top_count):
+    copies = {}
+
+    def fetch(name, source, target):
+        copies[name] = pltpu.make_async_copy(source, target, sems.at[len(copies)])
+        copies[name].start()
+
+    fetch("queries", queries_in, queries)
+    for b in range(rows // block):
+        at = pl.ds(b * block, block)
+        fetch(("keys", b), keys_in.at[at], keys.at[at])
+        if b == 0:
+            fetch("lengths", lengths_in, lengths)
+            fetch("ids", ids_in, ids)
+            fetch("gates", gates_in, gates)
+        fetch(("values", b), values_in.at[at], values.at[at])
+        if b == 0:
+            fetch("hidden", hidden_in, hidden)
+            fetch("gain", gain_in, gain)
+
+    copies["ids"].wait()
+    copies["gates"].wait()
+    number = lax.broadcasted_iota(jnp.int32, (experts, rows), 0)
+    table = jnp.zeros((experts, rows), f32)
+    for k in range(ids.shape[0]):
         table = table + jnp.where(ids[k : k + 1, :] == number, gates[k : k + 1, :], 0.0)
     high = table.astype(jnp.bfloat16).astype(f32)
     middle = (table - high).astype(jnp.bfloat16).astype(f32)
     low = table - high - middle
     parts[...] = jnp.zeros_like(parts)
     for i, part in enumerate((high, middle, low)):
-        parts[i * experts : (i + 1) * experts, :all_rows] = part
-    flipped = parts[...].T.astype(jnp.bfloat16)
-
-    for i in range(all_rows // rows):
-
-        @pl.when(step == i)
-        def _():
-            payload[:, width:] = flipped[i * rows : (i + 1) * rows, :]
+        parts[i * experts : (i + 1) * experts, :rows] = part
+    payload[:, width:] = parts[...].T[:rows].astype(jnp.bfloat16)
+
+    copies["lengths"].wait()
+    copies["queries"].wait()
+    request = lax.broadcasted_iota(jnp.int32, (block, LANES), 0)
+    lane = lax.broadcasted_iota(jnp.int32, (block, LANES), 1)
+    slab = jnp.concatenate([request // pair] * heads, axis=0)
+    for b in range(rows // block):
+        at = slice(b * block, (b + 1) * block)
+        blocks = []
+        for g in range(kv_heads):
+            own = jnp.concatenate(
+                [
+                    queries[at, h * head : (h + 1) * head]
+                    for h in range(g * group, (g + 1) * group)
+                ],
+                axis=0,
+            )
+            blank = jnp.zeros_like(own)
+            blocks.append(
+                jnp.concatenate([own if i == g else blank for i in range(kv_heads)], axis=1)
+            )
+        stacked = jnp.concatenate(blocks, axis=0)
+        copies["keys", b].wait()
+        scores = lax.dot_general(
+            stacked,
+            keys[at].reshape(block * slots, kv_width),
+            (((1,), (1,)), ((), ())),
+            preferred_element_type=f32,
+        )
+
+        length = jnp.zeros((block, LANES), jnp.int32)
+        for t in range(block):
+            length = jnp.where(request == t, lengths[b * block + t], length)
+        seen = (lane // slots == request % pair) & (lane % slots < length)
+        seen = jnp.concatenate([seen.astype(jnp.int32)] * heads, axis=0) != 0
+        compact = scores[:, :LANES]
+        for j in range(1, block // pair):
+            compact = jnp.where(slab == j, scores[:, j * LANES : (j + 1) * LANES], compact)
+        compact = jnp.where(seen, compact * scale, -1e30)
+        top = jnp.max(compact, axis=-1, keepdims=True)
+        expo = jnp.where(seen, jnp.exp(compact - top), 0.0)
+        probs = (expo / jnp.sum(expo, axis=-1, keepdims=True)).astype(jnp.bfloat16)
+        probs = probs.astype(f32)
+        wide = jnp.concatenate(
+            [jnp.where(slab == j, probs, 0.0).astype(jnp.bfloat16) for j in range(block // pair)],
+            axis=1,
+        )
+        copies["values", b].wait()
+        attended = jnp.dot(
+            wide, values[at].reshape(block * slots, kv_width), preferred_element_type=f32
+        )
+
+        if b == 0:
+            copies["hidden"].wait()
+            copies["gain"].wait()
+        square = jnp.zeros((block, LANES), f32)
+        for h in range(heads):
+            g = h // group
+            cols = slice(h * head, (h + 1) * head)
+            total = hidden[at, cols].astype(f32)
+            total = total + attended[h * block : (h + 1) * block, g * head : (g + 1) * head]
+            resid[at, cols] = total
+            square = square + total * total
+        mean_square = jnp.sum(square, axis=-1, keepdims=True) / width
+        inverse = lax.rsqrt(mean_square + 1e-06)
+        for h in range(heads):
+            cols = slice(h * head, (h + 1) * head)
+            payload[at, cols] = (resid[at, cols] * inverse * gain[:, cols]).astype(jnp.bfloat16)
 
 
 def attention(
@@ -220,43 +248,9 @@
     gate_weights, experts,
 ):
     rows, width = hidden_in.shape
-    _, slots, kv_width = stored_keys.shape
-    block = MB_ROWS
     whole = width + LANES
-
-    def row(columns):
-        return pl.BlockSpec((block, columns), lambda i, n: (i, 0))
-
-    def cache():
-        return pl.BlockSpec((block, slots, kv_width), lambda i, n: (i, 0, 0))
-
-    def full(shape):
-        return pl.BlockSpec(shape, lambda i, n: (0, 0))
-
-    return pl.pallas_call(
-        functools.partial(attention_body, experts=experts),
-        out_shape=(
-            jax.ShapeDtypeStruct((rows, whole), jnp.bfloat16),
-            jax.ShapeDtypeStruct((rows, width), jnp.float32),
-        ),
-        grid_spec=pltpu.PrefetchScalarGridSpec(
-            num_scalar_prefetch=1,
-            grid=(rows // block,),
-            in_specs=[
-                row(width),
-                row(width),
-                cache(),
-                cache(),
-                full((1, width)),
-                full((expert_ids.shape[1], rows)),
-                full((expert_ids.shape[1], rows)),
-            ],
-            out_specs=(row(whole), row(width)),
-            scratch_shapes=[pltpu.VMEM((LANES, LANES), jnp.float32)],
-        ),
-        compiler_params=pltpu.CompilerParams(vmem_limit_bytes=16 * MIB),
-        name="attention",
-    )(
+    vmem = pl.BlockSpec(memory_space=pltpu.VMEM)
+    operands = (
         stored_lengths,
         hidden_in,
         queries,
@@ -266,6 +260,53 @@
         expert_ids.T,
         gate_weights.T,
     )
+    return pl.pallas_call(
+        functools.partial(attention_body, experts=experts),
+        out_shape=(
+            jax.ShapeDtypeStruct((rows, whole), jnp.bfloat16),
+            jax.ShapeDtypeStruct((rows, width), jnp.float32),
+        ),
+        in_specs=[pl.BlockSpec(memory_space=pltpu.HBM)] * len(operands),
+        out_specs=(vmem, vmem),
+        scratch_shapes=[
+            pltpu.SMEM(operands[0].shape, operands[0].dtype),
+            *(pltpu.VMEM(x.shape, x.dtype) for x in operands[1:]),
+            pltpu.VMEM((LANES, LANES), jnp.float32),
+            pltpu.SemaphoreType.DMA((6 + 2 * (rows // MB_ROWS),)),
+        ],
+        compiler_params=pltpu.CompilerParams(vmem_limit_bytes=16 * MIB),
+        name="attention",
+    )(*(pltpu.with_memory_space_constraint(x, pltpu.HBM) for x in operands))
+
+
+def loader_body(*refs, count):
+    after, sources, targets, sems = refs[0], refs[1 : count + 1], refs[count + 1 : -1], refs[-1]
+    del after
+    copies = [
+        pltpu.make_async_copy(source, target, sems.at[i])
+        for i, (source, target) in enumerate(zip(sources, targets))
+    ]
+    for copy in copies:
+        copy.start()
+    for copy in copies:
+        copy.wait()
+
+
+def loaded(after, *arrays):
+    hbm = pl.BlockSpec(memory_space=pltpu.HBM)
+    vmem = pl.BlockSpec(memory_space=pltpu.VMEM)
+    return pl.pallas_call(
+        functools.partial(loader_body, count=len(arrays)),
+        out_shape=tuple(jax.ShapeDtypeStruct(x.shape, x.dtype) for x in arrays),
+        in_specs=[pl.BlockSpec(memory_space=pltpu.VMEM)] + [hbm] * len(arrays),
+        out_specs=(vmem,) * len(arrays),
+        scratch_shapes=[pltpu.SemaphoreType.DMA((len(arrays),))],
+        compiler_params=pltpu.CompilerParams(vmem_limit_bytes=16 * MIB),
+        cost_estimate=pl.CostEstimate(
+            flops=0, bytes_accessed=sum(2 * x.size for x in arrays), transcendentals=0
+        ),
+        name="loader",
+    )(after, *(pltpu.with_memory_space_constraint(x, pltpu.HBM) for x in arrays))
 
 
 TILE = 256
@@ -333,7 +374,7 @@
             pltpu.VMEM((count * rows, hidden), jnp.bfloat16),
             pltpu.VMEM((count * rows, LANES), jnp.float32),
         ],
-        compiler_params=pltpu.CompilerParams(vmem_limit_bytes=40 * MIB),
+        compiler_params=pltpu.CompilerParams(vmem_limit_bytes=16 * MIB),
         cost_estimate=pl.CostEstimate(
             flops=6 * count * rows * width * hidden * local_count,
             bytes_accessed=6 * width * hidden * local_count,
@@ -343,36 +384,36 @@
     )(*pieces, w_gate, w_up, w_down)
 
 
+def chunks_of(zs):
+    order = far_first(zs)
+    near = [dz for dz in order if dz in (0, zs // 2)]
+    return [chunk for chunk in (near, [dz for dz in order if dz not in near]) if chunk]
+
+
 def dense(payload, resid, w_gate, w_up, w_down):
     devices = lax.axis_size("ep")
-    local_count, width = w_gate.shape[:2]
+    local_count = w_gate.shape[0]
     experts = devices * local_count
-    zs, ys, cs = grid_of(devices)
+    zs, ys, _ = grid_of(devices)
     bf16, f32 = jnp.bfloat16, jnp.float32
     rows = payload.shape[0]
     pieces = gathered(payload)
-    order = far_first(zs)
-    near = [dz for dz in order if dz in (0, zs // 2)]
-    rest = [dz for dz in order if dz not in near]
+    weights = loaded(payload, w_gate, w_up, w_down)
     total = resid
-    for chunk in (near, rest):
-        if not chunk:
-            continue
+    for chunk in chunks_of(zs):
         dys = list(range(1, ys)) + [0]
-        names = [(dz, dy, dc) for dc in (1, 0) for dy in dys for dz in chunk]
-        away, kept = expert_rows(
-            [pieces[name] for name in names], w_gate, w_up, w_down, experts
-        )
+        names = [(dz, dy, dc) for dc in (1, 0) for dz in chunk for dy in dys]
+        away, kept = expert_rows([pieces[name] for name in names], *weights, experts)
         chip = kept + send(away, 0, 0, 1).astype(f32)
-        span = len(chunk) * rows
-        level = chip[(ys - 1) * span :]
-        for i, dy in enumerate(range(1, ys)):
-            level = level + send(
-                chip[i * span : (i + 1) * span].astype(bf16), 0, -dy, 0
-            ).astype(f32)
         for i, dz in enumerate(chunk):
-            part = level[i * rows : (i + 1) * rows]
-            total = total + (send(part.astype(bf16), -dz, 0, 0).astype(f32) if dz else part)
+            first = i * ys * rows
+            level = chip[first + (ys - 1) * rows : first + ys * rows]
+            for j, dy in enumerate(dys[:-1]):
+                part = chip[first + j * rows : first + (j + 1) * rows].astype(bf16)
+                level = level + send(part, 0, -dy, 0).astype(f32)
+            if dz:
+                level = send(level.astype(bf16), -dz, 0, 0).astype(f32)
+            total = total + level
     return total.astype(bf16)
 
 

time: 75.5 us -> 65 us (0.86)
  local copies, waits for them, and re-layouts: 12.7 us -> 0.04 us
  waiting for transfers between devices: 33.3 us -> 28.5 us
  Pallas kernels: 7.53 us -> 12.2 us
  starting transfers between devices: 20.3 us -> 22.9 us
    unnamed x24 -> x0, local copies, waits for them, and re-layouts: 12.6 us -> none
    ppermute x22 -> x24, waiting for transfers between devices: 33.3 us -> 28.5 us  [send(): return lax.ppermute(x, 'ep', shifted(lax.axis_size('ep'), dz, dy, dc))]
    pallas_call x0 -> x1, Pallas kernels: none -> 3.78 us  [loaded(): pl.pallas_call(functools.partial(loader_body, count=len(arrays)), out_sha...]
    ppermute x22 -> x24, starting transfers between devices: 20.3 us -> 22.9 us  [send(): return lax.ppermute(x, 'ep', shifted(lax.axis_size('ep'), dz, dy, dc))]
    pallas_call x1, Pallas kernels: 2.23 us -> 3.04 us  [attention(): pl.pallas_call(functools.partial(attention_body, experts=experts), out_sh...]
  transfers between devices with their start and end apart: 22 -> 24, of which waited for: 10 -> 11; matrix products, arithmetic and copies ran while one was open for 1% -> 1% of each run, Pallas kernels for 7% -> 14%
where the time goes in v3:
time: 65 us; the launch traced here: 64.8 us
  waiting for transfers between devices  28.5 us (44%)
  starting transfers between devices  22.9 us (35%)
  Pallas kernels  12.2 us (19%)
  other arithmetic  1.14 us (2%)
    ppermute x24, waiting for transfers between devices, send(): return lax.ppermute(x, 'ep', shifted(lax.axis_size('ep'), dz, dy, dc))  28.5 us
    ppermute x24, starting transfers between devices, send(): return lax.ppermute(x, 'ep', shifted(lax.axis_size('ep'), dz, dy, dc))  22.9 us
    pallas_call x2, Pallas kernels, expert_rows(): pl.pallas_call(functools.partial(expert_body, count=count, experts=expert...  5.37 us
    pallas_call x1, Pallas kernels, loaded(): pl.pallas_call(functools.partial(loader_body, count=len(arrays)), out_sha...  3.78 us
    pallas_call x1, Pallas kernels, attention(): pl.pallas_call(functools.partial(attention_body, experts=experts), out_sh...  3.04 us
  transfers between devices with their start and end apart: 24, of which 11 were waited for; matrix products, arithmetic and copies ran while one was open for 1% of the time, Pallas kernels for 14%

profile of v3, /device:TPU:0, one launch (start us, length us, event | category | flops | bytes accessed | tf_op | source)
XLA Modules:
  0.0 64.8 jit_solution(12092452780103661186)
XLA Ops:
  0.0 3.0 %attention.1 = (bf16[32,2176]{1,0:T(8,128)(2,1)S(1)}, f32[32,2048]{1,0:T(8,128)S(1)}) custom-call(s32[32]{0:T(128)} %lengths_in.1, bf16[32,2048]{1,0:T(8,128)(2,1)} %hidden_in.1, bf16[32,2048]{1,0:T(8,128)(2,1)} %queries_in.1, bf16[32,64,256]{2,1,0:T(8,128)(2,1)} %keys_in.1, bf16[32,64,256]{2,1,0:T(8,128)(2,1)} %values_in.1, f32[1,2048]{1,0:T(1,128)} %bitcast.3, ...), custom_call_target="tpu_custom_call" | custom-call | tf_op jit(solution)/shard_map/attention/pallas_call | solution.py:263
  3.0 4.1 %collective-permute-start = (bf16[32,2176]{1,0:T(8,128)(2,1)S(1)}, bf16[32,2176]{1,0:T(8,128)(2,1)S(1)}, u32[]{:S(2)}, u32[]{:S(2)}) collective-permute-start(bf16[32,2176]{1,0:T(8,128)(2,1)S(1)} %get-tuple-element.15.refs_0_.refs_7_), channel_id=1, source_target_pairs={{0,8},{1,9},{2,10},{3,11},{4,12},{5,13},{6,14},{7,15},{8,0},{9,1},... | collective-permute-start | bytes 417800 | tf_op jit(solution)/shard_map/ppermute | solution.py:102
  7.2 1.5 %collective-permute-start.4 = (bf16[32,2176]{1,0:T(8,128)(2,1)S(1)}, bf16[32,2176]{1,0:T(8,128)(2,1)S(1)}, u32[]{:S(2)}, u32[]{:S(2)}) collective-permute-start(bf16[32,2176]{1,0:T(8,128)(2,1)S(1)} %get-tuple-element.15.refs_0_.refs_7_), channel_id=1, source_target_pairs={{0,2},{1,3},{2,0},{3,1},{4,6},{5,7},{6,4},{7,5},{8,10},{9,11},{10,... | collective-permute-start | bytes 417800 | tf_op jit(solution)/shard_map/ppermute | solution.py:102
  8.7 5.1 %collective-permute-done.refs_5_ = bf16[32,2176]{1,0:T(8,128)(2,1)S(1)} collective-permute-done((bf16[32,2176]{1,0:T(8,128)(2,1)S(1)}, bf16[32,2176]{1,0:T(8,128)(2,1)S(1)}, u32[]{:S(2)}, u32[]{:S(2)}) %collective-permute-start) | collective-permute-done | bytes 139296 | tf_op jit(solution)/shard_map/ppermute | solution.py:102
  13.8 1.6 %collective-permute-start.1 = (bf16[32,2176]{1,0:T(8,128)(2,1)S(1)}, bf16[32,2176]{1,0:T(8,128)(2,1)S(1)}, u32[]{:S(2)}, u32[]{:S(2)}) collective-permute-start(bf16[32,2176]{1,0:T(8,128)(2,1)S(1)} %collective-permute-done.refs_5_), channel_id=1, source_target_pairs={{0,2},{1,3},{2,0},{3,1},{4,6},{5,7},{6,4},{7,5},{8,10},{9,11},{10,... | collective-permute-start | bytes 417800 | tf_op jit(solution)/shard_map/ppermute | solution.py:102
  15.4 0.0 collective-permute-start.6
  15.4 0.5 collective-permute-start.3
  15.9 0.0 collective-permute-done.4.refs_6_
  15.9 0.0 collective-permute-start.5
  15.9 3.0 %collective-permute-done.1.refs_4_ = bf16[32,2176]{1,0:T(8,128)(2,1)S(1)} collective-permute-done((bf16[32,2176]{1,0:T(8,128)(2,1)S(1)}, bf16[32,2176]{1,0:T(8,128)(2,1)S(1)}, u32[]{:S(2)}, u32[]{:S(2)}) %collective-permute-start.1) | collective-permute-done | bytes 139296 | tf_op jit(solution)/shard_map/ppermute | solution.py:102
  18.9 0.0 collective-permute-start.2
  18.9 1.3 %collective-permute-start.11 = (bf16[32,2176]{1,0:T(8,128)(2,1)S(1)}, bf16[32,2176]{1,0:T(8,128)(2,1)S(1)}, u32[]{:S(2)}, u32[]{:S(2)}) collective-permute-start(bf16[32,2176]{1,0:T(8,128)(2,1)S(1)} %get-tuple-element.15.refs_0_.refs_7_), channel_id=1, source_target_pairs={{0,4},{1,5},{2,6},{3,7},{4,8},{5,9},{6,10},{7,11},{8,12},{9,13},{1... | collective-permute-start | bytes 417800 | tf_op jit(solution)/shard_map/ppermute | solution.py:102
  20.2 3.8 %loader.1 = (bf16[1,2048,768]{2,1,0:T(8,128)(2,1)S(1)}, bf16[1,2048,768]{2,1,0:T(8,128)(2,1)S(1)}, bf16[1,768,2048]{2,1,0:T(8,128)(2,1)S(1)}) custom-call(bf16[32,2176]{1,0:T(8,128)(2,1)S(1)} %get-tuple-element.15.refs_0_.refs_7_, bf16[1,2048,768]{2,1,0:T(8,128)(2,1)} %refs_1_.1, bf16[1,2048,768]{2,1,0:T(8,128)(2,1)} %refs_2_.1, bf16[1,768,2048]{2,1,0:T(8,128)(2,1)} %refs_3_.1), custom_call_target="tpu_custom_call" | custom-call | bytes 9437184 | tf_op jit(solution)/shard_map/loader/pallas_call | solution.py:298
  23.9 0.0 collective-permute-done.6.refs_3_
  24.0 2.9 %collective-permute-start.15 = (bf16[32,2176]{1,0:T(8,128)(2,1)S(1)}, bf16[32,2176]{1,0:T(8,128)(2,1)S(1)}, u32[]{:S(2)}, u32[]{:S(2)}) collective-permute-start(bf16[32,2176]{1,0:T(8,128)(2,1)S(1)} %get-tuple-element.15.refs_0_.refs_7_), channel_id=1, source_target_pairs={{0,12},{1,13},{2,14},{3,15},{4,0},{5,1},{6,2},{7,3},{8,4},{9,5},{1... | collective-permute-start | bytes 417800 | tf_op jit(solution)/shard_map/ppermute | solution.py:102
  26.8 0.0 collective-permute-done.3.refs_1_
  26.8 0.0 collective-permute-done.5.refs_2_
  26.8 0.0 collective-permute-done.2.refs_0_
  26.8 2.7 %expert_rows.2 = (bf16[128,2048]{1,0:T(8,128)(2,1)S(1)}, f32[128,2048]{1,0:T(8,128)S(1)}) custom-call(bf16[32,2176]{1,0:T(8,128)(2,1)S(1)} %collective-permute-done.2.refs_0_, bf16[32,2176]{1,0:T(8,128)(2,1)S(1)} %collective-permute-done.3.refs_1_, bf16[32,2176]{1,0:T(8,128)(2,1)S(1)} %collective-permute-done.5.refs_2_, ...), custom_call_target="tpu_custom_call" | custom-call | flops 2415919104 | bytes 9437184 | tf_op jit(solution)/shard_map/expert_rows/pallas_call | solution.py:363
  29.5 0.3 collective-permute-start.7
  29.8 0.0 collective-permute-done.11.refs_5_
  29.8 1.5 %collective-permute-start.12 = (bf16[32,2176]{1,0:T(8,128)(2,1)S(1)}, bf16[32,2176]{1,0:T(8,128)(2,1)S(1)}, u32[]{:S(2)}, u32[]{:S(2)}) collective-permute-start(bf16[32,2176]{1,0:T(8,128)(2,1)S(1)} %collective-permute-done.11.refs_5_), channel_id=1, source_target_pairs={{0,2},{1,3},{2,0},{3,1},{4,6},{5,7},{6,4},{7,5},{8,10},{9,11},{10,... | collective-permute-start | bytes 417800 | tf_op jit(solution)/shard_map/ppermute | solution.py:102
  31.3 0.0 collective-permute-done.15.refs_7_
  31.3 0.6 collective-permute-start.16
  31.9 0.0 collective-permute-start.14
  32.0 0.5 collective-permute-start.18
  32.5 3.9 %collective-permute-done.12.refs_4_ = bf16[32,2176]{1,0:T(8,128)(2,1)S(1)} collective-permute-done((bf16[32,2176]{1,0:T(8,128)(2,1)S(1)}, bf16[32,2176]{1,0:T(8,128)(2,1)S(1)}, u32[]{:S(2)}, u32[]{:S(2)}) %collective-permute-start.12) | collective-permute-done | bytes 139296 | tf_op jit(solution)/shard_map/ppermute | solution.py:102
  36.4 0.0 collective-permute-start.13
  36.4 2.3 %collective-permute-done.16.refs_6_ = bf16[32,2176]{1,0:T(8,128)(2,1)S(1)} collective-permute-done((bf16[32,2176]{1,0:T(8,128)(2,1)S(1)}, bf16[32,2176]{1,0:T(8,128)(2,1)S(1)}, u32[]{:S(2)}, u32[]{:S(2)}) %collective-permute-start.16) | collective-permute-done | bytes 139296 | tf_op jit(solution)/shard_map/ppermute | solution.py:102
  38.7 0.0 collective-permute-start.17
  38.7 0.0 collective-permute-done.14.refs_1_
  38.7 0.0 collective-permute-done.18.refs_3_
  38.7 0.0 collective-permute-done.13.refs_0_
  38.7 1.3 %collective-permute-done.17.refs_2_ = bf16[32,2176]{1,0:T(8,128)(2,1)S(1)} collective-permute-done((bf16[32,2176]{1,0:T(8,128)(2,1)S(1)}, bf16[32,2176]{1,0:T(8,128)(2,1)S(1)}, u32[]{:S(2)}, u32[]{:S(2)}) %collective-permute-start.17) | collective-permute-done | bytes 139296 | tf_op jit(solution)/shard_map/ppermute | solution.py:102
  40.0 2.7 %expert_rows.3 = (bf16[128,2048]{1,0:T(8,128)(2,1)S(1)}, f32[128,2048]{1,0:T(8,128)S(1)}) custom-call(bf16[32,2176]{1,0:T(8,128)(2,1)S(1)} %collective-permute-done.13.refs_0_, bf16[32,2176]{1,0:T(8,128)(2,1)S(1)} %collective-permute-done.14.refs_1_, bf16[32,2176]{1,0:T(8,128)(2,1)S(1)} %collective-permute-done.17.refs_2_, ...), custom_call_target="tpu_custom_call" | custom-call | flops 2415919104 | bytes 9437184 | tf_op jit(solution)/shard_map/expert_rows/pallas_call | solution.py:363
  42.7 0.2 collective-permute-start.19
  42.9 0.0 collective-permute-done.7
  42.9 0.2 fusion.7
  43.1 1.6 %collective-permute-start.8 = (bf16[32,2048]{1,0:T(8,128)(2,1)S(1)}, bf16[32,2048]{1,0:T(8,128)(2,1)S(1)}, u32[]{:S(2)}, u32[]{:S(2)}) collective-permute-start(bf16[32,2048]{1,0:T(8,128)(2,1)S(1)} %get-tuple-element.29), channel_id=1, source_target_pairs={{0,2},{1,3},{2,0},{3,1},{4,6},{5,7},{6,4},{7,5},{8,10},{9,11},{10,... | collective-permute-start | bytes 393224 | tf_op jit(solution)/shard_map/ppermute | solution.py:102
  44.7 0.0 collective-permute-done.19
  44.7 0.1 fusion.8
  44.9 1.6 %collective-permute-start.20 = (bf16[32,2048]{1,0:T(8,128)(2,1)S(1)}, bf16[32,2048]{1,0:T(8,128)(2,1)S(1)}, u32[]{:S(2)}, u32[]{:S(2)}) collective-permute-start(bf16[32,2048]{1,0:T(8,128)(2,1)S(1)} %get-tuple-element.31), channel_id=1, source_target_pairs={{0,2},{1,3},{2,0},{3,1},{4,6},{5,7},{6,4},{7,5},{8,10},{9,11},{10,... | collective-permute-start | bytes 393224 | tf_op jit(solution)/shard_map/ppermute | solution.py:102
  46.5 0.5 collective-permute-start.22
  47.0 1.5 %collective-permute-start.10 = (bf16[32,2048]{1,0:T(8,128)(2,1)S(1)}, bf16[32,2048]{1,0:T(8,128)(2,1)S(1)}, u32[]{:S(2)}, u32[]{:S(2)}) collective-permute-start(bf16[32,2048]{1,0:T(8,128)(2,1)S(1)} %get-tuple-element.30), channel_id=1, source_target_pairs={{0,2},{1,3},{2,0},{3,1},{4,6},{5,7},{6,4},{7,5},{8,10},{9,11},{10,... | collective-permute-start | bytes 393224 | tf_op jit(solution)/shard_map/ppermute | solution.py:102
  48.5 1.1 %collective-permute-done.8 = bf16[32,2048]{1,0:T(8,128)(2,1)S(1)} collective-permute-done((bf16[32,2048]{1,0:T(8,128)(2,1)S(1)}, bf16[32,2048]{1,0:T(8,128)(2,1)S(1)}, u32[]{:S(2)}, u32[]{:S(2)}) %collective-permute-start.8) | collective-permute-done | bytes 131104 | tf_op jit(solution)/shard_map/ppermute | solution.py:102
  49.6 0.7 %collective-permute-start.9 = (bf16[32,2048]{1,0:T(8,128)(2,1)S(1)}, bf16[32,2048]{1,0:T(8,128)(2,1)S(1)}, u32[]{:S(2)}, u32[]{:S(2)}) collective-permute-start(bf16[32,2048]{1,0:T(8,128)(2,1)S(1)} %fusion.6), channel_id=1, source_target_pairs={{0,8},{1,9},{2,10},{3,11},{4,12},{5,13},{6,14},{7,15},{8,0},{9,1},... | collective-permute-start | bytes 393224 | tf_op jit(solution)/shard_map/ppermute | solution.py:102
  50.3 2.1 %collective-permute-done.20 = bf16[32,2048]{1,0:T(8,128)(2,1)S(1)} collective-permute-done((bf16[32,2048]{1,0:T(8,128)(2,1)S(1)}, bf16[32,2048]{1,0:T(8,128)(2,1)S(1)}, u32[]{:S(2)}, u32[]{:S(2)}) %collective-permute-start.20) | collective-permute-done | bytes 131104 | tf_op jit(solution)/shard_map/ppermute | solution.py:102
  52.4 2.8 %collective-permute-done.22 = bf16[32,2048]{1,0:T(8,128)(2,1)S(1)} collective-permute-done((bf16[32,2048]{1,0:T(8,128)(2,1)S(1)}, bf16[32,2048]{1,0:T(8,128)(2,1)S(1)}, u32[]{:S(2)}, u32[]{:S(2)}) %collective-permute-start.22) | collective-permute-done | bytes 131104 | tf_op jit(solution)/shard_map/ppermute | solution.py:102
  55.2 2.1 %collective-permute-start.21 = (bf16[32,2048]{1,0:T(8,128)(2,1)S(1)}, bf16[32,2048]{1,0:T(8,128)(2,1)S(1)}, u32[]{:S(2)}, u32[]{:S(2)}) collective-permute-start(bf16[32,2048]{1,0:T(8,128)(2,1)S(1)} %get-tuple-element.27), channel_id=1, source_target_pairs={{0,12},{1,13},{2,14},{3,15},{4,0},{5,1},{6,2},{7,3},{8,4},{9,5},{1... | collective-permute-start | bytes 393224 | tf_op jit(solution)/shard_map/ppermute | solution.py:102
  57.3 0.0 collective-permute-start.23
  57.3 0.1 collective-permute-done.10
  57.4 0.0 collective-permute-done.9
  57.4 3.1 %collective-permute-done.21 = bf16[32,2048]{1,0:T(8,128)(2,1)S(1)} collective-permute-done((bf16[32,2048]{1,0:T(8,128)(2,1)S(1)}, bf16[32,2048]{1,0:T(8,128)(2,1)S(1)}, u32[]{:S(2)}, u32[]{:S(2)}) %collective-permute-start.21) | collective-permute-done | bytes 131104 | tf_op jit(solution)/shard_map/ppermute | solution.py:102
  60.5 3.5 %collective-permute-done.23 = bf16[32,2048]{1,0:T(8,128)(2,1)S(1)} collective-permute-done((bf16[32,2048]{1,0:T(8,128)(2,1)S(1)}, bf16[32,2048]{1,0:T(8,128)(2,1)S(1)}, u32[]{:S(2)}, u32[]{:S(2)}) %collective-permute-start.23) | collective-permute-done | bytes 131104 | tf_op jit(solution)/shard_map/ppermute | solution.py:102
  64.1 0.8 %fusion.5 = bf16[32,2048]{1,0:T(8,128)(2,1)} fusion(f32[128,2048]{1,0:T(8,128)S(1)} %get-tuple-element.24, bf16[32,2048]{1,0:T(8,128)(2,1)S(1)} %collective-permute-done.23, bf16[32,2048]{1,0:T(8,128)(2,1)S(1)} %collective-permute-done.21, bf16[32,2048]{1,0:T(8,128)(2,1)S(1)} %collective-permute-done.10, f32[32,2048]{1,0:T(8,128)S(1)} %get-tuple-element.14, ...), kind=kLoop, calls=%fused_computation.10 | loop fusion | flops 655360 | bytes 1179648 | tf_op jit(solution)/shard_map/convert_element_type | solution.py:417
  (4 shorter events, 0.1 us)
Async XLA Ops:
  3.0 10.8 %collective-permute-start = (bf16[32,2176]{1,0:T(8,128)(2,1)S(1)}, bf16[32,2176]{1,0:T(8,128)(2,1)S(1)}, u32[]{:S(2)}, u32[]{:S(2)}) collective-permute-start(bf16[32,2176]{1,0:T(8,128)(2,1)S(1)} %get-tuple-element.15.refs_0_.refs_7_), channel_id=1, source_target_pairs={{0,8},{1,9},{2,10},{3,11},{4,12},{5,13},{6,14},{7,15},{8,0},{9,1},... | collective-permute-start | bytes 417800 | tf_op jit(solution)/shard_map/ppermute | solution.py:102
  7.2 8.7 %collective-permute-start.4 = (bf16[32,2176]{1,0:T(8,128)(2,1)S(1)}, bf16[32,2176]{1,0:T(8,128)(2,1)S(1)}, u32[]{:S(2)}, u32[]{:S(2)}) collective-permute-start(bf16[32,2176]{1,0:T(8,128)(2,1)S(1)} %get-tuple-element.15.refs_0_.refs_7_), channel_id=1, source_target_pairs={{0,2},{1,3},{2,0},{3,1},{4,6},{5,7},{6,4},{7,5},{8,10},{9,11},{10,... | collective-permute-start | bytes 417800 | tf_op jit(solution)/shard_map/ppermute | solution.py:102
  13.8 5.1 %collective-permute-start.1 = (bf16[32,2176]{1,0:T(8,128)(2,1)S(1)}, bf16[32,2176]{1,0:T(8,128)(2,1)S(1)}, u32[]{:S(2)}, u32[]{:S(2)}) collective-permute-start(bf16[32,2176]{1,0:T(8,128)(2,1)S(1)} %collective-permute-done.refs_5_), channel_id=1, source_target_pairs={{0,2},{1,3},{2,0},{3,1},{4,6},{5,7},{6,4},{7,5},{8,10},{9,11},{10,... | collective-permute-start | bytes 417800 | tf_op jit(solution)/shard_map/ppermute | solution.py:102
  15.4 8.5 %collective-permute-start.6 = (bf16[32,2176]{1,0:T(8,128)(2,1)S(1)}, bf16[32,2176]{1,0:T(8,128)(2,1)S(1)}, u32[]{:S(2)}, u32[]{:S(2)}) collective-permute-start(bf16[32,2176]{1,0:T(8,128)(2,1)S(1)} %get-tuple-element.15.refs_0_.refs_7_), channel_id=1, source_target_pairs={{0,1},{1,0},{2,3},{3,2},{4,5},{5,4},{6,7},{7,6},{8,9},{9,8},{10,11... | collective-permute-start | bytes 417800 | tf_op jit(solution)/shard_map/ppermute | solution.py:102
  15.4 11.4 %collective-permute-start.3 = (bf16[32,2176]{1,0:T(8,128)(2,1)S(1)}, bf16[32,2176]{1,0:T(8,128)(2,1)S(1)}, u32[]{:S(2)}, u32[]{:S(2)}) collective-permute-start(bf16[32,2176]{1,0:T(8,128)(2,1)S(1)} %collective-permute-done.refs_5_), channel_id=1, source_target_pairs={{0,1},{1,0},{2,3},{3,2},{4,5},{5,4},{6,7},{7,6},{8,9},{9,8},{10,11... | collective-permute-start | bytes 417800 | tf_op jit(solution)/shard_map/ppermute | solution.py:102
  15.9 10.9 %collective-permute-start.5 = (bf16[32,2176]{1,0:T(8,128)(2,1)S(1)}, bf16[32,2176]{1,0:T(8,128)(2,1)S(1)}, u32[]{:S(2)}, u32[]{:S(2)}) collective-permute-start(bf16[32,2176]{1,0:T(8,128)(2,1)S(1)} %collective-permute-done.4.refs_6_), channel_id=1, source_target_pairs={{0,1},{1,0},{2,3},{3,2},{4,5},{5,4},{6,7},{7,6},{8,9},{9,8},{10,11... | collective-permute-start | bytes 417800 | tf_op jit(solution)/shard_map/ppermute | solution.py:102
  18.9 7.9 %collective-permute-start.2 = (bf16[32,2176]{1,0:T(8,128)(2,1)S(1)}, bf16[32,2176]{1,0:T(8,128)(2,1)S(1)}, u32[]{:S(2)}, u32[]{:S(2)}) collective-permute-start(bf16[32,2176]{1,0:T(8,128)(2,1)S(1)} %collective-permute-done.1.refs_4_), channel_id=1, source_target_pairs={{0,1},{1,0},{2,3},{3,2},{4,5},{5,4},{6,7},{7,6},{8,9},{9,8},{10,11... | collective-permute-start | bytes 417800 | tf_op jit(solution)/shard_map/ppermute | solution.py:102
  18.9 10.9 %collective-permute-start.11 = (bf16[32,2176]{1,0:T(8,128)(2,1)S(1)}, bf16[32,2176]{1,0:T(8,128)(2,1)S(1)}, u32[]{:S(2)}, u32[]{:S(2)}) collective-permute-start(bf16[32,2176]{1,0:T(8,128)(2,1)S(1)} %get-tuple-element.15.refs_0_.refs_7_), channel_id=1, source_target_pairs={{0,4},{1,5},{2,6},{3,7},{4,8},{5,9},{6,10},{7,11},{8,12},{9,13},{1... | collective-permute-start | bytes 417800 | tf_op jit(solution)/shard_map/ppermute | solution.py:102
  24.0 7.4 %collective-permute-start.15 = (bf16[32,2176]{1,0:T(8,128)(2,1)S(1)}, bf16[32,2176]{1,0:T(8,128)(2,1)S(1)}, u32[]{:S(2)}, u32[]{:S(2)}) collective-permute-start(bf16[32,2176]{1,0:T(8,128)(2,1)S(1)} %get-tuple-element.15.refs_0_.refs_7_), channel_id=1, source_target_pairs={{0,12},{1,13},{2,14},{3,15},{4,0},{5,1},{6,2},{7,3},{8,4},{9,5},{1... | collective-permute-start | bytes 417800 | tf_op jit(solution)/shard_map/ppermute | solution.py:102
  29.5 13.4 %collective-permute-start.7 = (bf16[128,2048]{1,0:T(8,128)(2,1)S(1)}, bf16[128,2048]{1,0:T(8,128)(2,1)S(1)}, u32[]{:S(2)}, u32[]{:S(2)}) collective-permute-start(bf16[128,2048]{1,0:T(8,128)(2,1)S(1)} %get-tuple-element.20), channel_id=1, source_target_pairs={{0,1},{1,0},{2,3},{3,2},{4,5},{5,4},{6,7},{7,6},{8,9},{9,8},{10,11... | collective-permute-start | bytes 1572872 | tf_op jit(solution)/shard_map/ppermute | solution.py:102
  29.8 6.5 %collective-permute-start.12 = (bf16[32,2176]{1,0:T(8,128)(2,1)S(1)}, bf16[32,2176]{1,0:T(8,128)(2,1)S(1)}, u32[]{:S(2)}, u32[]{:S(2)}) collective-permute-start(bf16[32,2176]{1,0:T(8,128)(2,1)S(1)} %collective-permute-done.11.refs_5_), channel_id=1, source_target_pairs={{0,2},{1,3},{2,0},{3,1},{4,6},{5,7},{6,4},{7,5},{8,10},{9,11},{10,... | collective-permute-start | bytes 417800 | tf_op jit(solution)/shard_map/ppermute | solution.py:102
  31.3 7.3 %collective-permute-start.16 = (bf16[32,2176]{1,0:T(8,128)(2,1)S(1)}, bf16[32,2176]{1,0:T(8,128)(2,1)S(1)}, u32[]{:S(2)}, u32[]{:S(2)}) collective-permute-start(bf16[32,2176]{1,0:T(8,128)(2,1)S(1)} %collective-permute-done.15.refs_7_), channel_id=1, source_target_pairs={{0,2},{1,3},{2,0},{3,1},{4,6},{5,7},{6,4},{7,5},{8,10},{9,11},{10,... | collective-permute-start | bytes 417800 | tf_op jit(solution)/shard_map/ppermute | solution.py:102
  31.9 6.7 %collective-permute-start.14 = (bf16[32,2176]{1,0:T(8,128)(2,1)S(1)}, bf16[32,2176]{1,0:T(8,128)(2,1)S(1)}, u32[]{:S(2)}, u32[]{:S(2)}) collective-permute-start(bf16[32,2176]{1,0:T(8,128)(2,1)S(1)} %collective-permute-done.11.refs_5_), channel_id=1, source_target_pairs={{0,1},{1,0},{2,3},{3,2},{4,5},{5,4},{6,7},{7,6},{8,9},{9,8},{10,11... | collective-permute-start | bytes 417800 | tf_op jit(solution)/shard_map/ppermute | solution.py:102
  32.0 6.7 %collective-permute-start.18 = (bf16[32,2176]{1,0:T(8,128)(2,1)S(1)}, bf16[32,2176]{1,0:T(8,128)(2,1)S(1)}, u32[]{:S(2)}, u32[]{:S(2)}) collective-permute-start(bf16[32,2176]{1,0:T(8,128)(2,1)S(1)} %collective-permute-done.15.refs_7_), channel_id=1, source_target_pairs={{0,1},{1,0},{2,3},{3,2},{4,5},{5,4},{6,7},{7,6},{8,9},{9,8},{10,11... | collective-permute-start | bytes 417800 | tf_op jit(solution)/shard_map/ppermute | solution.py:102
  36.4 2.3 %collective-permute-start.13 = (bf16[32,2176]{1,0:T(8,128)(2,1)S(1)}, bf16[32,2176]{1,0:T(8,128)(2,1)S(1)}, u32[]{:S(2)}, u32[]{:S(2)}) collective-permute-start(bf16[32,2176]{1,0:T(8,128)(2,1)S(1)} %collective-permute-done.12.refs_4_), channel_id=1, source_target_pairs={{0,1},{1,0},{2,3},{3,2},{4,5},{5,4},{6,7},{7,6},{8,9},{9,8},{10,11... | collective-permute-start | bytes 417800 | tf_op jit(solution)/shard_map/ppermute | solution.py:102
  38.7 1.4 %collective-permute-start.17 = (bf16[32,2176]{1,0:T(8,128)(2,1)S(1)}, bf16[32,2176]{1,0:T(8,128)(2,1)S(1)}, u32[]{:S(2)}, u32[]{:S(2)}) collective-permute-start(bf16[32,2176]{1,0:T(8,128)(2,1)S(1)} %collective-permute-done.16.refs_6_), channel_id=1, source_target_pairs={{0,1},{1,0},{2,3},{3,2},{4,5},{5,4},{6,7},{7,6},{8,9},{9,8},{10,11... | collective-permute-start | bytes 417800 | tf_op jit(solution)/shard_map/ppermute | solution.py:102
  42.7 2.0 %collective-permute-start.19 = (bf16[128,2048]{1,0:T(8,128)(2,1)S(1)}, bf16[128,2048]{1,0:T(8,128)(2,1)S(1)}, u32[]{:S(2)}, u32[]{:S(2)}) collective-permute-start(bf16[128,2048]{1,0:T(8,128)(2,1)S(1)} %get-tuple-element.22), channel_id=1, source_target_pairs={{0,1},{1,0},{2,3},{3,2},{4,5},{5,4},{6,7},{7,6},{8,9},{9,8},{10,11... | collective-permute-start | bytes 1572872 | tf_op jit(solution)/shard_map/ppermute | solution.py:102
  43.1 6.4 %collective-permute-start.8 = (bf16[32,2048]{1,0:T(8,128)(2,1)S(1)}, bf16[32,2048]{1,0:T(8,128)(2,1)S(1)}, u32[]{:S(2)}, u32[]{:S(2)}) collective-permute-start(bf16[32,2048]{1,0:T(8,128)(2,1)S(1)} %get-tuple-element.29), channel_id=1, source_target_pairs={{0,2},{1,3},{2,0},{3,1},{4,6},{5,7},{6,4},{7,5},{8,10},{9,11},{10,... | collective-permute-start | bytes 393224 | tf_op jit(solution)/shard_map/ppermute | solution.py:102
  44.9 7.5 %collective-permute-start.20 = (bf16[32,2048]{1,0:T(8,128)(2,1)S(1)}, bf16[32,2048]{1,0:T(8,128)(2,1)S(1)}, u32[]{:S(2)}, u32[]{:S(2)}) collective-permute-start(bf16[32,2048]{1,0:T(8,128)(2,1)S(1)} %get-tuple-element.31), channel_id=1, source_target_pairs={{0,2},{1,3},{2,0},{3,1},{4,6},{5,7},{6,4},{7,5},{8,10},{9,11},{10,... | collective-permute-start | bytes 393224 | tf_op jit(solution)/shard_map/ppermute | solution.py:102
  46.5 8.7 %collective-permute-start.22 = (bf16[32,2048]{1,0:T(8,128)(2,1)S(1)}, bf16[32,2048]{1,0:T(8,128)(2,1)S(1)}, u32[]{:S(2)}, u32[]{:S(2)}) collective-permute-start(bf16[32,2048]{1,0:T(8,128)(2,1)S(1)} %get-tuple-element.32), channel_id=1, source_target_pairs={{0,2},{1,3},{2,0},{3,1},{4,6},{5,7},{6,4},{7,5},{8,10},{9,11},{10,... | collective-permute-start | bytes 393224 | tf_op jit(solution)/shard_map/ppermute | solution.py:102
  47.0 10.4 %collective-permute-start.10 = (bf16[32,2048]{1,0:T(8,128)(2,1)S(1)}, bf16[32,2048]{1,0:T(8,128)(2,1)S(1)}, u32[]{:S(2)}, u32[]{:S(2)}) collective-permute-start(bf16[32,2048]{1,0:T(8,128)(2,1)S(1)} %get-tuple-element.30), channel_id=1, source_target_pairs={{0,2},{1,3},{2,0},{3,1},{4,6},{5,7},{6,4},{7,5},{8,10},{9,11},{10,... | collective-permute-start | bytes 393224 | tf_op jit(solution)/shard_map/ppermute | solution.py:102
  49.6 7.8 %collective-permute-start.9 = (bf16[32,2048]{1,0:T(8,128)(2,1)S(1)}, bf16[32,2048]{1,0:T(8,128)(2,1)S(1)}, u32[]{:S(2)}, u32[]{:S(2)}) collective-permute-start(bf16[32,2048]{1,0:T(8,128)(2,1)S(1)} %fusion.6), channel_id=1, source_target_pairs={{0,8},{1,9},{2,10},{3,11},{4,12},{5,13},{6,14},{7,15},{8,0},{9,1},... | collective-permute-start | bytes 393224 | tf_op jit(solution)/shard_map/ppermute | solution.py:102
  55.2 5.3 %collective-permute-start.21 = (bf16[32,2048]{1,0:T(8,128)(2,1)S(1)}, bf16[32,2048]{1,0:T(8,128)(2,1)S(1)}, u32[]{:S(2)}, u32[]{:S(2)}) collective-permute-start(bf16[32,2048]{1,0:T(8,128)(2,1)S(1)} %get-tuple-element.27), channel_id=1, source_target_pairs={{0,12},{1,13},{2,14},{3,15},{4,0},{5,1},{6,2},{7,3},{8,4},{9,5},{1... | collective-permute-start | bytes 393224 | tf_op jit(solution)/shard_map/ppermute | solution.py:102
  57.3 6.8 %collective-permute-start.23 = (bf16[32,2048]{1,0:T(8,128)(2,1)S(1)}, bf16[32,2048]{1,0:T(8,128)(2,1)S(1)}, u32[]{:S(2)}, u32[]{:S(2)}) collective-permute-start(bf16[32,2048]{1,0:T(8,128)(2,1)S(1)} %get-tuple-element.28), channel_id=1, source_target_pairs={{0,4},{1,5},{2,6},{3,7},{4,8},{5,9},{6,10},{7,11},{8,12},{9,13},{1... | collective-permute-start | bytes 393224 | tf_op jit(solution)/shard_map/ppermute | solution.py:102

commit v4 on v3

--- a/solution.py
+++ b/solution.py
@@ -88,30 +88,23 @@
     return chips // minor, minor, cores
 
 
-def shifted(devices, dz, dy, dc):
-    zs, ys, cs = grid_of(devices)
-    pairs = []
-    for i in range(devices):
-        z, y, c = i // (ys * cs), i // cs % ys, i % cs
-        to = (((z + dz) % zs) * ys + (y + dy) % ys) * cs + (c + dc) % cs
-        pairs.append((i, to))
-    return pairs
+def dense_fits(devices):
+    zs, _, cs = grid_of(devices)
+    return devices & (devices - 1) == 0 and zs > 2 and cs == 2
 
 
 def send(x, dz, dy, dc):
-    return lax.ppermute(x, "ep", shifted(lax.axis_size("ep"), dz, dy, dc))
-
-
-def far_first(zs):
-    return sorted(range(zs), key=lambda d: (-min(d, zs - d), d))
+    devices = lax.axis_size("ep")
+    _, ys, cs = grid_of(devices)
+    mask = (dz * ys + dy) * cs + dc
+    return lax.ppermute(x, "ep", [(i, i ^ mask) for i in range(devices)])
 
 
 def gathered(x):
     zs, ys, cs = grid_of(lax.axis_size("ep"))
     pieces = {(0, 0, 0): x}
-    for dz in far_first(zs):
-        if dz:
-            pieces[dz, 0, 0] = send(x, dz, 0, 0)
+    for dz in range(1, zs):
+        pieces[dz, 0, 0] = send(x, dz, 0, 0)
     for dz in range(zs):
         for dy in range(1, ys):
             pieces[dz, dy, 0] = send(pieces[dz, 0, 0], 0, dy, 0)
@@ -127,7 +120,8 @@
 
 def attention_body(
     lengths_in, hidden_in, queries_in, keys_in, values_in, gain_in, ids_in, gates_in,
-    payload, resid,
+    w_gate_in,
+    payload, resid, w_gate,
     lengths, hidden, queries, keys, values, gain, ids, gates, parts, sems, *, experts,
 ):
     rows, width = hidden.shape
@@ -159,6 +153,7 @@
         if b == 0:
             fetch("hidden", hidden_in, hidden)
             fetch("gain", gain_in, gain)
+    fetch("w_gate", w_gate_in, w_gate)
 
     copies["ids"].wait()
     copies["gates"].wait()
@@ -241,11 +236,12 @@
         for h in range(heads):
             cols = slice(h * head, (h + 1) * head)
             payload[at, cols] = (resid[at, cols] * inverse * gain[:, cols]).astype(jnp.bfloat16)
+    copies["w_gate"].wait()
 
 
 def attention(
     hidden_in, queries, stored_keys, stored_values, stored_lengths, norm_gain, expert_ids,
-    gate_weights, experts,
+    gate_weights, w_gate, experts,
 ):
     rows, width = hidden_in.shape
     whole = width + LANES
@@ -259,54 +255,46 @@
         norm_gain[None, :],
         expert_ids.T,
         gate_weights.T,
+        w_gate,
     )
     return pl.pallas_call(
         functools.partial(attention_body, experts=experts),
         out_shape=(
             jax.ShapeDtypeStruct((rows, whole), jnp.bfloat16),
             jax.ShapeDtypeStruct((rows, width), jnp.float32),
+            jax.ShapeDtypeStruct(w_gate.shape, w_gate.dtype),
         ),
         in_specs=[pl.BlockSpec(memory_space=pltpu.HBM)] * len(operands),
-        out_specs=(vmem, vmem),
+        out_specs=(vmem,) * 3,
         scratch_shapes=[
             pltpu.SMEM(operands[0].shape, operands[0].dtype),
-            *(pltpu.VMEM(x.shape, x.dtype) for x in operands[1:]),
+            *(pltpu.VMEM(x.shape, x.dtype) for x in operands[1:-1]),
             pltpu.VMEM((LANES, LANES), jnp.float32),
-            pltpu.SemaphoreType.DMA((6 + 2 * (rows // MB_ROWS),)),
+            pltpu.SemaphoreType.DMA((7 + 2 * (rows // MB_ROWS),)),
         ],
         compiler_params=pltpu.CompilerParams(vmem_limit_bytes=16 * MIB),
         name="attention",
     )(*(pltpu.with_memory_space_constraint(x, pltpu.HBM) for x in operands))
 
 
-def loader_body(*refs, count):
-    after, sources, targets, sems = refs[0], refs[1 : count + 1], refs[count + 1 : -1], refs[-1]
+def loader_body(after, source, target, sem):
     del after
-    copies = [
-        pltpu.make_async_copy(source, target, sems.at[i])
-        for i, (source, target) in enumerate(zip(sources, targets))
-    ]
-    for copy in copies:
-        copy.start()
-    for copy in copies:
-        copy.wait()
-
-
-def loaded(after, *arrays):
-    hbm = pl.BlockSpec(memory_space=pltpu.HBM)
+    copy = pltpu.make_async_copy(source, target, sem)
+    copy.start()
+    copy.wait()
+
+
+def loaded(after, x):
     vmem = pl.BlockSpec(memory_space=pltpu.VMEM)
     return pl.pallas_call(
-        functools.partial(loader_body, count=len(arrays)),
-        out_shape=tuple(jax.ShapeDtypeStruct(x.shape, x.dtype) for x in arrays),
-        in_specs=[pl.BlockSpec(memory_space=pltpu.VMEM)] + [hbm] * len(arrays),
-        out_specs=(vmem,) * len(arrays),
-        scratch_shapes=[pltpu.SemaphoreType.DMA((len(arrays),))],
-        compiler_params=pltpu.CompilerParams(vmem_limit_bytes=16 * MIB),
-        cost_estimate=pl.CostEstimate(
-            flops=0, bytes_accessed=sum(2 * x.size for x in arrays), transcendentals=0
-        ),
+        loader_body,
+        out_shape=jax.ShapeDtypeStruct(x.shape, x.dtype),
+        in_specs=[vmem, pl.BlockSpec(memory_space=pltpu.HBM)],
+        out_specs=vmem,
+        scratch_shapes=[pltpu.SemaphoreType.DMA(())],
+        compiler_params=pltpu.CompilerParams(vmem_limit_bytes=4 * MIB),
         name="loader",
-    )(after, *(pltpu.with_memory_space_constraint(x, pltpu.HBM) for x in arrays))
+    )(after, pltpu.with_memory_space_constraint(x, pltpu.HBM))
 
 
 TILE = 256
@@ -384,10 +372,51 @@
     )(*pieces, w_gate, w_up, w_down)
 
 
+def chip_body(kept, arrived, *outs, dzs, ys):
+    rows = outs[0].shape[0]
+    for i in range(dzs):
+        for j in range(ys):
+            at = slice((i * ys + j) * rows, (i * ys + j + 1) * rows)
+            out = outs[i * ys + j]
+            out[...] = (kept[at] + arrived[at].astype(jnp.float32)).astype(out.dtype)
+
+
+def chip_sums(kept, arrived, dzs, ys):
+    rows, width = kept.shape[0] // (dzs * ys), kept.shape[1]
+    vmem = pl.BlockSpec(memory_space=pltpu.VMEM)
+    kinds = ([jnp.bfloat16] * (ys - 1) + [jnp.float32]) * dzs
+    return pl.pallas_call(
+        functools.partial(chip_body, dzs=dzs, ys=ys),
+        out_shape=tuple(jax.ShapeDtypeStruct((rows, width), kind) for kind in kinds),
+        in_specs=[vmem] * 2,
+        out_specs=(vmem,) * len(kinds),
+        compiler_params=pltpu.CompilerParams(vmem_limit_bytes=4 * MIB),
+        name="chip_sums",
+    )(kept, arrived)
+
+
+def level_body(own, *refs):
+    total = own[...]
+    for ref in refs[:-1]:
+        total = total + ref[...].astype(jnp.float32)
+    refs[-1][...] = total.astype(jnp.bfloat16)
+
+
+def level_sum(own, arrived):
+    vmem = pl.BlockSpec(memory_space=pltpu.VMEM)
+    return pl.pallas_call(
+        level_body,
+        out_shape=jax.ShapeDtypeStruct(own.shape, jnp.bfloat16),
+        in_specs=[vmem] * (1 + len(arrived)),
+        out_specs=vmem,
+        compiler_params=pltpu.CompilerParams(vmem_limit_bytes=4 * MIB),
+        name="level_sum",
+    )(own, *arrived)
+
+
 def chunks_of(zs):
-    order = far_first(zs)
-    near = [dz for dz in order if dz in (0, zs // 2)]
-    return [chunk for chunk in (near, [dz for dz in order if dz not in near]) if chunk]
+    order = [zs // 2] + [d for d in range(zs - 1, 0, -1) if d != zs // 2]
+    return [[order[0], 0], order[1:]]
 
 
 def dense(payload, resid, w_gate, w_up, w_down):
@@ -395,26 +424,29 @@
     local_count = w_gate.shape[0]
     experts = devices * local_count
     zs, ys, _ = grid_of(devices)
-    bf16, f32 = jnp.bfloat16, jnp.float32
-    rows = payload.shape[0]
+    f32 = jnp.float32
     pieces = gathered(payload)
-    weights = loaded(payload, w_gate, w_up, w_down)
+    w_down = loaded(payload, w_down)
+    w_up = loaded(payload, w_up)
     total = resid
     for chunk in chunks_of(zs):
         dys = list(range(1, ys)) + [0]
         names = [(dz, dy, dc) for dc in (1, 0) for dz in chunk for dy in dys]
-        away, kept = expert_rows([pieces[name] for name in names], *weights, experts)
-        chip = kept + send(away, 0, 0, 1).astype(f32)
+        away, kept = expert_rows([pieces[name] for name in names], w_gate, w_up, w_down, experts)
+        arrived = send(away, 0, 0, 1)
+        sums = chip_sums(kept, arrived, len(chunk), ys)
         for i, dz in enumerate(chunk):
-            first = i * ys * rows
-            level = chip[first + (ys - 1) * rows : first + ys * rows]
-            for j, dy in enumerate(dys[:-1]):
-                part = chip[first + j * rows : first + (j + 1) * rows].astype(bf16)
-                level = level + send(part, 0, -dy, 0).astype(f32)
+            level = sums[(i + 1) * ys - 1]
+            arrived = [send(sums[i * ys + j], 0, dy, 0) for j, dy in enumerate(dys[:-1])]
             if dz:
-                level = send(level.astype(bf16), -dz, 0, 0).astype(f32)
-            total = total + level
-    return total.astype(bf16)
+                level = level_sum(level, arrived)
+                arrived = [send(level, dz, 0, 0)]
+                total = total + arrived[0].astype(f32)
+            else:
+                total = total + level
+                for part in arrived:
+                    total = total + part.astype(f32)
+    return total.astype(jnp.bfloat16)
 
 
 def layer_rows(
@@ -433,10 +465,10 @@
 ):
     devices = lax.axis_size("ep")
     experts = devices * w_gate.shape[0]
-    if 2 * expert_ids.shape[1] >= experts and grid_of(devices)[2] == 2 and 3 * experts <= LANES:
-        payload, resid = attention(
+    if 2 * expert_ids.shape[1] >= experts and dense_fits(devices) and 3 * experts <= LANES:
+        payload, resid, w_gate = attention(
             hidden_in, queries, stored_keys, stored_values, stored_lengths, norm_gain,
-            expert_ids, gate_weights, experts,
+            expert_ids, gate_weights, w_gate, experts,
         )
         return dense(payload, resid, w_gate, w_up, w_down)
     attention_output = cached_attention(
@@ -496,4 +528,7 @@
         P("ep", None, None),
     )
     out_specs = P(("groups", "ep"), None)
-    return jax.shard_map(local, mesh=mesh, in_specs=in_specs, out_specs=out_specs, check_vma=False)
+    step = jax.shard_map(local, mesh=mesh, in_specs=in_specs, out_specs=out_specs, check_vma=False)
+    if not dense_fits(mesh.shape["ep"]):
+        return step
+    return step

time: 65 us -> 57.2 us (0.88)
  waiting for transfers between devices: 28.5 us -> 19.7 us
  starting transfers between devices: 22.9 us -> 24.1 us
    ppermute x24, waiting for transfers between devices: 28.5 us -> 19.7 us  [send(): return lax.ppermute(x, 'ep', [(i, i ^ mask) for i in range(devices)])]
    ppermute x24, starting transfers between devices: 22.9 us -> 24.1 us  [send(): return lax.ppermute(x, 'ep', [(i, i ^ mask) for i in range(devices)])]
    pallas_call x1 -> x7, Pallas kernels: 3.78 us -> 4.04 us  [the longest x2 3.8 us: loaded(): pl.pallas_call(loader_body, out_shape=jax.ShapeDtypeStruct(x.shape, x.dty...]
  transfers between devices with their start and end apart: 24 -> 24, of which waited for: 11 -> 9; matrix products, arithmetic and copies ran while one was open for 1% -> 0% of each run, Pallas kernels for 14% -> 16%
where the time goes in v4:
time: 57.2 us; the launch traced here: 57 us
  starting transfers between devices  24.1 us (42%)
  waiting for transfers between devices  19.7 us (34%)
  Pallas kernels  12.4 us (22%)
  other arithmetic  0.75 us (1%)
    ppermute x24, starting transfers between devices, send(): return lax.ppermute(x, 'ep', [(i, i ^ mask) for i in range(devices)])  24.1 us
    ppermute x24, waiting for transfers between devices, send(): return lax.ppermute(x, 'ep', [(i, i ^ mask) for i in range(devices)])  19.7 us
    pallas_call x2, Pallas kernels, expert_rows(): pl.pallas_call(functools.partial(expert_body, count=count, experts=expert...  5.36 us
    pallas_call x2, Pallas kernels, loaded(): pl.pallas_call(loader_body, out_shape=jax.ShapeDtypeStruct(x.shape, x.dty...  3.8 us
    pallas_call x1, Pallas kernels, attention(): pl.pallas_call(functools.partial(attention_body, experts=experts), out_sh...  3.05 us
  transfers between devices with their start and end apart: 24, of which 9 were waited for; matrix products, arithmetic and copies ran while one was open for 0% of the time, Pallas kernels for 16%

profile of v4, /device:TPU:0, one launch (start us, length us, event | category | flops | bytes accessed | tf_op | source)
XLA Modules:
  0.0 57.0 jit_solution(9220467671821406009)
XLA Ops:
  0.0 3.0 %attention.1 = (bf16[32,2176]{1,0:T(8,128)(2,1)S(1)}, f32[32,2048]{1,0:T(8,128)S(1)}, bf16[1,2048,768]{2,1,0:T(8,128)(2,1)S(1)}) custom-call(s32[32]{0:T(128)} %lengths_in.1, bf16[32,2048]{1,0:T(8,128)(2,1)} %hidden_in.1, bf16[32,2048]{1,0:T(8,128)(2,1)} %queries_in.1, bf16[32,64,256]{2,1,0:T(8,128)(2,1)} %keys_in.1, bf16[32,64,256]{2,1,0:T(8,128)(2,1)} %values_in.1, ...), custom_call_target="tpu_custom_call" | custom-call | tf_op jit(solution)/shard_map/attention/pallas_call | solution.py:260
  3.1 5.1 %collective-permute-start.11 = (bf16[32,2176]{1,0:T(8,128)(2,1)S(1)}, bf16[32,2176]{1,0:T(8,128)(2,1)S(1)}, u32[]{:S(2)}, u32[]{:S(2)}) collective-permute-start(bf16[32,2176]{1,0:T(8,128)(2,1)S(1)} %get-tuple-element.21.after.refs_7_), channel_id=1, source_target_pairs={{0,12},{1,13},{2,14},{3,15},{4,8},{5,9},{6,10},{7,11},{8,4},{9,5},... | collective-permute-start | bytes 417800 | tf_op jit(solution)/shard_map/ppermute | solution.py:100
  8.2 0.0 collective-permute-start.15
  8.2 0.6 %collective-permute-start = (bf16[32,2176]{1,0:T(8,128)(2,1)S(1)}, bf16[32,2176]{1,0:T(8,128)(2,1)S(1)}, u32[]{:S(2)}, u32[]{:S(2)}) collective-permute-start(bf16[32,2176]{1,0:T(8,128)(2,1)S(1)} %get-tuple-element.21.after.refs_7_), channel_id=1, source_target_pairs={{0,8},{1,9},{2,10},{3,11},{4,12},{5,13},{6,14},{7,15},{8,0},{9,1},... | collective-permute-start | bytes 417800 | tf_op jit(solution)/shard_map/ppermute | solution.py:100
  8.8 1.7 %collective-permute-start.4 = (bf16[32,2176]{1,0:T(8,128)(2,1)S(1)}, bf16[32,2176]{1,0:T(8,128)(2,1)S(1)}, u32[]{:S(2)}, u32[]{:S(2)}) collective-permute-start(bf16[32,2176]{1,0:T(8,128)(2,1)S(1)} %get-tuple-element.21.after.refs_7_), channel_id=1, source_target_pairs={{0,2},{1,3},{2,0},{3,1},{4,6},{5,7},{6,4},{7,5},{8,10},{9,11},{10,... | collective-permute-start | bytes 417800 | tf_op jit(solution)/shard_map/ppermute | solution.py:100
  10.5 2.3 %collective-permute-done.11.refs_5_ = bf16[32,2176]{1,0:T(8,128)(2,1)S(1)} collective-permute-done((bf16[32,2176]{1,0:T(8,128)(2,1)S(1)}, bf16[32,2176]{1,0:T(8,128)(2,1)S(1)}, u32[]{:S(2)}, u32[]{:S(2)}) %collective-permute-start.11) | collective-permute-done | bytes 139296 | tf_op jit(solution)/shard_map/ppermute | solution.py:100
  12.8 1.7 %collective-permute-start.12 = (bf16[32,2176]{1,0:T(8,128)(2,1)S(1)}, bf16[32,2176]{1,0:T(8,128)(2,1)S(1)}, u32[]{:S(2)}, u32[]{:S(2)}) collective-permute-start(bf16[32,2176]{1,0:T(8,128)(2,1)S(1)} %collective-permute-done.11.refs_5_), channel_id=1, source_target_pairs={{0,2},{1,3},{2,0},{3,1},{4,6},{5,7},{6,4},{7,5},{8,10},{9,11},{10,... | collective-permute-start | bytes 417800 | tf_op jit(solution)/shard_map/ppermute | solution.py:100
  14.5 1.5 %collective-permute-done.15.refs_7_ = bf16[32,2176]{1,0:T(8,128)(2,1)S(1)} collective-permute-done((bf16[32,2176]{1,0:T(8,128)(2,1)S(1)}, bf16[32,2176]{1,0:T(8,128)(2,1)S(1)}, u32[]{:S(2)}, u32[]{:S(2)}) %collective-permute-start.15) | collective-permute-done | bytes 139296 | tf_op jit(solution)/shard_map/ppermute | solution.py:100
  16.0 1.4 %collective-permute-start.16 = (bf16[32,2176]{1,0:T(8,128)(2,1)S(1)}, bf16[32,2176]{1,0:T(8,128)(2,1)S(1)}, u32[]{:S(2)}, u32[]{:S(2)}) collective-permute-start(bf16[32,2176]{1,0:T(8,128)(2,1)S(1)} %collective-permute-done.15.refs_7_), channel_id=1, source_target_pairs={{0,2},{1,3},{2,0},{3,1},{4,6},{5,7},{6,4},{7,5},{8,10},{9,11},{10,... | collective-permute-start | bytes 417800 | tf_op jit(solution)/shard_map/ppermute | solution.py:100
  17.4 0.0 collective-permute-start.14
  17.4 2.6 %collective-permute-done.refs_5_ = bf16[32,2176]{1,0:T(8,128)(2,1)S(1)} collective-permute-done((bf16[32,2176]{1,0:T(8,128)(2,1)S(1)}, bf16[32,2176]{1,0:T(8,128)(2,1)S(1)}, u32[]{:S(2)}, u32[]{:S(2)}) %collective-permute-start) | collective-permute-done | bytes 139296 | tf_op jit(solution)/shard_map/ppermute | solution.py:100
  20.0 0.0 collective-permute-start.18
  20.0 0.0 collective-permute-done.4.refs_6_
  20.0 1.5 %collective-permute-start.1 = (bf16[32,2176]{1,0:T(8,128)(2,1)S(1)}, bf16[32,2176]{1,0:T(8,128)(2,1)S(1)}, u32[]{:S(2)}, u32[]{:S(2)}) collective-permute-start(bf16[32,2176]{1,0:T(8,128)(2,1)S(1)} %collective-permute-done.refs_5_), channel_id=1, source_target_pairs={{0,2},{1,3},{2,0},{3,1},{4,6},{5,7},{6,4},{7,5},{8,10},{9,11},{10,... | collective-permute-start | bytes 417800 | tf_op jit(solution)/shard_map/ppermute | solution.py:100
  21.5 0.0 collective-permute-done.12.refs_4_
  21.5 0.2 collective-permute-start.13
  21.7 0.0 collective-permute-done.16.refs_6_
  21.7 0.3 collective-permute-start.17
  22.0 1.9 %loader.2.refs_9_ = bf16[1,2048,768]{2,1,0:T(8,128)(2,1)S(1)} custom-call(bf16[32,2176]{1,0:T(8,128)(2,1)S(1)} %get-tuple-element.21.after.refs_7_, bf16[1,2048,768]{2,1,0:T(8,128)(2,1)} %source.2), custom_call_target="tpu_custom_call" | custom-call | tf_op jit(solution)/shard_map/loader/pallas_call | solution.py:289
  23.9 1.9 %loader.3.refs_10_ = bf16[1,768,2048]{2,1,0:T(8,128)(2,1)S(1)} custom-call(bf16[32,2176]{1,0:T(8,128)(2,1)S(1)} %get-tuple-element.21.after.refs_7_, bf16[1,768,2048]{2,1,0:T(8,128)(2,1)} %source.3), custom_call_target="tpu_custom_call" | custom-call | tf_op jit(solution)/shard_map/loader/pallas_call | solution.py:289
  25.8 0.0 collective-permute-done.14.refs_1_
  25.8 0.3 collective-permute-start.6
  26.1 0.0 collective-permute-done.18.refs_3_
  26.1 0.3 collective-permute-start.3
  26.4 0.0 collective-permute-done.1.refs_4_
  26.4 0.2 collective-permute-start.5
  26.7 0.0 collective-permute-done.13.refs_0_
  26.7 0.3 collective-permute-start.2
  26.9 0.0 collective-permute-done.17.refs_2_
  26.9 2.7 %expert_rows.3 = (bf16[128,2048]{1,0:T(8,128)(2,1)S(1)}, f32[128,2048]{1,0:T(8,128)S(1)}) custom-call(bf16[32,2176]{1,0:T(8,128)(2,1)S(1)} %collective-permute-done.13.refs_0_, bf16[32,2176]{1,0:T(8,128)(2,1)S(1)} %collective-permute-done.14.refs_1_, bf16[32,2176]{1,0:T(8,128)(2,1)S(1)} %collective-permute-done.17.refs_2_, ...), custom_call_target="tpu_custom_call" | custom-call | flops 2415919104 | bytes 9437184 | tf_op jit(solution)/shard_map/expert_rows/pallas_call | solution.py:351
  29.6 0.3 collective-permute-start.19
  29.9 0.0 collective-permute-done.6.refs_3_
  29.9 0.0 collective-permute-done.3.refs_1_
  29.9 0.0 collective-permute-done.5.refs_2_
  29.9 0.0 collective-permute-done.2.refs_0_
  29.9 2.7 %expert_rows.2 = (bf16[128,2048]{1,0:T(8,128)(2,1)S(1)}, f32[128,2048]{1,0:T(8,128)S(1)}) custom-call(bf16[32,2176]{1,0:T(8,128)(2,1)S(1)} %collective-permute-done.2.refs_0_, bf16[32,2176]{1,0:T(8,128)(2,1)S(1)} %collective-permute-done.3.refs_1_, bf16[32,2176]{1,0:T(8,128)(2,1)S(1)} %collective-permute-done.5.refs_2_, ...), custom_call_target="tpu_custom_call" | custom-call | flops 2415919104 | bytes 9437184 | tf_op jit(solution)/shard_map/expert_rows/pallas_call | solution.py:351
  32.6 0.3 collective-permute-start.7
  33.0 0.0 collective-permute-done.19.arrived
  33.0 0.1 chip_sums.3
  33.1 1.2 %collective-permute-start.22 = (bf16[32,2048]{1,0:T(8,128)(2,1)S(1)}, bf16[32,2048]{1,0:T(8,128)(2,1)S(1)}, u32[]{:S(2)}, u32[]{:S(2)}) collective-permute-start(bf16[32,2048]{1,0:T(8,128)(2,1)S(1)} %get-tuple-element.34), channel_id=1, source_target_pairs={{0,2},{1,3},{2,0},{3,1},{4,6},{5,7},{6,4},{7,5},{8,10},{9,11},{10,... | collective-permute-start | bytes 393224 | tf_op jit(solution)/shard_map/ppermute | solution.py:100
  34.3 0.9 %collective-permute-start.20 = (bf16[32,2048]{1,0:T(8,128)(2,1)S(1)}, bf16[32,2048]{1,0:T(8,128)(2,1)S(1)}, u32[]{:S(2)}, u32[]{:S(2)}) collective-permute-start(bf16[32,2048]{1,0:T(8,128)(2,1)S(1)} %get-tuple-element.32), channel_id=1, source_target_pairs={{0,2},{1,3},{2,0},{3,1},{4,6},{5,7},{6,4},{7,5},{8,10},{9,11},{10,... | collective-permute-start | bytes 393224 | tf_op jit(solution)/shard_map/ppermute | solution.py:100
  35.2 0.0 collective-permute-done.7.arrived
  35.2 0.1 chip_sums.2
  35.3 1.2 %collective-permute-start.8 = (bf16[32,2048]{1,0:T(8,128)(2,1)S(1)}, bf16[32,2048]{1,0:T(8,128)(2,1)S(1)}, u32[]{:S(2)}, u32[]{:S(2)}) collective-permute-start(bf16[32,2048]{1,0:T(8,128)(2,1)S(1)} %get-tuple-element.26), channel_id=1, source_target_pairs={{0,2},{1,3},{2,0},{3,1},{4,6},{5,7},{6,4},{7,5},{8,10},{9,11},{10,... | collective-permute-start | bytes 393224 | tf_op jit(solution)/shard_map/ppermute | solution.py:100
  36.5 0.9 %collective-permute-start.10 = (bf16[32,2048]{1,0:T(8,128)(2,1)S(1)}, bf16[32,2048]{1,0:T(8,128)(2,1)S(1)}, u32[]{:S(2)}, u32[]{:S(2)}) collective-permute-start(bf16[32,2048]{1,0:T(8,128)(2,1)S(1)} %get-tuple-element.28), channel_id=1, source_target_pairs={{0,2},{1,3},{2,0},{3,1},{4,6},{5,7},{6,4},{7,5},{8,10},{9,11},{10,... | collective-permute-start | bytes 393224 | tf_op jit(solution)/shard_map/ppermute | solution.py:100
  37.3 2.2 %collective-permute-done.22.refs_0_ = bf16[32,2048]{1,0:T(8,128)(2,1)S(1)} collective-permute-done((bf16[32,2048]{1,0:T(8,128)(2,1)S(1)}, bf16[32,2048]{1,0:T(8,128)(2,1)S(1)}, u32[]{:S(2)}, u32[]{:S(2)}) %collective-permute-start.22) | collective-permute-done | bytes 131104 | tf_op jit(solution)/shard_map/ppermute | solution.py:100
  39.5 1.7 %collective-permute-start.23 = (bf16[32,2048]{1,0:T(8,128)(2,1)S(1)}, bf16[32,2048]{1,0:T(8,128)(2,1)S(1)}, u32[]{:S(2)}, u32[]{:S(2)}) collective-permute-start(bf16[32,2048]{1,0:T(8,128)(2,1)S(1)} %level_sum.5), channel_id=1, source_target_pairs={{0,4},{1,5},{2,6},{3,7},{4,0},{5,1},{6,2},{7,3},{8,12},{9,13},{10,... | collective-permute-start | bytes 393224 | tf_op jit(solution)/shard_map/ppermute | solution.py:100
  41.2 1.1 %collective-permute-done.20.refs_0_ = bf16[32,2048]{1,0:T(8,128)(2,1)S(1)} collective-permute-done((bf16[32,2048]{1,0:T(8,128)(2,1)S(1)}, bf16[32,2048]{1,0:T(8,128)(2,1)S(1)}, u32[]{:S(2)}, u32[]{:S(2)}) %collective-permute-start.20) | collective-permute-done | bytes 131104 | tf_op jit(solution)/shard_map/ppermute | solution.py:100
  42.3 2.5 %collective-permute-start.21 = (bf16[32,2048]{1,0:T(8,128)(2,1)S(1)}, bf16[32,2048]{1,0:T(8,128)(2,1)S(1)}, u32[]{:S(2)}, u32[]{:S(2)}) collective-permute-start(bf16[32,2048]{1,0:T(8,128)(2,1)S(1)} %level_sum.4), channel_id=1, source_target_pairs={{0,12},{1,13},{2,14},{3,15},{4,8},{5,9},{6,10},{7,11},{8,4},{9,5},... | collective-permute-start | bytes 393224 | tf_op jit(solution)/shard_map/ppermute | solution.py:100
  44.9 0.2 collective-permute-done.8.refs_0_
  45.2 1.4 %collective-permute-start.9 = (bf16[32,2048]{1,0:T(8,128)(2,1)S(1)}, bf16[32,2048]{1,0:T(8,128)(2,1)S(1)}, u32[]{:S(2)}, u32[]{:S(2)}) collective-permute-start(bf16[32,2048]{1,0:T(8,128)(2,1)S(1)} %level_sum.3), channel_id=1, source_target_pairs={{0,8},{1,9},{2,10},{3,11},{4,12},{5,13},{6,14},{7,15},{8,0},{9,1},... | collective-permute-start | bytes 393224 | tf_op jit(solution)/shard_map/ppermute | solution.py:100
  46.5 0.7 %collective-permute-done.10 = bf16[32,2048]{1,0:T(8,128)(2,1)S(1)} collective-permute-done((bf16[32,2048]{1,0:T(8,128)(2,1)S(1)}, bf16[32,2048]{1,0:T(8,128)(2,1)S(1)}, u32[]{:S(2)}, u32[]{:S(2)}) %collective-permute-start.10) | collective-permute-done | bytes 131104 | tf_op jit(solution)/shard_map/ppermute | solution.py:100
  47.2 0.0 collective-permute-done.23
  47.2 2.5 %collective-permute-done.21 = bf16[32,2048]{1,0:T(8,128)(2,1)S(1)} collective-permute-done((bf16[32,2048]{1,0:T(8,128)(2,1)S(1)}, bf16[32,2048]{1,0:T(8,128)(2,1)S(1)}, u32[]{:S(2)}, u32[]{:S(2)}) %collective-permute-start.21) | collective-permute-done | bytes 131104 | tf_op jit(solution)/shard_map/ppermute | solution.py:100
  49.7 6.6 %collective-permute-done.9 = bf16[32,2048]{1,0:T(8,128)(2,1)S(1)} collective-permute-done((bf16[32,2048]{1,0:T(8,128)(2,1)S(1)}, bf16[32,2048]{1,0:T(8,128)(2,1)S(1)}, u32[]{:S(2)}, u32[]{:S(2)}) %collective-permute-start.9) | collective-permute-done | bytes 131104 | tf_op jit(solution)/shard_map/ppermute | solution.py:100
  56.3 0.8 %add_convert_fusion = bf16[32,2048]{1,0:T(8,128)(2,1)} fusion(bf16[32,2048]{1,0:T(8,128)(2,1)S(1)} %collective-permute-done.23, bf16[32,2048]{1,0:T(8,128)(2,1)S(1)} %collective-permute-done.21, bf16[32,2048]{1,0:T(8,128)(2,1)S(1)} %collective-permute-done.10, f32[32,2048]{1,0:T(8,128)S(1)} %get-tuple-element.27, f32[32,2048]{1,0:T(8,128)S(1)} %get-tuple-element.20, ...), kind=kLoop, calls=%fused_computation | loop fusion | flops 655360 | bytes 1179648 | tf_op jit(solution)/shard_map/convert_element_type | solution.py:449
  (3 shorter events, 0.1 us)
Async XLA Ops:
  3.1 9.7 %collective-permute-start.11 = (bf16[32,2176]{1,0:T(8,128)(2,1)S(1)}, bf16[32,2176]{1,0:T(8,128)(2,1)S(1)}, u32[]{:S(2)}, u32[]{:S(2)}) collective-permute-start(bf16[32,2176]{1,0:T(8,128)(2,1)S(1)} %get-tuple-element.21.after.refs_7_), channel_id=1, source_target_pairs={{0,12},{1,13},{2,14},{3,15},{4,8},{5,9},{6,10},{7,11},{8,4},{9,5},... | collective-permute-start | bytes 417800 | tf_op jit(solution)/shard_map/ppermute | solution.py:100
  8.2 7.8 %collective-permute-start.15 = (bf16[32,2176]{1,0:T(8,128)(2,1)S(1)}, bf16[32,2176]{1,0:T(8,128)(2,1)S(1)}, u32[]{:S(2)}, u32[]{:S(2)}) collective-permute-start(bf16[32,2176]{1,0:T(8,128)(2,1)S(1)} %get-tuple-element.21.after.refs_7_), channel_id=1, source_target_pairs={{0,4},{1,5},{2,6},{3,7},{4,0},{5,1},{6,2},{7,3},{8,12},{9,13},{10,... | collective-permute-start | bytes 417800 | tf_op jit(solution)/shard_map/ppermute | solution.py:100
  8.2 11.8 %collective-permute-start = (bf16[32,2176]{1,0:T(8,128)(2,1)S(1)}, bf16[32,2176]{1,0:T(8,128)(2,1)S(1)}, u32[]{:S(2)}, u32[]{:S(2)}) collective-permute-start(bf16[32,2176]{1,0:T(8,128)(2,1)S(1)} %get-tuple-element.21.after.refs_7_), channel_id=1, source_target_pairs={{0,8},{1,9},{2,10},{3,11},{4,12},{5,13},{6,14},{7,15},{8,0},{9,1},... | collective-permute-start | bytes 417800 | tf_op jit(solution)/shard_map/ppermute | solution.py:100
  8.8 11.1 %collective-permute-start.4 = (bf16[32,2176]{1,0:T(8,128)(2,1)S(1)}, bf16[32,2176]{1,0:T(8,128)(2,1)S(1)}, u32[]{:S(2)}, u32[]{:S(2)}) collective-permute-start(bf16[32,2176]{1,0:T(8,128)(2,1)S(1)} %get-tuple-element.21.after.refs_7_), channel_id=1, source_target_pairs={{0,2},{1,3},{2,0},{3,1},{4,6},{5,7},{6,4},{7,5},{8,10},{9,11},{10,... | collective-permute-start | bytes 417800 | tf_op jit(solution)/shard_map/ppermute | solution.py:100
  12.8 8.7 %collective-permute-start.12 = (bf16[32,2176]{1,0:T(8,128)(2,1)S(1)}, bf16[32,2176]{1,0:T(8,128)(2,1)S(1)}, u32[]{:S(2)}, u32[]{:S(2)}) collective-permute-start(bf16[32,2176]{1,0:T(8,128)(2,1)S(1)} %collective-permute-done.11.refs_5_), channel_id=1, source_target_pairs={{0,2},{1,3},{2,0},{3,1},{4,6},{5,7},{6,4},{7,5},{8,10},{9,11},{10,... | collective-permute-start | bytes 417800 | tf_op jit(solution)/shard_map/ppermute | solution.py:100
  16.0 5.8 %collective-permute-start.16 = (bf16[32,2176]{1,0:T(8,128)(2,1)S(1)}, bf16[32,2176]{1,0:T(8,128)(2,1)S(1)}, u32[]{:S(2)}, u32[]{:S(2)}) collective-permute-start(bf16[32,2176]{1,0:T(8,128)(2,1)S(1)} %collective-permute-done.15.refs_7_), channel_id=1, source_target_pairs={{0,2},{1,3},{2,0},{3,1},{4,6},{5,7},{6,4},{7,5},{8,10},{9,11},{10,... | collective-permute-start | bytes 417800 | tf_op jit(solution)/shard_map/ppermute | solution.py:100
  17.4 8.4 %collective-permute-start.14 = (bf16[32,2176]{1,0:T(8,128)(2,1)S(1)}, bf16[32,2176]{1,0:T(8,128)(2,1)S(1)}, u32[]{:S(2)}, u32[]{:S(2)}) collective-permute-start(bf16[32,2176]{1,0:T(8,128)(2,1)S(1)} %collective-permute-done.11.refs_5_), channel_id=1, source_target_pairs={{0,1},{1,0},{2,3},{3,2},{4,5},{5,4},{6,7},{7,6},{8,9},{9,8},{10,11... | collective-permute-start | bytes 417800 | tf_op jit(solution)/shard_map/ppermute | solution.py:100
  20.0 6.2 %collective-permute-start.18 = (bf16[32,2176]{1,0:T(8,128)(2,1)S(1)}, bf16[32,2176]{1,0:T(8,128)(2,1)S(1)}, u32[]{:S(2)}, u32[]{:S(2)}) collective-permute-start(bf16[32,2176]{1,0:T(8,128)(2,1)S(1)} %collective-permute-done.15.refs_7_), channel_id=1, source_target_pairs={{0,1},{1,0},{2,3},{3,2},{4,5},{5,4},{6,7},{7,6},{8,9},{9,8},{10,11... | collective-permute-start | bytes 417800 | tf_op jit(solution)/shard_map/ppermute | solution.py:100
  20.0 6.4 %collective-permute-start.1 = (bf16[32,2176]{1,0:T(8,128)(2,1)S(1)}, bf16[32,2176]{1,0:T(8,128)(2,1)S(1)}, u32[]{:S(2)}, u32[]{:S(2)}) collective-permute-start(bf16[32,2176]{1,0:T(8,128)(2,1)S(1)} %collective-permute-done.refs_5_), channel_id=1, source_target_pairs={{0,2},{1,3},{2,0},{3,1},{4,6},{5,7},{6,4},{7,5},{8,10},{9,11},{10,... | collective-permute-start | bytes 417800 | tf_op jit(solution)/shard_map/ppermute | solution.py:100
  21.5 5.2 %collective-permute-start.13 = (bf16[32,2176]{1,0:T(8,128)(2,1)S(1)}, bf16[32,2176]{1,0:T(8,128)(2,1)S(1)}, u32[]{:S(2)}, u32[]{:S(2)}) collective-permute-start(bf16[32,2176]{1,0:T(8,128)(2,1)S(1)} %collective-permute-done.12.refs_4_), channel_id=1, source_target_pairs={{0,1},{1,0},{2,3},{3,2},{4,5},{5,4},{6,7},{7,6},{8,9},{9,8},{10,11... | collective-permute-start | bytes 417800 | tf_op jit(solution)/shard_map/ppermute | solution.py:100
  21.7 5.2 %collective-permute-start.17 = (bf16[32,2176]{1,0:T(8,128)(2,1)S(1)}, bf16[32,2176]{1,0:T(8,128)(2,1)S(1)}, u32[]{:S(2)}, u32[]{:S(2)}) collective-permute-start(bf16[32,2176]{1,0:T(8,128)(2,1)S(1)} %collective-permute-done.16.refs_6_), channel_id=1, source_target_pairs={{0,1},{1,0},{2,3},{3,2},{4,5},{5,4},{6,7},{7,6},{8,9},{9,8},{10,11... | collective-permute-start | bytes 417800 | tf_op jit(solution)/shard_map/ppermute | solution.py:100
  25.8 4.1 %collective-permute-start.6 = (bf16[32,2176]{1,0:T(8,128)(2,1)S(1)}, bf16[32,2176]{1,0:T(8,128)(2,1)S(1)}, u32[]{:S(2)}, u32[]{:S(2)}) collective-permute-start(bf16[32,2176]{1,0:T(8,128)(2,1)S(1)} %get-tuple-element.21.after.refs_7_), channel_id=1, source_target_pairs={{0,1},{1,0},{2,3},{3,2},{4,5},{5,4},{6,7},{7,6},{8,9},{9,8},{10,11... | collective-permute-start | bytes 417800 | tf_op jit(solution)/shard_map/ppermute | solution.py:100
  26.1 3.8 %collective-permute-start.3 = (bf16[32,2176]{1,0:T(8,128)(2,1)S(1)}, bf16[32,2176]{1,0:T(8,128)(2,1)S(1)}, u32[]{:S(2)}, u32[]{:S(2)}) collective-permute-start(bf16[32,2176]{1,0:T(8,128)(2,1)S(1)} %collective-permute-done.refs_5_), channel_id=1, source_target_pairs={{0,1},{1,0},{2,3},{3,2},{4,5},{5,4},{6,7},{7,6},{8,9},{9,8},{10,11... | collective-permute-start | bytes 417800 | tf_op jit(solution)/shard_map/ppermute | solution.py:100
  26.4 3.5 %collective-permute-start.5 = (bf16[32,2176]{1,0:T(8,128)(2,1)S(1)}, bf16[32,2176]{1,0:T(8,128)(2,1)S(1)}, u32[]{:S(2)}, u32[]{:S(2)}) collective-permute-start(bf16[32,2176]{1,0:T(8,128)(2,1)S(1)} %collective-permute-done.4.refs_6_), channel_id=1, source_target_pairs={{0,1},{1,0},{2,3},{3,2},{4,5},{5,4},{6,7},{7,6},{8,9},{9,8},{10,11... | collective-permute-start | bytes 417800 | tf_op jit(solution)/shard_map/ppermute | solution.py:100
  26.7 3.3 %collective-permute-start.2 = (bf16[32,2176]{1,0:T(8,128)(2,1)S(1)}, bf16[32,2176]{1,0:T(8,128)(2,1)S(1)}, u32[]{:S(2)}, u32[]{:S(2)}) collective-permute-start(bf16[32,2176]{1,0:T(8,128)(2,1)S(1)} %collective-permute-done.1.refs_4_), channel_id=1, source_target_pairs={{0,1},{1,0},{2,3},{3,2},{4,5},{5,4},{6,7},{7,6},{8,9},{9,8},{10,11... | collective-permute-start | bytes 417800 | tf_op jit(solution)/shard_map/ppermute | solution.py:100
  29.6 3.4 %collective-permute-start.19 = (bf16[128,2048]{1,0:T(8,128)(2,1)S(1)}, bf16[128,2048]{1,0:T(8,128)(2,1)S(1)}, u32[]{:S(2)}, u32[]{:S(2)}) collective-permute-start(bf16[128,2048]{1,0:T(8,128)(2,1)S(1)} %get-tuple-element.30), channel_id=1, source_target_pairs={{0,1},{1,0},{2,3},{3,2},{4,5},{5,4},{6,7},{7,6},{8,9},{9,8},{10,11... | collective-permute-start | bytes 1572872 | tf_op jit(solution)/shard_map/ppermute | solution.py:100
  32.6 2.5 %collective-permute-start.7 = (bf16[128,2048]{1,0:T(8,128)(2,1)S(1)}, bf16[128,2048]{1,0:T(8,128)(2,1)S(1)}, u32[]{:S(2)}, u32[]{:S(2)}) collective-permute-start(bf16[128,2048]{1,0:T(8,128)(2,1)S(1)} %get-tuple-element.24), channel_id=1, source_target_pairs={{0,1},{1,0},{2,3},{3,2},{4,5},{5,4},{6,7},{7,6},{8,9},{9,8},{10,11... | collective-permute-start | bytes 1572872 | tf_op jit(solution)/shard_map/ppermute | solution.py:100
  33.1 6.4 %collective-permute-start.22 = (bf16[32,2048]{1,0:T(8,128)(2,1)S(1)}, bf16[32,2048]{1,0:T(8,128)(2,1)S(1)}, u32[]{:S(2)}, u32[]{:S(2)}) collective-permute-start(bf16[32,2048]{1,0:T(8,128)(2,1)S(1)} %get-tuple-element.34), channel_id=1, source_target_pairs={{0,2},{1,3},{2,0},{3,1},{4,6},{5,7},{6,4},{7,5},{8,10},{9,11},{10,... | collective-permute-start | bytes 393224 | tf_op jit(solution)/shard_map/ppermute | solution.py:100
  34.3 8.0 %collective-permute-start.20 = (bf16[32,2048]{1,0:T(8,128)(2,1)S(1)}, bf16[32,2048]{1,0:T(8,128)(2,1)S(1)}, u32[]{:S(2)}, u32[]{:S(2)}) collective-permute-start(bf16[32,2048]{1,0:T(8,128)(2,1)S(1)} %get-tuple-element.32), channel_id=1, source_target_pairs={{0,2},{1,3},{2,0},{3,1},{4,6},{5,7},{6,4},{7,5},{8,10},{9,11},{10,... | collective-permute-start | bytes 393224 | tf_op jit(solution)/shard_map/ppermute | solution.py:100
  35.3 9.9 %collective-permute-start.8 = (bf16[32,2048]{1,0:T(8,128)(2,1)S(1)}, bf16[32,2048]{1,0:T(8,128)(2,1)S(1)}, u32[]{:S(2)}, u32[]{:S(2)}) collective-permute-start(bf16[32,2048]{1,0:T(8,128)(2,1)S(1)} %get-tuple-element.26), channel_id=1, source_target_pairs={{0,2},{1,3},{2,0},{3,1},{4,6},{5,7},{6,4},{7,5},{8,10},{9,11},{10,... | collective-permute-start | bytes 393224 | tf_op jit(solution)/shard_map/ppermute | solution.py:100
  36.5 10.7 %collective-permute-start.10 = (bf16[32,2048]{1,0:T(8,128)(2,1)S(1)}, bf16[32,2048]{1,0:T(8,128)(2,1)S(1)}, u32[]{:S(2)}, u32[]{:S(2)}) collective-permute-start(bf16[32,2048]{1,0:T(8,128)(2,1)S(1)} %get-tuple-element.28), channel_id=1, source_target_pairs={{0,2},{1,3},{2,0},{3,1},{4,6},{5,7},{6,4},{7,5},{8,10},{9,11},{10,... | collective-permute-start | bytes 393224 | tf_op jit(solution)/shard_map/ppermute | solution.py:100
  39.5 7.7 %collective-permute-start.23 = (bf16[32,2048]{1,0:T(8,128)(2,1)S(1)}, bf16[32,2048]{1,0:T(8,128)(2,1)S(1)}, u32[]{:S(2)}, u32[]{:S(2)}) collective-permute-start(bf16[32,2048]{1,0:T(8,128)(2,1)S(1)} %level_sum.5), channel_id=1, source_target_pairs={{0,4},{1,5},{2,6},{3,7},{4,0},{5,1},{6,2},{7,3},{8,12},{9,13},{10,... | collective-permute-start | bytes 393224 | tf_op jit(solution)/shard_map/ppermute | solution.py:100
  42.3 7.4 %collective-permute-start.21 = (bf16[32,2048]{1,0:T(8,128)(2,1)S(1)}, bf16[32,2048]{1,0:T(8,128)(2,1)S(1)}, u32[]{:S(2)}, u32[]{:S(2)}) collective-permute-start(bf16[32,2048]{1,0:T(8,128)(2,1)S(1)} %level_sum.4), channel_id=1, source_target_pairs={{0,12},{1,13},{2,14},{3,15},{4,8},{5,9},{6,10},{7,11},{8,4},{9,5},... | collective-permute-start | bytes 393224 | tf_op jit(solution)/shard_map/ppermute | solution.py:100
  45.2 11.1 %collective-permute-start.9 = (bf16[32,2048]{1,0:T(8,128)(2,1)S(1)}, bf16[32,2048]{1,0:T(8,128)(2,1)S(1)}, u32[]{:S(2)}, u32[]{:S(2)}) collective-permute-start(bf16[32,2048]{1,0:T(8,128)(2,1)S(1)} %level_sum.3), channel_id=1, source_target_pairs={{0,8},{1,9},{2,10},{3,11},{4,12},{5,13},{6,14},{7,15},{8,0},{9,1},... | collective-permute-start | bytes 393224 | tf_op jit(solution)/shard_map/ppermute | solution.py:100

commit v5 on v4

--- a/solution.py
+++ b/solution.py
@@ -100,17 +100,22 @@
     return lax.ppermute(x, "ep", [(i, i ^ mask) for i in range(devices)])
 
 
+def near_and_far(zs):
+    return list(range(zs // 2)), list(range(zs // 2, zs))
+
+
 def gathered(x):
-    zs, ys, cs = grid_of(lax.axis_size("ep"))
-    pieces = {(0, 0, 0): x}
-    for dz in range(1, zs):
-        pieces[dz, 0, 0] = send(x, dz, 0, 0)
-    for dz in range(zs):
+    zs, ys, _ = grid_of(lax.axis_size("ep"))
+    near, far = near_and_far(zs)
+    pieces = {(0, 0): x}
+    for dz in near:
+        for dy in range(ys):
+            if dz or dy:
+                pieces[dz, dy] = send(x, dz, dy, 0)
+    for dz in far:
+        pieces[dz, 0] = send(x, dz, 0, 0)
         for dy in range(1, ys):
-            pieces[dz, dy, 0] = send(pieces[dz, 0, 0], 0, dy, 0)
-    for dz, dy, _ in list(pieces):
-        for dc in range(1, cs):
-            pieces[dz, dy, dc] = send(pieces[dz, dy, 0], 0, 0, dc)
+            pieces[dz, dy] = send(pieces[dz, 0], 0, dy, 0)
     return pieces
 
 
@@ -301,98 +306,76 @@
 
 
 def expert_body(*refs, count, experts, local_count):
-    pieces = refs[:count]
-    w_gate, w_up, w_down, away, kept, inner, weight = refs[count:]
-    width = w_gate.shape[1]
-    hidden = w_gate.shape[2]
+    pieces, refs = refs[:count], refs[count:]
+    sides, outs, (inner, weight) = refs[:6], refs[6:-2], refs[-2:]
+    width, hidden = sides[0].shape[1:]
     rows = pieces[0].shape[0]
     f32 = jnp.float32
-    x = jnp.concatenate([piece[:, :width] for piece in pieces], axis=0)
-    table = jnp.concatenate([piece[:, width:] for piece in pieces], axis=0).astype(f32)
+    filler = [pieces[-1]] * max(0, LANES // rows - count)
+    x = jnp.concatenate([piece[:, :width] for piece in (*pieces, *filler)], axis=0)
+    table = jnp.concatenate([piece[:, width:] for piece in (*pieces, *filler)], axis=0)
+    table = table.astype(f32)
     lane = lax.broadcasted_iota(jnp.int32, table.shape, 1)
-    for local in range(local_count):
-        expert = lax.axis_index("ep") * local_count + local
-        mine = (
-            (lane == expert) | (lane == expert + experts) | (lane == expert + 2 * experts)
-        )
-        weight[...] = jnp.broadcast_to(
-            jnp.sum(jnp.where(mine, table, 0.0), axis=1, keepdims=True), weight.shape
-        )
-        for f in range(0, hidden, TILE):
-            cols = slice(f, f + TILE)
-            gate_part = jnp.dot(x, w_gate[local, :, cols], preferred_element_type=f32)
-            up_part = jnp.dot(x, w_up[local, :, cols], preferred_element_type=f32)
-            silu = gate_part / (1.0 + jnp.exp(-gate_part))
-            inner[:, cols] = (silu * up_part).astype(jnp.bfloat16)
-        mid = inner[...]
-        half = count // 2 * rows
-        for d in range(0, width, TILE):
-            cols = slice(d, d + TILE)
-            out = jnp.dot(mid, w_down[local, :, cols], preferred_element_type=f32)
+    place = lax.axis_index("ep")
+    partner = place + 1 - 2 * (place % 2)
+    downs = []
+    for side, owner in enumerate((place, partner)):
+        w_gate, w_up, w_down = sides[3 * side : 3 * side + 3]
+        for local in range(local_count):
+            expert = owner * local_count + local
+            mine = (
+                (lane == expert) | (lane == expert + experts) | (lane == expert + 2 * experts)
+            )
+            slot = len(downs)
+            weight[slot] = jnp.broadcast_to(
+                jnp.sum(jnp.where(mine, table, 0.0), axis=1, keepdims=True), table.shape
+            )
+            for f in range(0, hidden, TILE):
+                cols = slice(f, f + TILE)
+                gate_part = jnp.dot(x, w_gate[local, :, cols], preferred_element_type=f32)
+                up_part = jnp.dot(x, w_up[local, :, cols], preferred_element_type=f32)
+                silu = gate_part / (1.0 + jnp.exp(-gate_part))
+                inner[slot, :, cols] = (silu * up_part).astype(jnp.bfloat16)
+            downs.append((w_down, local))
+    for d in range(0, width, TILE):
+        totals = [0.0] * (TILE // LANES)
+        for slot, (w_down, local) in enumerate(downs):
+            out = jnp.dot(inner[slot], w_down[local, :, d : d + TILE], preferred_element_type=f32)
             out = out.astype(jnp.bfloat16).astype(f32)
-            for j in range(0, TILE, LANES):
-                part = slice(d + j, d + j + LANES)
-                scaled = out[:, j : j + LANES] * weight[...]
-                if local == 0:
-                    away_sum, kept_sum = scaled[:half], scaled[half:]
-                else:
-                    away_sum = away[:, part].astype(f32) + scaled[:half]
-                    kept_sum = kept[:, part] + scaled[half:]
-                away[:, part] = away_sum.astype(away.dtype)
-                kept[:, part] = kept_sum
-
-
-def expert_rows(pieces, w_gate, w_up, w_down, experts):
+            for j in range(TILE // LANES):
+                totals[j] = totals[j] + out[:, j * LANES : (j + 1) * LANES] * weight[slot]
+        for j, total in enumerate(totals):
+            cols = slice(d + j * LANES, d + (j + 1) * LANES)
+            for i, result in enumerate(outs):
+                result[:, cols] = total[i * rows : (i + 1) * rows].astype(result.dtype)
+
+
+def expert_rows(pieces, weights, experts):
     rows = pieces[0].shape[0]
-    local_count, width, hidden = w_gate.shape
+    local_count, width, hidden = weights[0].shape
     count = len(pieces)
-    half = count // 2 * rows
+    kinds = [jnp.bfloat16] * (count - 1) + [jnp.float32]
+    padded = max(count, LANES // rows) * rows
     vmem = pl.BlockSpec(memory_space=pltpu.VMEM)
     return pl.pallas_call(
         functools.partial(
             expert_body, count=count, experts=experts, local_count=local_count
         ),
-        out_shape=(
-            jax.ShapeDtypeStruct((half, width), jnp.bfloat16),
-            jax.ShapeDtypeStruct((count * rows - half, width), jnp.float32),
-        ),
-        in_specs=[vmem] * (count + 3),
-        out_specs=(vmem, vmem),
+        out_shape=tuple(jax.ShapeDtypeStruct((rows, width), kind) for kind in kinds),
+        in_specs=[vmem] * (count + 6),
+        out_specs=(vmem,) * count,
         scratch_shapes=[
-            pltpu.VMEM((count * rows, hidden), jnp.bfloat16),
-            pltpu.VMEM((count * rows, LANES), jnp.float32),
+            pltpu.VMEM((2 * local_count, padded, hidden), jnp.bfloat16),
+            pltpu.VMEM((2 * local_count, padded, LANES), jnp.float32),
         ],
         compiler_params=pltpu.CompilerParams(vmem_limit_bytes=16 * MIB),
         cost_estimate=pl.CostEstimate(
-            flops=6 * count * rows * width * hidden * local_count,
-            bytes_accessed=6 * width * hidden * local_count,
-            transcendentals=count * rows * hidden,
+            flops=12 * count * rows * width * hidden * local_count,
+            bytes_accessed=12 * width * hidden * local_count,
+            transcendentals=2 * count * rows * hidden,
         ),
         name="expert_rows",
-    )(*pieces, w_gate, w_up, w_down)
-
-
-def chip_body(kept, arrived, *outs, dzs, ys):
-    rows = outs[0].shape[0]
-    for i in range(dzs):
-        for j in range(ys):
-            at = slice((i * ys + j) * rows, (i * ys + j + 1) * rows)
-            out = outs[i * ys + j]
-            out[...] = (kept[at] + arrived[at].astype(jnp.float32)).astype(out.dtype)
-
-
-def chip_sums(kept, arrived, dzs, ys):
-    rows, width = kept.shape[0] // (dzs * ys), kept.shape[1]
-    vmem = pl.BlockSpec(memory_space=pltpu.VMEM)
-    kinds = ([jnp.bfloat16] * (ys - 1) + [jnp.float32]) * dzs
-    return pl.pallas_call(
-        functools.partial(chip_body, dzs=dzs, ys=ys),
-        out_shape=tuple(jax.ShapeDtypeStruct((rows, width), kind) for kind in kinds),
-        in_specs=[vmem] * 2,
-        out_specs=(vmem,) * len(kinds),
-        compiler_params=pltpu.CompilerParams(vmem_limit_bytes=4 * MIB),
-        name="chip_sums",
-    )(kept, arrived)
+    )(*pieces, *weights)
 
 
 def level_body(own, *refs):
@@ -414,38 +397,29 @@
     )(own, *arrived)
 
 
-def chunks_of(zs):
-    order = [zs // 2] + [d for d in range(zs - 1, 0, -1) if d != zs // 2]
-    return [[order[0], 0], order[1:]]
-
-
-def dense(payload, resid, w_gate, w_up, w_down):
+def chunks_of(zs, ys):
+    near, far = near_and_far(zs)
+    places = [(dz, dy) for dz in near[::-1] for dy in range(ys - 1, -1, -1)]
+    return [places] + [[(dz, dy) for dy in range(ys - 1, -1, -1)] for dz in far]
+
+
+def dense(payload, resid, weights):
     devices = lax.axis_size("ep")
-    local_count = w_gate.shape[0]
-    experts = devices * local_count
+    experts = devices * weights[0].shape[0]
     zs, ys, _ = grid_of(devices)
-    f32 = jnp.float32
     pieces = gathered(payload)
-    w_down = loaded(payload, w_down)
-    w_up = loaded(payload, w_up)
     total = resid
-    for chunk in chunks_of(zs):
-        dys = list(range(1, ys)) + [0]
-        names = [(dz, dy, dc) for dc in (1, 0) for dz in chunk for dy in dys]
-        away, kept = expert_rows([pieces[name] for name in names], w_gate, w_up, w_down, experts)
-        arrived = send(away, 0, 0, 1)
-        sums = chip_sums(kept, arrived, len(chunk), ys)
-        for i, dz in enumerate(chunk):
-            level = sums[(i + 1) * ys - 1]
-            arrived = [send(sums[i * ys + j], 0, dy, 0) for j, dy in enumerate(dys[:-1])]
-            if dz:
-                level = level_sum(level, arrived)
-                arrived = [send(level, dz, 0, 0)]
-                total = total + arrived[0].astype(f32)
-            else:
-                total = total + level
-                for part in arrived:
-                    total = total + part.astype(f32)
+    for number, places in enumerate(chunks_of(zs, ys)):
+        *leaving, own = expert_rows([pieces[place] for place in places], weights, experts)
+        back = [own]
+        for (dz, dy), part in zip(places, leaving):
+            back.append(send(part, 0 if number else dz, dy, 0))
+        if number:
+            dz = places[0][0]
+            level = level_sum(back[0], back[1:])
+            back = [send(level, dz, 0, 0)]
+        for part in back:
+            total = total + part.astype(jnp.float32)
     return total.astype(jnp.bfloat16)
 
 
@@ -466,11 +440,14 @@
     devices = lax.axis_size("ep")
     experts = devices * w_gate.shape[0]
     if 2 * expert_ids.shape[1] >= experts and dense_fits(devices) and 3 * experts <= LANES:
+        other = [send(w, 0, 0, 1) for w in (w_gate, w_up, w_down)]
         payload, resid, w_gate = attention(
             hidden_in, queries, stored_keys, stored_values, stored_lengths, norm_gain,
             expert_ids, gate_weights, w_gate, experts,
         )
-        return dense(payload, resid, w_gate, w_up, w_down)
+        w_down = loaded(payload, w_down)
+        w_up = loaded(payload, w_up)
+        return dense(payload, resid, (w_gate, w_up, w_down, *other))
     attention_output = cached_attention(
         queries, stored_keys, stored_values, stored_lengths, QUERY_HEADS, KEY_VALUE_HEADS
     )

time: 57.2 us -> 55.9 us (0.977)
  Pallas kernels: 12.4 us -> 15.1 us
  waiting for transfers between devices: 19.7 us -> 17.6 us
  starting transfers between devices: 24.1 us -> 22.1 us
    pallas_call x2 -> x3, Pallas kernels: 5.36 us -> 8.22 us  [expert_rows(): pl.pallas_call(functools.partial(expert_body, count=count, experts=expert...]
    ppermute x24 -> x17, waiting for transfers between devices: 19.7 us -> 17.6 us  [send(): return lax.ppermute(x, 'ep', [(i, i ^ mask) for i in range(devices)])]
    ppermute x24 -> x17, starting transfers between devices: 24.1 us -> 22.1 us  [send(): return lax.ppermute(x, 'ep', [(i, i ^ mask) for i in range(devices)])]
  transfers between devices with their start and end apart: 24 -> 17, of which waited for: 9 -> 4; matrix products, arithmetic and copies ran while one was open for 0% -> 0% of each run, Pallas kernels for 16% -> 27%
where the time goes in v5:
time: 55.9 us; the launch traced here: 55.7 us
  starting transfers between devices  22.1 us (40%)
  waiting for transfers between devices  17.6 us (31%)
  Pallas kernels  15.1 us (27%)
  other arithmetic  0.77 us (1%)
    ppermute x17, starting transfers between devices, send(): return lax.ppermute(x, 'ep', [(i, i ^ mask) for i in range(devices)])  22.1 us
    ppermute x17, waiting for transfers between devices, send(): return lax.ppermute(x, 'ep', [(i, i ^ mask) for i in range(devices)])  17.6 us
    pallas_call x3, Pallas kernels, expert_rows(): pl.pallas_call(functools.partial(expert_body, count=count, experts=expert...  8.22 us
    pallas_call x2, Pallas kernels, loaded(): pl.pallas_call(loader_body, out_shape=jax.ShapeDtypeStruct(x.shape, x.dty...  3.8 us
    pallas_call x1, Pallas kernels, attention(): pl.pallas_call(functools.partial(attention_body, experts=experts), out_sh...  3.05 us
  transfers between devices with their start and end apart: 17, of which 4 were waited for; matrix products, arithmetic and copies ran while one was open for 0% of the time, Pallas kernels for 27%

profile of v5, /device:TPU:0, one launch (start us, length us, event | category | flops | bytes accessed | tf_op | source)
XLA Modules:
  0.0 55.7 jit_solution(5939953182110426908)
XLA Ops:
  0.0 0.5 collective-permute-start.3
  0.5 0.0 collective-permute-start.4
  0.5 0.5 collective-permute-start.5
  1.0 3.0 %attention.1 = (bf16[32,2176]{1,0:T(8,128)(2,1)S(1)}, f32[32,2048]{1,0:T(8,128)S(1)}, bf16[1,2048,768]{2,1,0:T(8,128)(2,1)S(1)}) custom-call(s32[32]{0:T(128)} %lengths_in.1, bf16[32,2048]{1,0:T(8,128)(2,1)} %hidden_in.1, bf16[32,2048]{1,0:T(8,128)(2,1)} %queries_in.1, bf16[32,64,256]{2,1,0:T(8,128)(2,1)} %keys_in.1, bf16[32,64,256]{2,1,0:T(8,128)(2,1)} %values_in.1, ...), custom_call_target="tpu_custom_call" | custom-call | tf_op jit(solution)/shard_map/attention/pallas_call | solution.py:265
  4.1 3.6 %collective-permute-start.9 = (bf16[32,2176]{1,0:T(8,128)(2,1)S(1)}, bf16[32,2176]{1,0:T(8,128)(2,1)S(1)}, u32[]{:S(2)}, u32[]{:S(2)}) collective-permute-start(bf16[32,2176]{1,0:T(8,128)(2,1)S(1)} %get-tuple-element.17.after.refs_3_), channel_id=1, source_target_pairs={{0,8},{1,9},{2,10},{3,11},{4,12},{5,13},{6,14},{7,15},{8,0},{9,1},... | collective-permute-start | bytes 417800 | tf_op jit(solution)/shard_map/ppermute | solution.py:100
  7.7 1.4 %collective-permute-start.13 = (bf16[32,2176]{1,0:T(8,128)(2,1)S(1)}, bf16[32,2176]{1,0:T(8,128)(2,1)S(1)}, u32[]{:S(2)}, u32[]{:S(2)}) collective-permute-start(bf16[32,2176]{1,0:T(8,128)(2,1)S(1)} %get-tuple-element.17.after.refs_3_), channel_id=1, source_target_pairs={{0,12},{1,13},{2,14},{3,15},{4,8},{5,9},{6,10},{7,11},{8,4},{9,5},... | collective-permute-start | bytes 417800 | tf_op jit(solution)/shard_map/ppermute | solution.py:100
  9.0 9.1 %collective-permute-done.9.refs_1_ = bf16[32,2176]{1,0:T(8,128)(2,1)S(1)} collective-permute-done((bf16[32,2176]{1,0:T(8,128)(2,1)S(1)}, bf16[32,2176]{1,0:T(8,128)(2,1)S(1)}, u32[]{:S(2)}, u32[]{:S(2)}) %collective-permute-start.9) | collective-permute-done | bytes 139296 | tf_op jit(solution)/shard_map/ppermute | solution.py:100
  18.2 1.9 %collective-permute-start.10 = (bf16[32,2176]{1,0:T(8,128)(2,1)S(1)}, bf16[32,2176]{1,0:T(8,128)(2,1)S(1)}, u32[]{:S(2)}, u32[]{:S(2)}) collective-permute-start(bf16[32,2176]{1,0:T(8,128)(2,1)S(1)} %collective-permute-done.9.refs_1_), channel_id=1, source_target_pairs={{0,2},{1,3},{2,0},{3,1},{4,6},{5,7},{6,4},{7,5},{8,10},{9,11},{10,... | collective-permute-start | bytes 417800 | tf_op jit(solution)/shard_map/ppermute | solution.py:100
  20.1 0.0 collective-permute-done.13.refs_1_
  20.1 0.2 collective-permute-start.14
  20.2 1.9 %loader.2.refs_5_.refs_3_ = bf16[1,2048,768]{2,1,0:T(8,128)(2,1)S(1)} custom-call(bf16[32,2176]{1,0:T(8,128)(2,1)S(1)} %get-tuple-element.17.after.refs_3_, bf16[1,2048,768]{2,1,0:T(8,128)(2,1)} %source.2), custom_call_target="tpu_custom_call" | custom-call | tf_op jit(solution)/shard_map/loader/pallas_call | solution.py:294
  22.1 1.9 %loader.3.refs_6_.refs_4_ = bf16[1,768,2048]{2,1,0:T(8,128)(2,1)S(1)} custom-call(bf16[32,2176]{1,0:T(8,128)(2,1)S(1)} %get-tuple-element.17.after.refs_3_, bf16[1,768,2048]{2,1,0:T(8,128)(2,1)} %source.3), custom_call_target="tpu_custom_call" | custom-call | tf_op jit(solution)/shard_map/loader/pallas_call | solution.py:294
  24.0 0.7 %collective-permute-done.10.refs_0_ = bf16[32,2176]{1,0:T(8,128)(2,1)S(1)} collective-permute-done((bf16[32,2176]{1,0:T(8,128)(2,1)S(1)}, bf16[32,2176]{1,0:T(8,128)(2,1)S(1)}, u32[]{:S(2)}, u32[]{:S(2)}) %collective-permute-start.10) | collective-permute-done | bytes 139296 | tf_op jit(solution)/shard_map/ppermute | solution.py:100
  24.7 2.4 %collective-permute-start = (bf16[32,2176]{1,0:T(8,128)(2,1)S(1)}, bf16[32,2176]{1,0:T(8,128)(2,1)S(1)}, u32[]{:S(2)}, u32[]{:S(2)}) collective-permute-start(bf16[32,2176]{1,0:T(8,128)(2,1)S(1)} %get-tuple-element.17.after.refs_3_), channel_id=1, source_target_pairs={{0,6},{1,7},{2,4},{3,5},{4,2},{5,3},{6,0},{7,1},{8,14},{9,15},{10,... | collective-permute-start | bytes 417800 | tf_op jit(solution)/shard_map/ppermute | solution.py:100
  27.1 0.0 collective-permute-done.3.refs_7_.refs_5_
  27.1 0.7 %collective-permute-start.1 = (bf16[32,2176]{1,0:T(8,128)(2,1)S(1)}, bf16[32,2176]{1,0:T(8,128)(2,1)S(1)}, u32[]{:S(2)}, u32[]{:S(2)}) collective-permute-start(bf16[32,2176]{1,0:T(8,128)(2,1)S(1)} %get-tuple-element.17.after.refs_3_), channel_id=1, source_target_pairs={{0,4},{1,5},{2,6},{3,7},{4,0},{5,1},{6,2},{7,3},{8,12},{9,13},{10,... | collective-permute-start | bytes 417800 | tf_op jit(solution)/shard_map/ppermute | solution.py:100
  27.8 0.0 collective-permute-done.4.refs_8_.refs_6_
  27.8 0.9 %collective-permute-start.2 = (bf16[32,2176]{1,0:T(8,128)(2,1)S(1)}, bf16[32,2176]{1,0:T(8,128)(2,1)S(1)}, u32[]{:S(2)}, u32[]{:S(2)}) collective-permute-start(bf16[32,2176]{1,0:T(8,128)(2,1)S(1)} %get-tuple-element.17.after.refs_3_), channel_id=1, source_target_pairs={{0,2},{1,3},{2,0},{3,1},{4,6},{5,7},{6,4},{7,5},{8,10},{9,11},{10,... | collective-permute-start | bytes 417800 | tf_op jit(solution)/shard_map/ppermute | solution.py:100
  28.7 0.0 collective-permute-done.5.refs_9_.refs_7_
  28.7 2.7 %expert_rows.4 = (bf16[32,2048]{1,0:T(8,128)(2,1)S(1)}, f32[32,2048]{1,0:T(8,128)S(1)}) custom-call(bf16[32,2176]{1,0:T(8,128)(2,1)S(1)} %collective-permute-done.10.refs_0_, bf16[32,2176]{1,0:T(8,128)(2,1)S(1)} %collective-permute-done.9.refs_1_, bf16[1,2048,768]{2,1,0:T(8,128)(2,1)S(1)} %get-tuple-element.18.refs_4_.refs_2_, ...), custom_call_target="tpu_custom_call" | custom-call | flops 1207959552 | bytes 18874368 | tf_op jit(solution)/shard_map/expert_rows/pallas_call | solution.py:360
  31.4 1.2 %collective-permute-start.11 = (bf16[32,2048]{1,0:T(8,128)(2,1)S(1)}, bf16[32,2048]{1,0:T(8,128)(2,1)S(1)}, u32[]{:S(2)}, u32[]{:S(2)}) collective-permute-start(bf16[32,2048]{1,0:T(8,128)(2,1)S(1)} %get-tuple-element.24), channel_id=1, source_target_pairs={{0,2},{1,3},{2,0},{3,1},{4,6},{5,7},{6,4},{7,5},{8,10},{9,11},{10,... | collective-permute-start | bytes 393224 | tf_op jit(solution)/shard_map/ppermute | solution.py:100
  32.6 0.0 collective-permute-done.14.refs_0_
  32.6 2.7 %expert_rows.5 = (bf16[32,2048]{1,0:T(8,128)(2,1)S(1)}, f32[32,2048]{1,0:T(8,128)S(1)}) custom-call(bf16[32,2176]{1,0:T(8,128)(2,1)S(1)} %collective-permute-done.14.refs_0_, bf16[32,2176]{1,0:T(8,128)(2,1)S(1)} %collective-permute-done.13.refs_1_, bf16[1,2048,768]{2,1,0:T(8,128)(2,1)S(1)} %get-tuple-element.18.refs_4_.refs_2_, ...), custom_call_target="tpu_custom_call" | custom-call | flops 1207959552 | bytes 18874368 | tf_op jit(solution)/shard_map/expert_rows/pallas_call | solution.py:360
  35.3 1.0 %collective-permute-start.15 = (bf16[32,2048]{1,0:T(8,128)(2,1)S(1)}, bf16[32,2048]{1,0:T(8,128)(2,1)S(1)}, u32[]{:S(2)}, u32[]{:S(2)}) collective-permute-start(bf16[32,2048]{1,0:T(8,128)(2,1)S(1)} %get-tuple-element.26), channel_id=1, source_target_pairs={{0,2},{1,3},{2,0},{3,1},{4,6},{5,7},{6,4},{7,5},{8,10},{9,11},{10,... | collective-permute-start | bytes 393224 | tf_op jit(solution)/shard_map/ppermute | solution.py:100
  36.3 0.0 collective-permute-done.refs_0_
  36.3 0.0 collective-permute-done.1.refs_1_
  36.3 0.0 collective-permute-done.2.refs_2_
  36.3 2.8 %expert_rows.3 = (bf16[32,2048]{1,0:T(8,128)(2,1)S(1)}, bf16[32,2048]{1,0:T(8,128)(2,1)S(1)}, bf16[32,2048]{1,0:T(8,128)(2,1)S(1)}, f32[32,2048]{1,0:T(8,128)S(1)}) custom-call(bf16[32,2176]{1,0:T(8,128)(2,1)S(1)} %collective-permute-done.refs_0_, bf16[32,2176]{1,0:T(8,128)(2,1)S(1)} %collective-permute-done.1.refs_1_, ...), custom_call_target="tpu_custom_call" | custom-call | flops 2415919104 | bytes 18874368 | tf_op jit(solution)/shard_map/expert_rows/pallas_call | solution.py:360
  39.1 2.0 %collective-permute-start.6 = (bf16[32,2048]{1,0:T(8,128)(2,1)S(1)}, bf16[32,2048]{1,0:T(8,128)(2,1)S(1)}, u32[]{:S(2)}, u32[]{:S(2)}) collective-permute-start(bf16[32,2048]{1,0:T(8,128)(2,1)S(1)} %get-tuple-element.20), channel_id=1, source_target_pairs={{0,6},{1,7},{2,4},{3,5},{4,2},{5,3},{6,0},{7,1},{8,14},{9,15},{10,... | collective-permute-start | bytes 393224 | tf_op jit(solution)/shard_map/ppermute | solution.py:100
  41.1 0.7 %collective-permute-start.7 = (bf16[32,2048]{1,0:T(8,128)(2,1)S(1)}, bf16[32,2048]{1,0:T(8,128)(2,1)S(1)}, u32[]{:S(2)}, u32[]{:S(2)}) collective-permute-start(bf16[32,2048]{1,0:T(8,128)(2,1)S(1)} %get-tuple-element.21), channel_id=1, source_target_pairs={{0,4},{1,5},{2,6},{3,7},{4,0},{5,1},{6,2},{7,3},{8,12},{9,13},{10,... | collective-permute-start | bytes 393224 | tf_op jit(solution)/shard_map/ppermute | solution.py:100
  41.7 0.9 %collective-permute-start.8 = (bf16[32,2048]{1,0:T(8,128)(2,1)S(1)}, bf16[32,2048]{1,0:T(8,128)(2,1)S(1)}, u32[]{:S(2)}, u32[]{:S(2)}) collective-permute-start(bf16[32,2048]{1,0:T(8,128)(2,1)S(1)} %get-tuple-element.22), channel_id=1, source_target_pairs={{0,2},{1,3},{2,0},{3,1},{4,6},{5,7},{6,4},{7,5},{8,10},{9,11},{10,... | collective-permute-start | bytes 393224 | tf_op jit(solution)/shard_map/ppermute | solution.py:100
  42.7 0.0 collective-permute-done.11.refs_0_
  42.7 3.9 %collective-permute-start.12 = (bf16[32,2048]{1,0:T(8,128)(2,1)S(1)}, bf16[32,2048]{1,0:T(8,128)(2,1)S(1)}, u32[]{:S(2)}, u32[]{:S(2)}) collective-permute-start(bf16[32,2048]{1,0:T(8,128)(2,1)S(1)} %level_sum.2), channel_id=1, source_target_pairs={{0,8},{1,9},{2,10},{3,11},{4,12},{5,13},{6,14},{7,15},{8,0},{9,1},... | collective-permute-start | bytes 393224 | tf_op jit(solution)/shard_map/ppermute | solution.py:100
  46.6 0.0 collective-permute-done.15.refs_0_
  46.7 0.5 collective-permute-start.16
  47.2 0.0 collective-permute-done.6
  47.2 0.3 collective-permute-done.7
  47.5 0.0 collective-permute-done.8
  47.5 7.4 %collective-permute-done.12 = bf16[32,2048]{1,0:T(8,128)(2,1)S(1)} collective-permute-done((bf16[32,2048]{1,0:T(8,128)(2,1)S(1)}, bf16[32,2048]{1,0:T(8,128)(2,1)S(1)}, u32[]{:S(2)}, u32[]{:S(2)}) %collective-permute-start.12) | collective-permute-done | bytes 131104 | tf_op jit(solution)/shard_map/ppermute | solution.py:100
  54.9 0.0 collective-permute-done.16
  54.9 0.8 %add_convert_fusion = bf16[32,2048]{1,0:T(8,128)(2,1)} fusion(bf16[32,2048]{1,0:T(8,128)(2,1)S(1)} %collective-permute-done.16, bf16[32,2048]{1,0:T(8,128)(2,1)S(1)} %collective-permute-done.12, bf16[32,2048]{1,0:T(8,128)(2,1)S(1)} %collective-permute-done.8, bf16[32,2048]{1,0:T(8,128)(2,1)S(1)} %collective-permute-done.7, ...), kind=kLoop, calls=%fused_computation | loop fusion | flops 786432 | bytes 1310720 | tf_op jit(solution)/shard_map/convert_element_type | solution.py:423
  (2 shorter events, 0.1 us)
Async XLA Ops:
  0.0 27.1 %collective-permute-start.3 = (bf16[1,2048,768]{2,1,0:T(8,128)(2,1)}, bf16[1,2048,768]{2,1,0:T(8,128)(2,1)S(1)}, u32[]{:S(2)}, u32[]{:S(2)}) collective-permute-start(bf16[1,2048,768]{2,1,0:T(8,128)(2,1)} %w_gate_in.1), channel_id=1, source_target_pairs={{0,1},{1,0},{2,3},{3,2},{4,5},{5,4},{6,7},{7,6},{8,9},{9,8},{10,11... | collective-permute-start | bytes 9437192 | tf_op jit(solution)/shard_map/ppermute | solution.py:100
  0.5 27.3 %collective-permute-start.4 = (bf16[1,2048,768]{2,1,0:T(8,128)(2,1)}, bf16[1,2048,768]{2,1,0:T(8,128)(2,1)S(1)}, u32[]{:S(2)}, u32[]{:S(2)}) collective-permute-start(bf16[1,2048,768]{2,1,0:T(8,128)(2,1)} %source.2), channel_id=1, source_target_pairs={{0,1},{1,0},{2,3},{3,2},{4,5},{5,4},{6,7},{7,6},{8,9},{9,8},{10,11... | collective-permute-start | bytes 9437192 | tf_op jit(solution)/shard_map/ppermute | solution.py:100
  0.5 28.2 %collective-permute-start.5 = (bf16[1,768,2048]{2,1,0:T(8,128)(2,1)}, bf16[1,768,2048]{2,1,0:T(8,128)(2,1)S(1)}, u32[]{:S(2)}, u32[]{:S(2)}) collective-permute-start(bf16[1,768,2048]{2,1,0:T(8,128)(2,1)} %source.3), channel_id=1, source_target_pairs={{0,1},{1,0},{2,3},{3,2},{4,5},{5,4},{6,7},{7,6},{8,9},{9,8},{10,11... | collective-permute-start | bytes 9437192 | tf_op jit(solution)/shard_map/ppermute | solution.py:100
  4.1 14.1 %collective-permute-start.9 = (bf16[32,2176]{1,0:T(8,128)(2,1)S(1)}, bf16[32,2176]{1,0:T(8,128)(2,1)S(1)}, u32[]{:S(2)}, u32[]{:S(2)}) collective-permute-start(bf16[32,2176]{1,0:T(8,128)(2,1)S(1)} %get-tuple-element.17.after.refs_3_), channel_id=1, source_target_pairs={{0,8},{1,9},{2,10},{3,11},{4,12},{5,13},{6,14},{7,15},{8,0},{9,1},... | collective-permute-start | bytes 417800 | tf_op jit(solution)/shard_map/ppermute | solution.py:100
  7.7 12.4 %collective-permute-start.13 = (bf16[32,2176]{1,0:T(8,128)(2,1)S(1)}, bf16[32,2176]{1,0:T(8,128)(2,1)S(1)}, u32[]{:S(2)}, u32[]{:S(2)}) collective-permute-start(bf16[32,2176]{1,0:T(8,128)(2,1)S(1)} %get-tuple-element.17.after.refs_3_), channel_id=1, source_target_pairs={{0,12},{1,13},{2,14},{3,15},{4,8},{5,9},{6,10},{7,11},{8,4},{9,5},... | collective-permute-start | bytes 417800 | tf_op jit(solution)/shard_map/ppermute | solution.py:100
  18.2 6.5 %collective-permute-start.10 = (bf16[32,2176]{1,0:T(8,128)(2,1)S(1)}, bf16[32,2176]{1,0:T(8,128)(2,1)S(1)}, u32[]{:S(2)}, u32[]{:S(2)}) collective-permute-start(bf16[32,2176]{1,0:T(8,128)(2,1)S(1)} %collective-permute-done.9.refs_1_), channel_id=1, source_target_pairs={{0,2},{1,3},{2,0},{3,1},{4,6},{5,7},{6,4},{7,5},{8,10},{9,11},{10,... | collective-permute-start | bytes 417800 | tf_op jit(solution)/shard_map/ppermute | solution.py:100
  20.1 12.5 %collective-permute-start.14 = (bf16[32,2176]{1,0:T(8,128)(2,1)S(1)}, bf16[32,2176]{1,0:T(8,128)(2,1)S(1)}, u32[]{:S(2)}, u32[]{:S(2)}) collective-permute-start(bf16[32,2176]{1,0:T(8,128)(2,1)S(1)} %collective-permute-done.13.refs_1_), channel_id=1, source_target_pairs={{0,2},{1,3},{2,0},{3,1},{4,6},{5,7},{6,4},{7,5},{8,10},{9,11},{10,... | collective-permute-start | bytes 417800 | tf_op jit(solution)/shard_map/ppermute | solution.py:100
  24.7 11.6 %collective-permute-start = (bf16[32,2176]{1,0:T(8,128)(2,1)S(1)}, bf16[32,2176]{1,0:T(8,128)(2,1)S(1)}, u32[]{:S(2)}, u32[]{:S(2)}) collective-permute-start(bf16[32,2176]{1,0:T(8,128)(2,1)S(1)} %get-tuple-element.17.after.refs_3_), channel_id=1, source_target_pairs={{0,6},{1,7},{2,4},{3,5},{4,2},{5,3},{6,0},{7,1},{8,14},{9,15},{10,... | collective-permute-start | bytes 417800 | tf_op jit(solution)/shard_map/ppermute | solution.py:100
  27.1 9.2 %collective-permute-start.1 = (bf16[32,2176]{1,0:T(8,128)(2,1)S(1)}, bf16[32,2176]{1,0:T(8,128)(2,1)S(1)}, u32[]{:S(2)}, u32[]{:S(2)}) collective-permute-start(bf16[32,2176]{1,0:T(8,128)(2,1)S(1)} %get-tuple-element.17.after.refs_3_), channel_id=1, source_target_pairs={{0,4},{1,5},{2,6},{3,7},{4,0},{5,1},{6,2},{7,3},{8,12},{9,13},{10,... | collective-permute-start | bytes 417800 | tf_op jit(solution)/shard_map/ppermute | solution.py:100
  27.8 8.5 %collective-permute-start.2 = (bf16[32,2176]{1,0:T(8,128)(2,1)S(1)}, bf16[32,2176]{1,0:T(8,128)(2,1)S(1)}, u32[]{:S(2)}, u32[]{:S(2)}) collective-permute-start(bf16[32,2176]{1,0:T(8,128)(2,1)S(1)} %get-tuple-element.17.after.refs_3_), channel_id=1, source_target_pairs={{0,2},{1,3},{2,0},{3,1},{4,6},{5,7},{6,4},{7,5},{8,10},{9,11},{10,... | collective-permute-start | bytes 417800 | tf_op jit(solution)/shard_map/ppermute | solution.py:100
  31.4 11.3 %collective-permute-start.11 = (bf16[32,2048]{1,0:T(8,128)(2,1)S(1)}, bf16[32,2048]{1,0:T(8,128)(2,1)S(1)}, u32[]{:S(2)}, u32[]{:S(2)}) collective-permute-start(bf16[32,2048]{1,0:T(8,128)(2,1)S(1)} %get-tuple-element.24), channel_id=1, source_target_pairs={{0,2},{1,3},{2,0},{3,1},{4,6},{5,7},{6,4},{7,5},{8,10},{9,11},{10,... | collective-permute-start | bytes 393224 | tf_op jit(solution)/shard_map/ppermute | solution.py:100
  35.3 11.3 %collective-permute-start.15 = (bf16[32,2048]{1,0:T(8,128)(2,1)S(1)}, bf16[32,2048]{1,0:T(8,128)(2,1)S(1)}, u32[]{:S(2)}, u32[]{:S(2)}) collective-permute-start(bf16[32,2048]{1,0:T(8,128)(2,1)S(1)} %get-tuple-element.26), channel_id=1, source_target_pairs={{0,2},{1,3},{2,0},{3,1},{4,6},{5,7},{6,4},{7,5},{8,10},{9,11},{10,... | collective-permute-start | bytes 393224 | tf_op jit(solution)/shard_map/ppermute | solution.py:100
  39.1 8.1 %collective-permute-start.6 = (bf16[32,2048]{1,0:T(8,128)(2,1)S(1)}, bf16[32,2048]{1,0:T(8,128)(2,1)S(1)}, u32[]{:S(2)}, u32[]{:S(2)}) collective-permute-start(bf16[32,2048]{1,0:T(8,128)(2,1)S(1)} %get-tuple-element.20), channel_id=1, source_target_pairs={{0,6},{1,7},{2,4},{3,5},{4,2},{5,3},{6,0},{7,1},{8,14},{9,15},{10,... | collective-permute-start | bytes 393224 | tf_op jit(solution)/shard_map/ppermute | solution.py:100
  41.1 6.4 %collective-permute-start.7 = (bf16[32,2048]{1,0:T(8,128)(2,1)S(1)}, bf16[32,2048]{1,0:T(8,128)(2,1)S(1)}, u32[]{:S(2)}, u32[]{:S(2)}) collective-permute-start(bf16[32,2048]{1,0:T(8,128)(2,1)S(1)} %get-tuple-element.21), channel_id=1, source_target_pairs={{0,4},{1,5},{2,6},{3,7},{4,0},{5,1},{6,2},{7,3},{8,12},{9,13},{10,... | collective-permute-start | bytes 393224 | tf_op jit(solution)/shard_map/ppermute | solution.py:100
  41.7 5.8 %collective-permute-start.8 = (bf16[32,2048]{1,0:T(8,128)(2,1)S(1)}, bf16[32,2048]{1,0:T(8,128)(2,1)S(1)}, u32[]{:S(2)}, u32[]{:S(2)}) collective-permute-start(bf16[32,2048]{1,0:T(8,128)(2,1)S(1)} %get-tuple-element.22), channel_id=1, source_target_pairs={{0,2},{1,3},{2,0},{3,1},{4,6},{5,7},{6,4},{7,5},{8,10},{9,11},{10,... | collective-permute-start | bytes 393224 | tf_op jit(solution)/shard_map/ppermute | solution.py:100
  42.7 12.2 %collective-permute-start.12 = (bf16[32,2048]{1,0:T(8,128)(2,1)S(1)}, bf16[32,2048]{1,0:T(8,128)(2,1)S(1)}, u32[]{:S(2)}, u32[]{:S(2)}) collective-permute-start(bf16[32,2048]{1,0:T(8,128)(2,1)S(1)} %level_sum.2), channel_id=1, source_target_pairs={{0,8},{1,9},{2,10},{3,11},{4,12},{5,13},{6,14},{7,15},{8,0},{9,1},... | collective-permute-start | bytes 393224 | tf_op jit(solution)/shard_map/ppermute | solution.py:100
  46.7 8.2 %collective-permute-start.16 = (bf16[32,2048]{1,0:T(8,128)(2,1)S(1)}, bf16[32,2048]{1,0:T(8,128)(2,1)S(1)}, u32[]{:S(2)}, u32[]{:S(2)}) collective-permute-start(bf16[32,2048]{1,0:T(8,128)(2,1)S(1)} %level_sum.3), channel_id=1, source_target_pairs={{0,12},{1,13},{2,14},{3,15},{4,8},{5,9},{6,10},{7,11},{8,4},{9,5},... | collective-permute-start | bytes 393224 | tf_op jit(solution)/shard_map/ppermute | solution.py:100

commit v6 on v5

--- a/solution.py
+++ b/solution.py
@@ -350,11 +350,10 @@
                 result[:, cols] = total[i * rows : (i + 1) * rows].astype(result.dtype)
 
 
-def expert_rows(pieces, weights, experts):
+def expert_rows(pieces, weights, experts, kinds):
     rows = pieces[0].shape[0]
     local_count, width, hidden = weights[0].shape
     count = len(pieces)
-    kinds = [jnp.bfloat16] * (count - 1) + [jnp.float32]
     padded = max(count, LANES // rows) * rows
     vmem = pl.BlockSpec(memory_space=pltpu.VMEM)
     return pl.pallas_call(
@@ -399,27 +398,31 @@
 
 def chunks_of(zs, ys):
     near, far = near_and_far(zs)
-    places = [(dz, dy) for dz in near[::-1] for dy in range(ys - 1, -1, -1)]
-    return [places] + [[(dz, dy) for dy in range(ys - 1, -1, -1)] for dz in far]
+    return [[(dz, dy) for dy in range(ys) for dz in pair] for pair in zip(far, near)]
 
 
 def dense(payload, resid, weights):
     devices = lax.axis_size("ep")
     experts = devices * weights[0].shape[0]
     zs, ys, _ = grid_of(devices)
+    far = near_and_far(zs)[1]
     pieces = gathered(payload)
     total = resid
     for number, places in enumerate(chunks_of(zs, ys)):
-        *leaving, own = expert_rows([pieces[place] for place in places], weights, experts)
-        back = [own]
-        for (dz, dy), part in zip(places, leaving):
-            back.append(send(part, 0 if number else dz, dy, 0))
-        if number:
-            dz = places[0][0]
-            level = level_sum(back[0], back[1:])
-            back = [send(level, dz, 0, 0)]
-        for part in back:
-            total = total + part.astype(jnp.float32)
+        here = [(far[number], 0), (0, 0)]
+        kinds = [jnp.float32 if place in here else jnp.bfloat16 for place in places]
+        sums = expert_rows([pieces[place] for place in places], weights, experts, kinds)
+        sums = dict(zip(places, sums))
+        arrived = []
+        for (dz, dy), part in sums.items():
+            if dz == far[number]:
+                arrived += [send(part, 0, dy, 0)] if dy else []
+            else:
+                back = send(part, dz, dy, 0) if dz or dy else part
+                total = total + back.astype(jnp.float32)
+        level = level_sum(sums[far[number], 0], arrived)
+        back = send(level, far[number], 0, 0)
+        total = total + back.astype(jnp.float32)
     return total.astype(jnp.bfloat16)
 
 

time: 55.9 us -> 53.7 us (0.961)
  Pallas kernels: 15.1 us -> 12.5 us
  starting transfers between devices: 22.1 us -> 24.4 us
  waiting for transfers between devices: 17.6 us -> 15.7 us
    pallas_call x3 -> x2, Pallas kernels: 8.22 us -> 5.6 us  [expert_rows(): pl.pallas_call(functools.partial(expert_body, count=count, experts=expert...]
    ppermute x17, starting transfers between devices: 22.1 us -> 24.4 us  [send(): return lax.ppermute(x, 'ep', [(i, i ^ mask) for i in range(devices)])]
    ppermute x17, waiting for transfers between devices: 17.6 us -> 15.7 us  [send(): return lax.ppermute(x, 'ep', [(i, i ^ mask) for i in range(devices)])]
  transfers between devices with their start and end apart: 17 -> 17, of which waited for: 4 -> 5; matrix products, arithmetic and copies ran while one was open for 0% -> 0% of each run, Pallas kernels for 27% -> 23%
where the time goes in v6:
time: 53.7 us; the launch traced here: 53.5 us
  starting transfers between devices  24.4 us (45%)
  waiting for transfers between devices  15.7 us (29%)
  Pallas kernels  12.5 us (23%)
  other arithmetic  0.77 us (1%)
    ppermute x17, starting transfers between devices, send(): return lax.ppermute(x, 'ep', [(i, i ^ mask) for i in range(devices)])  24.4 us
    ppermute x17, waiting for transfers between devices, send(): return lax.ppermute(x, 'ep', [(i, i ^ mask) for i in range(devices)])  15.7 us
    pallas_call x2, Pallas kernels, expert_rows(): pl.pallas_call(functools.partial(expert_body, count=count, experts=expert...  5.6 us
    pallas_call x2, Pallas kernels, loaded(): pl.pallas_call(loader_body, out_shape=jax.ShapeDtypeStruct(x.shape, x.dty...  3.8 us
    pallas_call x1, Pallas kernels, attention(): pl.pallas_call(functools.partial(attention_body, experts=experts), out_sh...  3.05 us
  transfers between devices with their start and end apart: 17, of which 5 were waited for; matrix products, arithmetic and copies ran while one was open for 0% of the time, Pallas kernels for 23%

profile of v6, /device:TPU:0, one launch (start us, length us, event | category | flops | bytes accessed | tf_op | source)
XLA Modules:
  0.0 53.5 jit_solution(2267432689282315765)
XLA Ops:
  0.0 0.5 collective-permute-start.3
  0.5 0.0 collective-permute-start.4
  0.5 0.5 collective-permute-start.5
  1.0 3.0 %attention.1 = (bf16[32,2176]{1,0:T(8,128)(2,1)S(1)}, f32[32,2048]{1,0:T(8,128)S(1)}, bf16[1,2048,768]{2,1,0:T(8,128)(2,1)S(1)}) custom-call(s32[32]{0:T(128)} %lengths_in.1, bf16[32,2048]{1,0:T(8,128)(2,1)} %hidden_in.1, bf16[32,2048]{1,0:T(8,128)(2,1)} %queries_in.1, bf16[32,64,256]{2,1,0:T(8,128)(2,1)} %keys_in.1, bf16[32,64,256]{2,1,0:T(8,128)(2,1)} %values_in.1, ...), custom_call_target="tpu_custom_call" | custom-call | tf_op jit(solution)/shard_map/attention/pallas_call | solution.py:265
  4.1 3.6 %collective-permute-start = (bf16[32,2176]{1,0:T(8,128)(2,1)S(1)}, bf16[32,2176]{1,0:T(8,128)(2,1)S(1)}, u32[]{:S(2)}, u32[]{:S(2)}) collective-permute-start(bf16[32,2176]{1,0:T(8,128)(2,1)S(1)} %get-tuple-element.17.after.refs_1_), channel_id=1, source_target_pairs={{0,8},{1,9},{2,10},{3,11},{4,12},{5,13},{6,14},{7,15},{8,0},{9,1},... | collective-permute-start | bytes 417800 | tf_op jit(solution)/shard_map/ppermute | solution.py:100
  7.7 1.5 %collective-permute-start.2 = (bf16[32,2176]{1,0:T(8,128)(2,1)S(1)}, bf16[32,2176]{1,0:T(8,128)(2,1)S(1)}, u32[]{:S(2)}, u32[]{:S(2)}) collective-permute-start(bf16[32,2176]{1,0:T(8,128)(2,1)S(1)} %get-tuple-element.17.after.refs_1_), channel_id=1, source_target_pairs={{0,2},{1,3},{2,0},{3,1},{4,6},{5,7},{6,4},{7,5},{8,10},{9,11},{10,... | collective-permute-start | bytes 417800 | tf_op jit(solution)/shard_map/ppermute | solution.py:100
  9.2 5.8 %collective-permute-done.refs_0_ = bf16[32,2176]{1,0:T(8,128)(2,1)S(1)} collective-permute-done((bf16[32,2176]{1,0:T(8,128)(2,1)S(1)}, bf16[32,2176]{1,0:T(8,128)(2,1)S(1)}, u32[]{:S(2)}, u32[]{:S(2)}) %collective-permute-start) | collective-permute-done | bytes 139296 | tf_op jit(solution)/shard_map/ppermute | solution.py:100
  15.0 3.5 %collective-permute-start.9 = (bf16[32,2176]{1,0:T(8,128)(2,1)S(1)}, bf16[32,2176]{1,0:T(8,128)(2,1)S(1)}, u32[]{:S(2)}, u32[]{:S(2)}) collective-permute-start(bf16[32,2176]{1,0:T(8,128)(2,1)S(1)} %get-tuple-element.17.after.refs_1_), channel_id=1, source_target_pairs={{0,12},{1,13},{2,14},{3,15},{4,8},{5,9},{6,10},{7,11},{8,4},{9,5},... | collective-permute-start | bytes 417800 | tf_op jit(solution)/shard_map/ppermute | solution.py:100
  18.6 0.0 collective-permute-done.2.refs_3_
  18.6 1.5 %collective-permute-start.1 = (bf16[32,2176]{1,0:T(8,128)(2,1)S(1)}, bf16[32,2176]{1,0:T(8,128)(2,1)S(1)}, u32[]{:S(2)}, u32[]{:S(2)}) collective-permute-start(bf16[32,2176]{1,0:T(8,128)(2,1)S(1)} %collective-permute-done.refs_0_), channel_id=1, source_target_pairs={{0,2},{1,3},{2,0},{3,1},{4,6},{5,7},{6,4},{7,5},{8,10},{9,11},{10,... | collective-permute-start | bytes 417800 | tf_op jit(solution)/shard_map/ppermute | solution.py:100
  20.1 1.9 %loader.2.refs_5_ = bf16[1,2048,768]{2,1,0:T(8,128)(2,1)S(1)} custom-call(bf16[32,2176]{1,0:T(8,128)(2,1)S(1)} %get-tuple-element.17.after.refs_1_, bf16[1,2048,768]{2,1,0:T(8,128)(2,1)} %source.2), custom_call_target="tpu_custom_call" | custom-call | tf_op jit(solution)/shard_map/loader/pallas_call | solution.py:294
  22.0 1.9 %loader.3.refs_6_ = bf16[1,768,2048]{2,1,0:T(8,128)(2,1)S(1)} custom-call(bf16[32,2176]{1,0:T(8,128)(2,1)S(1)} %get-tuple-element.17.after.refs_1_, bf16[1,768,2048]{2,1,0:T(8,128)(2,1)} %source.3), custom_call_target="tpu_custom_call" | custom-call | tf_op jit(solution)/shard_map/loader/pallas_call | solution.py:294
  23.9 0.0 collective-permute-done.9.refs_0_
  23.9 0.5 collective-permute-start.10
  24.4 0.0 collective-permute-done.1.refs_2_
  24.4 1.6 %collective-permute-start.12 = (bf16[32,2176]{1,0:T(8,128)(2,1)S(1)}, bf16[32,2176]{1,0:T(8,128)(2,1)S(1)}, u32[]{:S(2)}, u32[]{:S(2)}) collective-permute-start(bf16[32,2176]{1,0:T(8,128)(2,1)S(1)} %get-tuple-element.17.after.refs_1_), channel_id=1, source_target_pairs={{0,6},{1,7},{2,4},{3,5},{4,2},{5,3},{6,0},{7,1},{8,14},{9,15},{10,... | collective-permute-start | bytes 417800 | tf_op jit(solution)/shard_map/ppermute | solution.py:100
  26.0 0.0 collective-permute-done.3.refs_7_
  26.0 1.5 %collective-permute-start.11 = (bf16[32,2176]{1,0:T(8,128)(2,1)S(1)}, bf16[32,2176]{1,0:T(8,128)(2,1)S(1)}, u32[]{:S(2)}, u32[]{:S(2)}) collective-permute-start(bf16[32,2176]{1,0:T(8,128)(2,1)S(1)} %collective-permute-done.9.refs_0_), channel_id=1, source_target_pairs={{0,2},{1,3},{2,0},{3,1},{4,6},{5,7},{6,4},{7,5},{8,10},{9,11},{10,... | collective-permute-start | bytes 417800 | tf_op jit(solution)/shard_map/ppermute | solution.py:100
  27.5 0.0 collective-permute-done.4.refs_8_
  27.5 0.0 collective-permute-done.5.refs_9_
  27.5 2.8 %expert_rows.2 = (f32[32,2048]{1,0:T(8,128)S(1)}, f32[32,2048]{1,0:T(8,128)S(1)}, bf16[32,2048]{1,0:T(8,128)(2,1)S(1)}, bf16[32,2048]{1,0:T(8,128)(2,1)S(1)}) custom-call(bf16[32,2176]{1,0:T(8,128)(2,1)S(1)} %collective-permute-done.refs_0_, bf16[32,2176]{1,0:T(8,128)(2,1)S(1)} %get-tuple-element.17.after.refs_1_, ...), custom_call_target="tpu_custom_call" | custom-call | flops 2415919104 | bytes 18874368 | tf_op jit(solution)/shard_map/expert_rows/pallas_call | solution.py:359
  30.3 0.6 %collective-permute-start.7 = (bf16[32,2048]{1,0:T(8,128)(2,1)S(1)}, bf16[32,2048]{1,0:T(8,128)(2,1)S(1)}, u32[]{:S(2)}, u32[]{:S(2)}) collective-permute-start(bf16[32,2048]{1,0:T(8,128)(2,1)S(1)} %get-tuple-element.22), channel_id=1, source_target_pairs={{0,2},{1,3},{2,0},{3,1},{4,6},{5,7},{6,4},{7,5},{8,10},{9,11},{10,... | collective-permute-start | bytes 393224 | tf_op jit(solution)/shard_map/ppermute | solution.py:100
  30.8 0.0 collective-permute-done.10.refs_1_
  30.9 1.3 %collective-permute-done.12.refs_3_ = bf16[32,2176]{1,0:T(8,128)(2,1)S(1)} collective-permute-done((bf16[32,2176]{1,0:T(8,128)(2,1)S(1)}, bf16[32,2176]{1,0:T(8,128)(2,1)S(1)}, u32[]{:S(2)}, u32[]{:S(2)}) %collective-permute-start.12) | collective-permute-done | bytes 139296 | tf_op jit(solution)/shard_map/ppermute | solution.py:100
  32.1 2.4 %collective-permute-done.11.refs_2_ = bf16[32,2176]{1,0:T(8,128)(2,1)S(1)} collective-permute-done((bf16[32,2176]{1,0:T(8,128)(2,1)S(1)}, bf16[32,2176]{1,0:T(8,128)(2,1)S(1)}, u32[]{:S(2)}, u32[]{:S(2)}) %collective-permute-start.11) | collective-permute-done | bytes 139296 | tf_op jit(solution)/shard_map/ppermute | solution.py:100
  34.5 2.8 %expert_rows.3 = (f32[32,2048]{1,0:T(8,128)S(1)}, bf16[32,2048]{1,0:T(8,128)(2,1)S(1)}, bf16[32,2048]{1,0:T(8,128)(2,1)S(1)}, bf16[32,2048]{1,0:T(8,128)(2,1)S(1)}) custom-call(bf16[32,2176]{1,0:T(8,128)(2,1)S(1)} %collective-permute-done.9.refs_0_, bf16[32,2176]{1,0:T(8,128)(2,1)S(1)} %collective-permute-done.10.refs_1_, ...), custom_call_target="tpu_custom_call" | custom-call | flops 2415919104 | bytes 18874368 | tf_op jit(solution)/shard_map/expert_rows/pallas_call | solution.py:359
  37.3 1.6 %collective-permute-start.15 = (bf16[32,2048]{1,0:T(8,128)(2,1)S(1)}, bf16[32,2048]{1,0:T(8,128)(2,1)S(1)}, u32[]{:S(2)}, u32[]{:S(2)}) collective-permute-start(bf16[32,2048]{1,0:T(8,128)(2,1)S(1)} %get-tuple-element.26), channel_id=1, source_target_pairs={{0,2},{1,3},{2,0},{3,1},{4,6},{5,7},{6,4},{7,5},{8,10},{9,11},{10,... | collective-permute-start | bytes 393224 | tf_op jit(solution)/shard_map/ppermute | solution.py:100
  38.9 0.5 collective-permute-start.6
  39.4 1.2 %collective-permute-start.13 = (bf16[32,2048]{1,0:T(8,128)(2,1)S(1)}, bf16[32,2048]{1,0:T(8,128)(2,1)S(1)}, u32[]{:S(2)}, u32[]{:S(2)}) collective-permute-start(bf16[32,2048]{1,0:T(8,128)(2,1)S(1)} %get-tuple-element.23), channel_id=1, source_target_pairs={{0,4},{1,5},{2,6},{3,7},{4,0},{5,1},{6,2},{7,3},{8,12},{9,13},{10,... | collective-permute-start | bytes 393224 | tf_op jit(solution)/shard_map/ppermute | solution.py:100
  40.6 1.8 %collective-permute-start.14 = (bf16[32,2048]{1,0:T(8,128)(2,1)S(1)}, bf16[32,2048]{1,0:T(8,128)(2,1)S(1)}, u32[]{:S(2)}, u32[]{:S(2)}) collective-permute-start(bf16[32,2048]{1,0:T(8,128)(2,1)S(1)} %get-tuple-element.24), channel_id=1, source_target_pairs={{0,6},{1,7},{2,4},{3,5},{4,2},{5,3},{6,0},{7,1},{8,14},{9,15},{10,... | collective-permute-start | bytes 393224 | tf_op jit(solution)/shard_map/ppermute | solution.py:100
  42.4 0.0 collective-permute-done.7.refs_0_
  42.5 1.1 %collective-permute-start.8 = (bf16[32,2048]{1,0:T(8,128)(2,1)S(1)}, bf16[32,2048]{1,0:T(8,128)(2,1)S(1)}, u32[]{:S(2)}, u32[]{:S(2)}) collective-permute-start(bf16[32,2048]{1,0:T(8,128)(2,1)S(1)} %level_sum.2), channel_id=1, source_target_pairs={{0,8},{1,9},{2,10},{3,11},{4,12},{5,13},{6,14},{7,15},{8,0},{9,1},... | collective-permute-start | bytes 393224 | tf_op jit(solution)/shard_map/ppermute | solution.py:100
  43.6 0.0 collective-permute-done.15.refs_0_
  43.6 2.9 %collective-permute-start.16 = (bf16[32,2048]{1,0:T(8,128)(2,1)S(1)}, bf16[32,2048]{1,0:T(8,128)(2,1)S(1)}, u32[]{:S(2)}, u32[]{:S(2)}) collective-permute-start(bf16[32,2048]{1,0:T(8,128)(2,1)S(1)} %level_sum.3), channel_id=1, source_target_pairs={{0,12},{1,13},{2,14},{3,15},{4,8},{5,9},{6,10},{7,11},{8,4},{9,5},... | collective-permute-start | bytes 393224 | tf_op jit(solution)/shard_map/ppermute | solution.py:100
  46.5 0.0 collective-permute-done.6
  46.5 0.0 collective-permute-done.13
  46.5 3.8 %collective-permute-done.14 = bf16[32,2048]{1,0:T(8,128)(2,1)S(1)} collective-permute-done((bf16[32,2048]{1,0:T(8,128)(2,1)S(1)}, bf16[32,2048]{1,0:T(8,128)(2,1)S(1)}, u32[]{:S(2)}, u32[]{:S(2)}) %collective-permute-start.14) | collective-permute-done | bytes 131104 | tf_op jit(solution)/shard_map/ppermute | solution.py:100
  50.3 2.4 %collective-permute-done.8 = bf16[32,2048]{1,0:T(8,128)(2,1)S(1)} collective-permute-done((bf16[32,2048]{1,0:T(8,128)(2,1)S(1)}, bf16[32,2048]{1,0:T(8,128)(2,1)S(1)}, u32[]{:S(2)}, u32[]{:S(2)}) %collective-permute-start.8) | collective-permute-done | bytes 131104 | tf_op jit(solution)/shard_map/ppermute | solution.py:100
  52.8 0.0 collective-permute-done.16
  52.8 0.8 %add_convert_fusion = bf16[32,2048]{1,0:T(8,128)(2,1)} fusion(bf16[32,2048]{1,0:T(8,128)(2,1)S(1)} %collective-permute-done.16, bf16[32,2048]{1,0:T(8,128)(2,1)S(1)} %collective-permute-done.14, bf16[32,2048]{1,0:T(8,128)(2,1)S(1)} %collective-permute-done.13, bf16[32,2048]{1,0:T(8,128)(2,1)S(1)} %collective-permute-done.8, ...), kind=kLoop, calls=%fused_computation | loop fusion | flops 786432 | bytes 1310720 | tf_op jit(solution)/shard_map/convert_element_type | solution.py:426
  (2 shorter events, 0.1 us)
Async XLA Ops:
  0.0 26.0 %collective-permute-start.3 = (bf16[1,2048,768]{2,1,0:T(8,128)(2,1)}, bf16[1,2048,768]{2,1,0:T(8,128)(2,1)S(1)}, u32[]{:S(2)}, u32[]{:S(2)}) collective-permute-start(bf16[1,2048,768]{2,1,0:T(8,128)(2,1)} %w_gate_in.1), channel_id=1, source_target_pairs={{0,1},{1,0},{2,3},{3,2},{4,5},{5,4},{6,7},{7,6},{8,9},{9,8},{10,11... | collective-permute-start | bytes 9437192 | tf_op jit(solution)/shard_map/ppermute | solution.py:100
  0.5 27.0 %collective-permute-start.4 = (bf16[1,2048,768]{2,1,0:T(8,128)(2,1)}, bf16[1,2048,768]{2,1,0:T(8,128)(2,1)S(1)}, u32[]{:S(2)}, u32[]{:S(2)}) collective-permute-start(bf16[1,2048,768]{2,1,0:T(8,128)(2,1)} %source.2), channel_id=1, source_target_pairs={{0,1},{1,0},{2,3},{3,2},{4,5},{5,4},{6,7},{7,6},{8,9},{9,8},{10,11... | collective-permute-start | bytes 9437192 | tf_op jit(solution)/shard_map/ppermute | solution.py:100
  0.5 27.0 %collective-permute-start.5 = (bf16[1,768,2048]{2,1,0:T(8,128)(2,1)}, bf16[1,768,2048]{2,1,0:T(8,128)(2,1)S(1)}, u32[]{:S(2)}, u32[]{:S(2)}) collective-permute-start(bf16[1,768,2048]{2,1,0:T(8,128)(2,1)} %source.3), channel_id=1, source_target_pairs={{0,1},{1,0},{2,3},{3,2},{4,5},{5,4},{6,7},{7,6},{8,9},{9,8},{10,11... | collective-permute-start | bytes 9437192 | tf_op jit(solution)/shard_map/ppermute | solution.py:100
  4.1 11.0 %collective-permute-start = (bf16[32,2176]{1,0:T(8,128)(2,1)S(1)}, bf16[32,2176]{1,0:T(8,128)(2,1)S(1)}, u32[]{:S(2)}, u32[]{:S(2)}) collective-permute-start(bf16[32,2176]{1,0:T(8,128)(2,1)S(1)} %get-tuple-element.17.after.refs_1_), channel_id=1, source_target_pairs={{0,8},{1,9},{2,10},{3,11},{4,12},{5,13},{6,14},{7,15},{8,0},{9,1},... | collective-permute-start | bytes 417800 | tf_op jit(solution)/shard_map/ppermute | solution.py:100
  7.7 10.9 %collective-permute-start.2 = (bf16[32,2176]{1,0:T(8,128)(2,1)S(1)}, bf16[32,2176]{1,0:T(8,128)(2,1)S(1)}, u32[]{:S(2)}, u32[]{:S(2)}) collective-permute-start(bf16[32,2176]{1,0:T(8,128)(2,1)S(1)} %get-tuple-element.17.after.refs_1_), channel_id=1, source_target_pairs={{0,2},{1,3},{2,0},{3,1},{4,6},{5,7},{6,4},{7,5},{8,10},{9,11},{10,... | collective-permute-start | bytes 417800 | tf_op jit(solution)/shard_map/ppermute | solution.py:100
  15.0 8.9 %collective-permute-start.9 = (bf16[32,2176]{1,0:T(8,128)(2,1)S(1)}, bf16[32,2176]{1,0:T(8,128)(2,1)S(1)}, u32[]{:S(2)}, u32[]{:S(2)}) collective-permute-start(bf16[32,2176]{1,0:T(8,128)(2,1)S(1)} %get-tuple-element.17.after.refs_1_), channel_id=1, source_target_pairs={{0,12},{1,13},{2,14},{3,15},{4,8},{5,9},{6,10},{7,11},{8,4},{9,5},... | collective-permute-start | bytes 417800 | tf_op jit(solution)/shard_map/ppermute | solution.py:100
  18.6 5.8 %collective-permute-start.1 = (bf16[32,2176]{1,0:T(8,128)(2,1)S(1)}, bf16[32,2176]{1,0:T(8,128)(2,1)S(1)}, u32[]{:S(2)}, u32[]{:S(2)}) collective-permute-start(bf16[32,2176]{1,0:T(8,128)(2,1)S(1)} %collective-permute-done.refs_0_), channel_id=1, source_target_pairs={{0,2},{1,3},{2,0},{3,1},{4,6},{5,7},{6,4},{7,5},{8,10},{9,11},{10,... | collective-permute-start | bytes 417800 | tf_op jit(solution)/shard_map/ppermute | solution.py:100
  23.9 6.9 %collective-permute-start.10 = (bf16[32,2176]{1,0:T(8,128)(2,1)S(1)}, bf16[32,2176]{1,0:T(8,128)(2,1)S(1)}, u32[]{:S(2)}, u32[]{:S(2)}) collective-permute-start(bf16[32,2176]{1,0:T(8,128)(2,1)S(1)} %get-tuple-element.17.after.refs_1_), channel_id=1, source_target_pairs={{0,4},{1,5},{2,6},{3,7},{4,0},{5,1},{6,2},{7,3},{8,12},{9,13},{10,... | collective-permute-start | bytes 417800 | tf_op jit(solution)/shard_map/ppermute | solution.py:100
  24.4 7.7 %collective-permute-start.12 = (bf16[32,2176]{1,0:T(8,128)(2,1)S(1)}, bf16[32,2176]{1,0:T(8,128)(2,1)S(1)}, u32[]{:S(2)}, u32[]{:S(2)}) collective-permute-start(bf16[32,2176]{1,0:T(8,128)(2,1)S(1)} %get-tuple-element.17.after.refs_1_), channel_id=1, source_target_pairs={{0,6},{1,7},{2,4},{3,5},{4,2},{5,3},{6,0},{7,1},{8,14},{9,15},{10,... | collective-permute-start | bytes 417800 | tf_op jit(solution)/shard_map/ppermute | solution.py:100
  26.0 8.5 %collective-permute-start.11 = (bf16[32,2176]{1,0:T(8,128)(2,1)S(1)}, bf16[32,2176]{1,0:T(8,128)(2,1)S(1)}, u32[]{:S(2)}, u32[]{:S(2)}) collective-permute-start(bf16[32,2176]{1,0:T(8,128)(2,1)S(1)} %collective-permute-done.9.refs_0_), channel_id=1, source_target_pairs={{0,2},{1,3},{2,0},{3,1},{4,6},{5,7},{6,4},{7,5},{8,10},{9,11},{10,... | collective-permute-start | bytes 417800 | tf_op jit(solution)/shard_map/ppermute | solution.py:100
  30.3 12.1 %collective-permute-start.7 = (bf16[32,2048]{1,0:T(8,128)(2,1)S(1)}, bf16[32,2048]{1,0:T(8,128)(2,1)S(1)}, u32[]{:S(2)}, u32[]{:S(2)}) collective-permute-start(bf16[32,2048]{1,0:T(8,128)(2,1)S(1)} %get-tuple-element.22), channel_id=1, source_target_pairs={{0,2},{1,3},{2,0},{3,1},{4,6},{5,7},{6,4},{7,5},{8,10},{9,11},{10,... | collective-permute-start | bytes 393224 | tf_op jit(solution)/shard_map/ppermute | solution.py:100
  37.3 6.2 %collective-permute-start.15 = (bf16[32,2048]{1,0:T(8,128)(2,1)S(1)}, bf16[32,2048]{1,0:T(8,128)(2,1)S(1)}, u32[]{:S(2)}, u32[]{:S(2)}) collective-permute-start(bf16[32,2048]{1,0:T(8,128)(2,1)S(1)} %get-tuple-element.26), channel_id=1, source_target_pairs={{0,2},{1,3},{2,0},{3,1},{4,6},{5,7},{6,4},{7,5},{8,10},{9,11},{10,... | collective-permute-start | bytes 393224 | tf_op jit(solution)/shard_map/ppermute | solution.py:100
  38.9 7.6 %collective-permute-start.6 = (bf16[32,2048]{1,0:T(8,128)(2,1)S(1)}, bf16[32,2048]{1,0:T(8,128)(2,1)S(1)}, u32[]{:S(2)}, u32[]{:S(2)}) collective-permute-start(bf16[32,2048]{1,0:T(8,128)(2,1)S(1)} %get-tuple-element.20), channel_id=1, source_target_pairs={{0,2},{1,3},{2,0},{3,1},{4,6},{5,7},{6,4},{7,5},{8,10},{9,11},{10,... | collective-permute-start | bytes 393224 | tf_op jit(solution)/shard_map/ppermute | solution.py:100
  39.4 7.1 %collective-permute-start.13 = (bf16[32,2048]{1,0:T(8,128)(2,1)S(1)}, bf16[32,2048]{1,0:T(8,128)(2,1)S(1)}, u32[]{:S(2)}, u32[]{:S(2)}) collective-permute-start(bf16[32,2048]{1,0:T(8,128)(2,1)S(1)} %get-tuple-element.23), channel_id=1, source_target_pairs={{0,4},{1,5},{2,6},{3,7},{4,0},{5,1},{6,2},{7,3},{8,12},{9,13},{10,... | collective-permute-start | bytes 393224 | tf_op jit(solution)/shard_map/ppermute | solution.py:100
  40.6 9.7 %collective-permute-start.14 = (bf16[32,2048]{1,0:T(8,128)(2,1)S(1)}, bf16[32,2048]{1,0:T(8,128)(2,1)S(1)}, u32[]{:S(2)}, u32[]{:S(2)}) collective-permute-start(bf16[32,2048]{1,0:T(8,128)(2,1)S(1)} %get-tuple-element.24), channel_id=1, source_target_pairs={{0,6},{1,7},{2,4},{3,5},{4,2},{5,3},{6,0},{7,1},{8,14},{9,15},{10,... | collective-permute-start | bytes 393224 | tf_op jit(solution)/shard_map/ppermute | solution.py:100
  42.5 10.3 %collective-permute-start.8 = (bf16[32,2048]{1,0:T(8,128)(2,1)S(1)}, bf16[32,2048]{1,0:T(8,128)(2,1)S(1)}, u32[]{:S(2)}, u32[]{:S(2)}) collective-permute-start(bf16[32,2048]{1,0:T(8,128)(2,1)S(1)} %level_sum.2), channel_id=1, source_target_pairs={{0,8},{1,9},{2,10},{3,11},{4,12},{5,13},{6,14},{7,15},{8,0},{9,1},... | collective-permute-start | bytes 393224 | tf_op jit(solution)/shard_map/ppermute | solution.py:100
  43.6 9.2 %collective-permute-start.16 = (bf16[32,2048]{1,0:T(8,128)(2,1)S(1)}, bf16[32,2048]{1,0:T(8,128)(2,1)S(1)}, u32[]{:S(2)}, u32[]{:S(2)}) collective-permute-start(bf16[32,2048]{1,0:T(8,128)(2,1)S(1)} %level_sum.3), channel_id=1, source_target_pairs={{0,12},{1,13},{2,14},{3,15},{4,8},{5,9},{6,10},{7,11},{8,4},{9,5},... | collective-permute-start | bytes 393224 | tf_op jit(solution)/shard_map/ppermute | solution.py:100
